TPU v7x, 128 devices: a whole 4x4x4 slice. The times are simulated.
128 devices in a mesh: gx: 16 (over x, z_hi, core), gy: 8 (over y, z_lo).
Axes of the slice: x: 4, y: 4, z: 4 (z_hi: 2, z_lo: 2; z = z_hi * 2 + z_lo), core: 2. Of those that a mesh axis runs over, the one named last changes fastest.
Arguments:
- disc_pos: float32 [2, 64, 256, 128], P(None, 'gy', 'gx'), may hold values from 0 to 1
- disc_vel: float32 [2, 64, 256, 128], P(None, 'gy', 'gx'), may hold values from -3 to 3
- radius: float32 [64, 256, 128], P('gy', 'gx'), may hold values from 0.04 to 0.08
- bond_list: int32 [4, 64, 256, 128], P(None, 'gy', 'gx'), may hold values from 0 to 127
- contact_mask: int32 [8, 64, 256], P(None, 'gy', 'gx'), may hold values 0 or 1
- remap_block: int32 [128, 128, 2], P(('gx', 'gy')), may hold values from -1 to 127, as said below
- ocean_state: float32 [4, 48, 256, 2048], P(None, None, 'gy', 'gx'), may hold values from -6 to 6
- mix_coef: float32 [48, 256, 2048], P(None, 'gy', 'gx'), may hold values from 0.02 to 0.2
- remap_cell: int32 [128, 128, 2], P(('gx', 'gy')), may hold values from 0 to 4095
- fold_perm: int32 [2048], P('gx'), may hold values from 0 to 2047, as said below
Outputs:
- pos_next: float32 [2, 64, 256, 128], P(None, 'gy', 'gx')
- vel_next: float32 [2, 64, 256, 128], P(None, 'gy', 'gx')
- ocean_next: float32 [4, 48, 256, 2048], P(None, None, 'gy', 'gx')
Inputs may be any that keep to these rules, and one draw needn't show every extreme that they name: `remap_block`: for each ice tile, every one of its 128 local blocks stands in exactly one slot and the other slots hold -1; in every draw some ocean tile gets all 2 of its slots filled by every ice tile. `fold_perm`: A permutation of the 2048 columns.
All inputs are finite; a program needn't handle non-finite values. No bound on the sum of `contact_mask` on one device may be relied on, other than what follows from the above.
Results may differ from a plain program's by a relative error of at most 0.0003.
Values sent between devices are 32-bit elements; how exact they have to be, the bound alone decides.
A program may use at most 128 MiB of HBM per device.

v0:
```python
import functools

import jax
import jax.numpy as jnp
from jax import lax
from jax.experimental import pallas as pl
from jax.experimental.pallas import tpu as pltpu
from jax.sharding import PartitionSpec as P

BONDS = 4
SUB = 3
SOFTEN = 0.0001
STIFFNESS = 2.0
BOND_STIFF = 0.1
TIME_STEP = 0.05
DRAG_ICE = 15.0
DRAG_BACK = 0.5
VERT_MIX = 0.1
SPIN_RATE = 0.3
NEIGHBOURS = ((-1, -1), (-1, 0), (-1, 1), (0, -1), (0, 1), (1, -1), (1, 0), (1, 1))
TOGETHER = 4
STATIC = 2
ROWS = 2
CHUNK = 8
TURNERS = 12
TURN_ROWS = 16
MESH = pl.DeviceIdType.MESH
VMEM = pl.BlockSpec(memory_space=pltpu.VMEM)
ANY = pl.BlockSpec(memory_space=pl.ANY)


def grant(mib, **more):
    return pltpu.CompilerParams(vmem_limit_bytes=mib << 20, **more)


def shape(*dims):
    return jax.ShapeDtypeStruct(dims, jnp.float32)


def split(value):
    high = value.astype(jnp.bfloat16)
    rest = value - high.astype(jnp.float32)
    middle = rest.astype(jnp.bfloat16)
    low = (rest - middle.astype(jnp.float32)).astype(jnp.bfloat16)
    return jnp.concatenate([high, middle, low], axis=0)


def joined(value):
    rows = value.shape[0] // 3
    return value[:rows] + value[rows : 2 * rows] + value[2 * rows :]


def lane_take(rows, index):
    return jnp.take_along_axis(rows, index, axis=1, mode="promise_in_bounds")


def pair_terms(acc_x, acc_y, own_x, own_y, own_r, other_x, other_y, other_r):
    sep_x = other_x - own_x
    sep_y = other_y - own_y
    inverse = lax.rsqrt(sep_x * sep_x + sep_y * sep_y + SOFTEN)
    push = jnp.maximum((other_r + own_r) * inverse - 1.0, 0.0)
    return acc_x + push * sep_x, acc_y + push * sep_y


def turn(rows, perms, turned):
    lanes = rows.shape[2]

    def one(h, carry):
        wanted = jnp.broadcast_to(perms[h], (8, lanes))
        owner, column = wanted // lanes, wanted % lanes
        for half in range(TURN_ROWS // 8):
            at = pl.ds(8 * half, 8)
            got = jnp.zeros((8, lanes), jnp.float32)
            for source in range(rows.shape[0]):
                got = jnp.where(owner == source, lane_take(rows[source, at, :], column), got)
            turned[h, at, :] = got
        return carry

    lax.fori_loop(0, perms.shape[0], one, 0)


def contact_kernel(which, n_gy, pos, vel, rad, bonds, mask, halo, halo_first, *refs):
    last = which == SUB - 1
    if last:
        slots, pos_out, vel_out, sent, *scratch = refs
    elif which == 0:
        rows, perms, pos_out, vel_out, edges, turned, *scratch = refs

        @pl.when(lax.axis_index("gy") == n_gy - 1)
        def _():
            turn(rows, perms, turned)

    else:
        pos_out, vel_out, edges, *scratch = refs
    wide, columns, found, found_t, force, tally, counts, sem = scratch
    rows_dev, cols_dev = wide.shape[1] - 2, pos.shape[1] // (wide.shape[1] - 2)
    for comp in range(3):
        source = pos.at[comp] if comp < 2 else rad
        frame = halo if comp < 2 else halo_first
        for y in range(rows_dev):
            wide[comp, y + 1, pl.ds(1, cols_dev), :] = source[pl.ds(y * cols_dev, cols_dev), :]
            wide[comp, y + 1, pl.ds(0, 1), :] = frame[3, comp, pl.ds(y, 1), :]
            wide[comp, y + 1, pl.ds(cols_dev + 1, 1), :] = frame[4, comp, pl.ds(y, 1), :]
        for side, y in ((0, 0), (5, rows_dev + 1)):
            wide[comp, y, pl.ds(0, 1), :] = frame[side, comp, pl.ds(7, 1), :]
            wide[comp, y, pl.ds(1, cols_dev), :] = frame[side + 1, comp]
            wide[comp, y, pl.ds(cols_dev + 1, 1), :] = frame[side + 2, comp, pl.ds(0, 1), :]
    blocks, discs = rad.shape
    lane = lax.broadcasted_iota(jnp.int32, (8, discs), 1)
    lane_f = lane.astype(jnp.float32)
    tri_row = lax.broadcasted_iota(jnp.int32, (discs, 2 * discs), 0)
    tri_col = lax.broadcasted_iota(jnp.int32, (discs, 2 * discs), 1)
    triangle = (tri_row <= tri_col).astype(jnp.bfloat16)
    for comp in range(2):
        columns[comp] = pos[comp].T
    columns[2] = rad[...].T

    def collect(start):
        def one_row(step_y, carry):
            for half in range(ROWS * cols_dev // 8):
                y = step_y * ROWS + half // (cols_dev // 8)
                x0 = half % (cols_dev // 8) * 8
                at = pl.multiple_of(y * cols_dev + x0, 8)
                own = [pos[0, pl.ds(at, 8), :], pos[1, pl.ds(at, 8), :], rad[pl.ds(at, 8), :]]
                reach = jnp.max(own[2], axis=1, keepdims=True)
                low = [jnp.min(own[c], axis=1, keepdims=True) - reach for c in range(2)]
                high = [jnp.max(own[c], axis=1, keepdims=True) + reach for c in range(2)]
                weights = mask[pl.ds(at, 8), :]
                near = []
                for k, (sy, sx) in enumerate(NEIGHBOURS):
                    where = (y + 1 + sy, pl.ds(x0 + 1 + sx, 8), slice(None))
                    nx = wide[(0,) + where] + float(sx)
                    ny = wide[(1,) + where] + float(sy)
                    nr = wide[(2,) + where]
                    close = (nx - nr < high[0]) & (nx + nr > low[0])
                    close = close & (ny - nr < high[1]) & (ny + nr > low[1])
                    close = close & (weights[:, k : k + 1] > 0.5)
                    near.append((nx, ny, nr, close))
                flags = jnp.concatenate([n[3].astype(jnp.float32) for n in near], axis=0)
                ranks = jnp.dot(
                    flags.astype(jnp.bfloat16), triangle, preferred_element_type=jnp.float32
                )
                base = jnp.zeros((8, discs), jnp.float32) - start
                gx = jnp.zeros((8, discs), jnp.float32)
                gy = jnp.zeros((8, discs), jnp.float32)
                gr = jnp.full((8, discs), -1.0, jnp.float32)
                for k in range(8):
                    nx, ny, nr, _ = near[k]
                    rank = ranks[8 * k : 8 * k + 8, :discs]
                    total = ranks[8 * k : 8 * k + 8, discs:]
                    want = lane_f - base
                    source = jnp.zeros((8, discs), jnp.int32)
                    step = discs // 2
                    while step >= 1:
                        probe = lane_take(rank, source + (step - 1))
                        source = jnp.where(probe <= want, source + step, source)
                        step //= 2
                    valid = (want >= 0.0) & (want < total)
                    gx = jnp.where(valid, lane_take(nx, source), gx)
                    gy = jnp.where(valid, lane_take(ny, source), gy)
                    gr = jnp.where(valid, lane_take(nr, source), gr)
                    base = base + total
                found[0, pl.ds(at, 8), :] = gx
                found[1, pl.ds(at, 8), :] = gy
                found[2, pl.ds(at, 8), :] = gr
                found[3, pl.ds(at, 8), :] = base
            return carry

        lax.fori_loop(0, rows_dev // ROWS, one_row, 0)
        for comp in range(3):
            found_t[comp] = found[comp].T
        left = found[3].T[0:8]
        groups = jnp.clip(jnp.ceil(left * (1.0 / 32.0)), 0.0, 4.0).astype(jnp.int32)
        passes = jnp.ceil(jnp.max(left, axis=1, keepdims=True) * (1.0 / discs)).astype(jnp.int32)
        tally[0:8] = groups
        tally[8:16] = jnp.broadcast_to(passes, (8, discs))
        copy = pltpu.make_async_copy(tally, counts, sem)
        copy.start()
        copy.wait()

    def gather_own(b):
        own = (pos[0, pl.ds(b, 1), :], pos[1, pl.ds(b, 1), :], rad[pl.ds(b, 1), :])
        return own, jnp.full((8, discs), b, jnp.int32)

    def visit(source, at, target, acc):
        own, index = target
        return pair_terms(*acc, *own, *[lane_take(source[k, at, :], index) for k in range(3)])

    zero = jnp.zeros((8, discs), jnp.float32)

    def sweep(first, static_groups):
        def some(t, carry):
            blocks_here = [t * TOGETHER + u for u in range(TOGETHER)]
            targets = [gather_own(b) for b in blocks_here]
            accs = [(zero, zero)] * TOGETHER
            for u in range(TOGETHER):
                if first:
                    for c in range(discs // 8):
                        accs[u] = visit(columns, pl.ds(c * 8, 8), targets[u], accs[u])
                for c in range(4 * static_groups):
                    accs[u] = visit(found_t, pl.ds(c * 8, 8), targets[u], accs[u])

            def group(g, accs):
                accs = list(accs)
                for u in range(TOGETHER):
                    for c in range(4):
                        at = pl.ds(pl.multiple_of(g * 32 + c * 8, 8), 8)
                        accs[u] = visit(found_t, at, targets[u], accs[u])
                return tuple(accs)

            most = counts[0, blocks_here[0]]
            for b in blocks_here[1:]:
                most = jnp.maximum(most, counts[0, b])
            accs = lax.fori_loop(static_groups, most, group, tuple(accs))
            for u in range(TOGETHER):
                for k in range(2):
                    total = jnp.sum(accs[u][k], axis=0, keepdims=True)
                    if first:
                        force[k, pl.ds(blocks_here[u], 1), :] = total
                    else:
                        force[k, pl.ds(blocks_here[u], 1), :] += total
            return carry

        lax.fori_loop(0, blocks // TOGETHER, some, 0)

    collect(0.0)
    sweep(True, STATIC)

    def more(p, carry):
        collect(p.astype(jnp.float32) * discs)
        sweep(False, 0)
        return carry

    lax.fori_loop(1, counts[8, 0], more, 0)

    def update(g, carry):
        at = pl.ds(pl.multiple_of(g * 8, 8), 8)
        scale = 0.06 / rad[at, :]
        scale = scale * scale
        for k in range(2):
            here = pos[k, at, :]
            bonded = lane_take(here, bonds[0, at, :])
            for p in range(1, BONDS):
                bonded = bonded + lane_take(here, bonds[p, at, :])
            total = BOND_STIFF * (bonded - BONDS * here) - STIFFNESS * force[k, at, :]
            speed = vel[k, at, :] + total * scale
            vel_out[k, at, :] = speed
            pos_out[k, at, :] = here + TIME_STEP * speed
        return carry

    lax.fori_loop(0, blocks // 8, update, 0)
    if last:
        spots = [jnp.broadcast_to(slots[k : k + 1], (8, blocks)) for k in range(2)]
        rows = []
        for comp in range(2):
            drag = rad[...] * rad[...] * vel_out[comp]
            total = DRAG_ICE * jnp.sum(drag.T, axis=0, keepdims=True)
            total = jnp.broadcast_to(total, (8, blocks))
            for spot in spots:
                moved = lane_take(total, jnp.maximum(spot, 0))
                rows.append(jnp.where(spot >= 0, moved, 0.0)[0:1])
        rows.append(jnp.zeros((blocks - 4, blocks), jnp.float32))
        sent[:, 0, :] = jnp.concatenate(rows, axis=0).T
    else:
        for side in range(2):
            for comp in range(2):
                at = pl.ds(side * (cols_dev - 1), rows_dev, stride=cols_dev)
                edges[side, comp] = pos_out[comp, at, :]


def contact_step(which, n_gy, pos, vel, rad, bonds, mask, halo, halo_first, *extra):
    blocks, discs = rad.shape
    rows_dev = blocks // 16
    square = shape(2, blocks, discs)
    tail = shape(blocks, 1, discs) if which == SUB - 1 else shape(2, 2, rows_dev, discs)
    outs = (square, square, tail)
    if which == 0:
        outs += (shape(*extra[0].shape),)
    args = (pos, vel, rad, bonds, mask, halo, halo_first) + extra
    return pl.pallas_call(
        functools.partial(contact_kernel, which, n_gy),
        out_shape=outs,
        in_specs=[VMEM] * len(args),
        out_specs=(VMEM,) * len(outs),
        scratch_shapes=[
            pltpu.VMEM((3, rows_dev + 2, 24, discs), jnp.float32),
            pltpu.VMEM((3, discs, blocks), jnp.float32),
            pltpu.VMEM((4, blocks, discs), jnp.float32),
            pltpu.VMEM((3, discs, blocks), jnp.float32),
            pltpu.VMEM((2, blocks, discs), jnp.float32),
            pltpu.VMEM((16, blocks), jnp.int32),
            pltpu.SMEM((16, blocks), jnp.int32),
            pltpu.SemaphoreType.DMA,
        ],
        compiler_params=grant(16),
        name=("contact_first", "contact", "contact_last")[which],
    )(*args)


def pack_kernel(n_gy, ocean, pos, rad, allowed, columns, bottom, top, state, edges, mask):
    rows = ocean.shape[2]
    lane = lax.broadcasted_iota(jnp.int32, (8, 128), 1)
    packed = [jnp.zeros((8, 128), jnp.float32)] * 2
    for field in range(4):
        for layer in range(CHUNK):
            for v in range(rows // 8):
                g = (field * CHUNK + layer) * (rows // 8) + v
                place = g % 64
                turned = pltpu.roll(ocean[field, layer, pl.ds(8 * v, 8), :], 2 * place + 1, 1)
                packed[g // 64] = jnp.where(lane // 2 == place, turned, packed[g // 64])
    columns[0] = jnp.concatenate(packed, axis=0)
    bottom[...] = ocean[:, :, 0, :]
    top[...] = ocean[:, :, rows - 1, :]

    @pl.when(pl.program_id(0) == 0)
    def _():
        for comp in range(3):
            source = pos.at[comp] if comp < 2 else rad
            state[comp] = source[...]
            for side in range(2):
                edges[side, comp] = source[pl.ds(side * 15, 8, stride=16), :]
        _, rows_dev, cols_dev = allowed.shape
        spread = jnp.zeros((8, 128), jnp.float32)
        for y in range(rows_dev):
            part = allowed[:, y, :].astype(jnp.float32)
            part = jnp.concatenate([part, jnp.zeros((8, 128 - cols_dev), jnp.float32)], axis=1)
            spread = spread + (pltpu.roll(part, y * cols_dev, 1) if y else part)
        which = lax.broadcasted_iota(jnp.int32, (8, 128), 0)
        shift_y = jnp.where(which < 3, -1, jnp.where(which < 5, 0, 1))
        row = lax.axis_index("gy") * rows_dev + lane // cols_dev + shift_y
        spread = jnp.where((row >= 0) & (row < n_gy * rows_dev), spread, 0.0)
        mask[...] = jnp.concatenate([spread, jnp.zeros((120, 128), jnp.float32)], axis=0).T


def pack(n_gy, ocean, pos, rad, allowed):
    fields, layers, rows, lanes = ocean.shape
    steps = layers // CHUNK
    whole = lambda *dims: pl.BlockSpec(dims, lambda i: (0,) * len(dims))
    row = pl.BlockSpec((fields, CHUNK, lanes), lambda i: (0, i, 0))
    return pl.pallas_call(
        functools.partial(pack_kernel, n_gy),
        grid=(steps,),
        out_shape=(
            shape(steps, 16, lanes),
            shape(fields, layers, lanes),
            shape(fields, layers, lanes),
            shape(3, *rad.shape),
            shape(2, 3, 8, lanes),
            shape(*rad.shape),
        ),
        in_specs=[
            pl.BlockSpec((fields, CHUNK, rows, lanes), lambda i: (0, i, 0, 0)),
            whole(*pos.shape),
            whole(*rad.shape),
            whole(*allowed.shape),
        ],
        out_specs=(
            pl.BlockSpec((1, 16, lanes), lambda i: (i, 0, 0)),
            row,
            row,
            whole(3, *rad.shape),
            whole(2, 3, 8, lanes),
            whole(*rad.shape),
        ),
        compiler_params=grant(8),
        name="pack",
    )(ocean, pos, rad, allowed)


def exchange_kernel(which, n_gx, n_gy, *refs):
    if which == 0:
        state, edges, top, bottom, columns, perm, halo, lon, lat, rows, perms, *sems = refs
        send_sem, recv_sem, sea_send, sea_recv, far_send, far_recv, perm_send, perm_recv, own = sems
    elif which == 1:
        state, edges, turned, halo, mirror, send_sem, recv_sem, far_send, far_recv, own = refs
    else:
        state, edges, halo, send_sem, recv_sem = refs
    gx, gy = lax.axis_index("gx"), lax.axis_index("gy")
    is_top = gy == n_gy - 1

    def at(dx, dy):
        return lax.rem(gx + dx + n_gx, n_gx), lax.rem(gy + dy + n_gy, n_gy)

    barrier = pltpu.get_barrier_semaphore()
    for dy, dx in NEIGHBOURS:
        pl.semaphore_signal(barrier, inc=1, device_id=at(dx, dy), device_id_type=MESH)
    if which < 2:

        @pl.when(is_top)
        def _():
            for d in range(1, n_gx):
                pl.semaphore_signal(barrier, inc=1, device_id=at(d, 0), device_id_type=MESH)
            pl.semaphore_wait(barrier, len(NEIGHBOURS) + n_gx - 1)

        @pl.when(jnp.logical_not(is_top))
        def _():
            pl.semaphore_wait(barrier, len(NEIGHBOURS))

    else:
        pl.semaphore_wait(barrier, len(NEIGHBOURS))

    def send(source, target, sems, index, device):
        return pltpu.make_async_remote_copy(
            src_ref=source,
            dst_ref=target,
            send_sem=sems[0].at[index],
            recv_sem=sems[1].at[index],
            device_id=device,
            device_id_type=MESH,
        )

    blocks = state.shape[1]
    copies = []
    for k, (sy, sx) in enumerate(NEIGHBOURS):
        device = at(-sx, -sy)
        first = 0 if sy == 1 else blocks - 16
        if sy == 0:
            source, target = edges.at[0 if sx == 1 else 1], halo.at[k, :, pl.ds(0, 8), :]
        elif sx == 0:
            source, target = state.at[:, pl.ds(first, 16), :], halo.at[k]
        else:
            first = first if sx == 1 else first + 8
            source, target = state.at[:, pl.ds(first, 8), :], halo.at[k, :, pl.ds(0, 8), :]
        copies.append(send(source, target, (send_sem, recv_sem), k, device))
    for copy in copies:
        copy.start()
    if which == 0:
        sea = (sea_send, sea_recv)
        later = [
            send(columns, lon.at[0], sea, 0, at(1, 0)),
            send(columns, lon.at[1], sea, 1, at(-1, 0)),
            send(top, lat.at[0], sea, 2, at(0, 1)),
            send(bottom, lat.at[1], sea, 3, at(0, -1)),
        ]
        copies += later

    if which == 0:

        @pl.when(is_top)
        def _():
            kept = pltpu.make_async_copy(perm, perms.at[gx], own.at[0])
            kept.start()
            notes = [
                send(perm, perms.at[gx], (perm_send, perm_recv), d - 1, at(d, 0))
                for d in range(1, n_gx)
            ]
            for note in notes:
                note.start()
            far = []
            for d in range(1, n_gx):
                peer = lax.rem(gx + d, n_gx)
                first = pl.multiple_of(jnp.minimum(peer, TURNERS - 1) * TURN_ROWS, TURN_ROWS)
                source = top.at[pl.ds(first, TURN_ROWS), :]
                far.append(send(source, rows.at[gx], (far_send, far_recv), d - 1, at(d, 0)))

                @pl.when(peer < TURNERS)
                def _(copy=far[-1]):
                    copy.start()

            @pl.when(gx < TURNERS)
            def _():
                first = pl.multiple_of(jnp.minimum(gx, TURNERS - 1) * TURN_ROWS, TURN_ROWS)
                mine = pltpu.make_async_copy(top.at[pl.ds(first, TURN_ROWS), :], rows.at[gx], own.at[1])
                mine.start()
                mine.wait()
                for copy in far:
                    copy.wait_recv()

            for d in range(1, n_gx):

                @pl.when(lax.rem(gx + d, n_gx) < TURNERS)
                def _(copy=far[d - 1]):
                    copy.wait_send()

            kept.wait()
            for note in notes:
                note.wait()

        for copy in later:
            copy.start()

    if which == 1:

        @pl.when(is_top)
        def _():
            me = jnp.minimum(gx, TURNERS - 1)
            far = [
                send(turned.at[lax.rem(gx + d, n_gx)], mirror.at[me], (far_send, far_recv), d - 1, at(d, 0))
                for d in range(1, n_gx)
            ]

            @pl.when(gx < TURNERS)
            def _():
                mine = pltpu.make_async_copy(turned.at[gx], mirror.at[me], own)
                mine.start()
                for copy in far:
                    copy.start()
                mine.wait()
                for copy in far:
                    copy.wait_send()

            for d in range(1, n_gx):

                @pl.when(lax.rem(gx - d + n_gx, n_gx) < TURNERS)
                def _(copy=far[d - 1]):
                    copy.wait_recv()

    for copy in copies:
        copy.wait()


def exchange(which, n_gx, n_gy, state, edges, *args):
    comps = state.shape[0]
    lanes = state.shape[2]
    outs = [shape(8, comps, 16, lanes)]
    dma = pltpu.SemaphoreType.DMA
    scratch = [dma((8,)), dma((8,))]
    far = [dma((n_gx - 1,)), dma((n_gx - 1,))]
    if which == 0:
        top, bottom, columns, perm = args
        outs += [shape(2, *columns.shape), shape(2, *top.shape)]
        outs += [shape(n_gx, TURN_ROWS, lanes), jax.ShapeDtypeStruct((n_gx, 1, lanes), jnp.int32)]
        scratch += [dma((4,)), dma((4,))] + far + far + [dma((2,))]
    if which == 1:
        outs += [shape(TURNERS, TURN_ROWS, lanes)]
        scratch += far + [dma]
    return pl.pallas_call(
        functools.partial(exchange_kernel, which, n_gx, n_gy),
        out_shape=tuple(outs),
        in_specs=[VMEM] * (2 + len(args)),
        out_specs=(VMEM,) * len(outs),
        scratch_shapes=scratch,
        compiler_params=grant(4, collective_id=which, has_side_effects=True),
        name=("exchange_first", "exchange_second", "exchange_third")[which],
    )(state, edges, *args)


def ocean_kernel(n_gy, ocean, above, below, mix, lon, lat, mirror, out, skin):
    step = pl.program_id(0)
    rows, lanes = ocean.shape[2], ocean.shape[3]
    gy = lax.axis_index("gy")
    lane = lax.broadcasted_iota(jnp.int32, (rows, lanes), 1)
    sub = lax.broadcasted_iota(jnp.int32, (rows, lanes), 0)
    lane8 = lax.broadcasted_iota(jnp.int32, (8, lanes), 1)
    bands = []
    for half in range(2):
        at = pl.ds(8 * half, 8)
        west, east = pltpu.roll(lon[0, 0, at, :], 1, 1), pltpu.roll(lon[1, 0, at, :], lanes - 1, 1)
        bands.append(jnp.where(lane8 % 2 == 1, west, east))
    spin = 2.0 * ((gy * rows + sub).astype(jnp.float32) + 0.5) / (rows * n_gy) - 1.0
    spin = SPIN_RATE * spin
    is_top, is_low = gy == n_gy - 1, gy == 0
    for field in range(4):
        folded = -mirror[field] if field < 2 else mirror[field]
        upper = jnp.where(is_top, folded, lat[1, field])
        lower = jnp.where(is_low, 0.0, lat[0, field])
        for layer in range(CHUNK):
            here = ocean[field, layer]
            up = ocean[field, layer - 1] if layer > 0 else above[field, 0]
            down = ocean[field, layer + 1] if layer < CHUNK - 1 else below[field, 0]
            sides = []
            for v in range(rows // 8):
                g = (field * CHUNK + layer) * (rows // 8) + v
                sides.append(pltpu.roll(bands[g // 64], lanes - 1 - 2 * (g % 64), 1))
            sides = jnp.concatenate(sides, axis=0)
            west = jnp.where(lane == 0, sides, pltpu.roll(here, 1, 1))
            east = jnp.where(lane == lanes - 1, sides, pltpu.roll(here, lanes - 1, 1))
            south = jnp.where(sub == 0, lower[layer : layer + 1], pltpu.roll(here, 1, 0))
            north = jnp.where(sub == rows - 1, upper[layer : layer + 1], pltpu.roll(here, rows - 1, 0))
            laplace = east + west + north + south - 4.0 * here
            value = here + mix[layer] * laplace + VERT_MIX * (up + down - 2.0 * here)
            if field == 0:
                value = value + spin * ocean[1, layer]
            if field == 1:
                value = value - spin * ocean[0, layer]
            out[field, layer] = value
            if field < 2 and layer == 0:

                @pl.when(step == 0)
                def _():
                    skin[field] = value


def ocean_step(n_gy, ocean, mix, lon, lat, mirror):
    fields, layers, rows, lanes = ocean.shape
    steps = layers // CHUNK
    block = pl.BlockSpec((fields, CHUNK, rows, lanes), lambda i: (0, i, 0, 0))
    one = (fields, 1, rows, lanes)
    return pl.pallas_call(
        functools.partial(ocean_kernel, n_gy),
        grid=(steps,),
        out_shape=(shape(*ocean.shape), shape(2, rows, lanes)),
        in_specs=[
            block,
            pl.BlockSpec(one, lambda i: (0, jnp.maximum(i * CHUNK - 1, 0), 0, 0)),
            pl.BlockSpec(one, lambda i: (0, jnp.minimum(i * CHUNK + CHUNK, layers - 1), 0, 0)),
            pl.BlockSpec((CHUNK, rows, lanes), lambda i: (i, 0, 0)),
            pl.BlockSpec((2, 1, 16, lanes), lambda i: (0, i, 0, 0)),
            pl.BlockSpec((2, fields, CHUNK, lanes), lambda i: (0, 0, i, 0)),
            pl.BlockSpec((fields, CHUNK, lanes), lambda i: (0, i, 0)),
        ],
        out_specs=(block, pl.BlockSpec((2, rows, lanes), lambda i: (0, 0, 0))),
        compiler_params=grant(24),
        name="ocean",
    )(ocean, ocean, ocean, mix, lon, lat, mirror)


def couple_kernel(n_gx, n_gy, sent, skin, cell, surface, current, *refs):
    here, there, back, home, *sems = refs
    gx, gy = lax.axis_index("gx"), lax.axis_index("gy")
    tiles, lanes = n_gx * n_gy, skin.shape[2]
    rows = skin.shape[1]
    barrier = pltpu.get_barrier_semaphore()
    for d in range(1, n_gx):
        peer = (lax.rem(gx + d, n_gx), gy)
        pl.semaphore_signal(barrier, inc=1, device_id=peer, device_id_type=MESH)
    for d in range(1, n_gy):
        peer = (gx, lax.rem(gy + d, n_gy))
        pl.semaphore_signal(barrier, inc=1, device_id=peer, device_id_type=MESH)
    pl.semaphore_wait(barrier, n_gx + n_gy - 2)

    def swap(source, middle, target, sems):
        send_x, recv_x, send_y, recv_y, local = sems
        own = pltpu.make_async_copy(source.at[gx], middle.at[gx], local)
        own.start()
        copies = []
        for d in range(1, n_gx):
            peer = lax.rem(gx + d, n_gx)
            copies.append(
                pltpu.make_async_remote_copy(
                    src_ref=source.at[peer],
                    dst_ref=middle.at[gx],
                    send_sem=send_x.at[d - 1],
                    recv_sem=recv_x.at[d - 1],
                    device_id=(peer, gy),
                    device_id_type=MESH,
                )
            )
        for copy in copies:
            copy.start()
        own.wait()
        for copy in copies:
            copy.wait()
        own = pltpu.make_async_copy(middle.at[:, gy], target.at[:, gy], local)
        own.start()
        copies = []
        for d in range(1, n_gy):
            peer = lax.rem(gy + d, n_gy)
            copies.append(
                pltpu.make_async_remote_copy(
                    src_ref=middle.at[:, peer],
                    dst_ref=target.at[:, gy],
                    send_sem=send_y.at[d - 1],
                    recv_sem=recv_y.at[d - 1],
                    device_id=(gx, peer),
                    device_id_type=MESH,
                )
            )
        for copy in copies:
            copy.start()
        own.wait()
        for copy in copies:
            copy.wait()

    swap(sent, here, there, sems[0:5])
    cells = jnp.concatenate([cell[0:1], cell[1:2]], axis=1)
    cell_row, cell_col = cells // lanes, cells % lanes
    pick = (lax.broadcasted_iota(jnp.int32, (lanes, 2 * tiles), 0) == cell_col).astype(jnp.bfloat16)
    in_row = lax.broadcasted_iota(jnp.int32, (rows, 2 * tiles), 0) == cell_row
    arrived = there[...].reshape(tiles, lanes).T
    spread = []
    for comp in range(2):
        values = jnp.concatenate([arrived[2 * comp : 2 * comp + 1], arrived[2 * comp + 1 : 2 * comp + 2]], axis=1)
        spread.append(jnp.where(in_row, values, 0.0))
    forcing = lax.dot_general(
        split(jnp.concatenate(spread, axis=0)),
        pick,
        (((1,), (1,)), ((), ())),
        preferred_element_type=jnp.float32,
    )
    level = skin[...].reshape(2 * rows, lanes) + joined(forcing)
    surface[...] = level.reshape(2, rows, lanes)
    found = joined(jnp.dot(split(level), pick, preferred_element_type=jnp.float32))
    replies = []
    for comp in range(2):
        values = jnp.where(in_row, found[comp * rows : (comp + 1) * rows], 0.0)
        values = jnp.sum(values, axis=0, keepdims=True)
        replies += [values[:, :tiles], values[:, tiles:]]
    replies.append(jnp.zeros((lanes - 4, tiles), jnp.float32))
    back[...] = jnp.concatenate(replies, axis=0).T.reshape(back.shape)
    swap(back, home, current, sems[5:10])


def couple(n_gx, n_gy, sent, skin, cell):
    tiles, lanes = n_gx * n_gy, skin.shape[2]
    box = (n_gx, n_gy, 1, lanes)
    dma = pltpu.SemaphoreType.DMA
    sems = [dma((n_gx - 1,)), dma((n_gx - 1,)), dma((n_gy - 1,)), dma((n_gy - 1,)), dma]
    return pl.pallas_call(
        functools.partial(couple_kernel, n_gx, n_gy),
        out_shape=(shape(*skin.shape), shape(*box)),
        in_specs=[VMEM] * 3,
        out_specs=(VMEM,) * 2,
        scratch_shapes=[pltpu.VMEM(box, jnp.float32)] * 4 + sems + sems,
        compiler_params=grant(4, collective_id=SUB, has_side_effects=True),
        name="couple",
    )(sent.reshape(box), skin, cell)


def finish_kernel(ocean, surface, current, slots, vel, vel_out, ocean_out, sem):
    copy = pltpu.make_async_copy(surface, ocean_out.at[pl.ds(0, 2), 0], sem)
    copy.start()
    blocks, discs = vel.shape[1], vel.shape[2]
    tiles = current.shape[0]
    got = current[...].reshape(tiles, discs).T
    spots = jnp.concatenate([slots[0:1], slots[1:2]], axis=1)
    place = lax.broadcasted_iota(jnp.int32, (blocks, 2 * tiles), 0) == spots
    for comp in range(2):
        values = jnp.concatenate([got[2 * comp : 2 * comp + 1], got[2 * comp + 1 : 2 * comp + 2]], axis=1)
        values = jnp.sum(jnp.where(place, values, 0.0), axis=1, keepdims=True)
        speed = vel[comp]
        vel_out[comp] = speed + DRAG_BACK * (values - speed)
    copy.wait()


def finish(ocean, surface, current, slots, vel):
    tiles = current.shape[0] * current.shape[1]
    return pl.pallas_call(
        finish_kernel,
        out_shape=(shape(*vel.shape), shape(*ocean.shape)),
        in_specs=[ANY, VMEM, VMEM, VMEM, VMEM],
        out_specs=(VMEM, ANY),
        scratch_shapes=[pltpu.SemaphoreType.DMA],
        input_output_aliases={0: 1},
        compiler_params=grant(4),
        name="finish",
    )(ocean, surface, current.reshape(tiles, 1, current.shape[3]), slots, vel)


def body(
    disc_pos,
    disc_vel,
    radius,
    bond_list,
    contact_mask,
    remap_block,
    ocean_state,
    mix_coef,
    remap_cell,
    fold_perm,
):
    n_gx, n_gy = lax.axis_size("gx"), lax.axis_size("gy")
    rows_dev, cols_dev, discs = radius.shape
    blocks = rows_dev * cols_dev
    slots = remap_block[0].T
    cell = remap_cell[0].T
    perm = fold_perm.reshape(1, discs)
    position = disc_pos.reshape(2, blocks, discs)
    velocity = disc_vel.reshape(2, blocks, discs)
    rad = radius.reshape(blocks, discs)
    bonds = bond_list.reshape(BONDS, blocks, discs)
    sea_shape = (4, mix_coef.shape[0], discs)
    columns, bottom, top, state, edges, mask = pack(n_gy, ocean_state, position, rad, contact_mask)
    flat = (4 * mix_coef.shape[0], discs)
    halo, lon, lat, rows, perms = exchange(
        0, n_gx, n_gy, state, edges, top.reshape(flat), bottom.reshape(flat), columns, perm
    )
    first = halo
    position, velocity, edges, turned = contact_step(
        0, n_gy, position, velocity, rad, bonds, mask, halo, first, rows, perms
    )
    halo, mirror = exchange(1, n_gx, n_gy, position, edges, turned)
    position, velocity, edges = contact_step(
        1, n_gy, position, velocity, rad, bonds, mask, halo, first
    )
    (halo,) = exchange(2, n_gx, n_gy, position, edges)
    position, velocity, sent = contact_step(
        2, n_gy, position, velocity, rad, bonds, mask, halo, first, slots
    )
    ocean, skin = ocean_step(
        n_gy, ocean_state, mix_coef, lon, lat.reshape(2, *sea_shape), mirror.reshape(sea_shape)
    )
    surface, current = couple(n_gx, n_gy, sent, skin, cell)
    vel_next, ocean_next = finish(ocean, surface, current, slots, velocity)
    return (position.reshape(disc_pos.shape), vel_next.reshape(disc_vel.shape), ocean_next)


def solution(mesh):
    in_specs = (
        P(None, "gy", "gx", None),
        P(None, "gy", "gx", None),
        P("gy", "gx", None),
        P(None, "gy", "gx", None),
        P(None, "gy", "gx"),
        P(("gx", "gy"), None, None),
        P(None, None, "gy", "gx"),
        P(None, "gy", "gx"),
        P(("gx", "gy"), None, None),
        P("gx"),
    )
    out_specs = (P(None, "gy", "gx", None), P(None, "gy", "gx", None), P(None, None, "gy", "gx"))
    return jax.shard_map(body, mesh=mesh, in_specs=in_specs, out_specs=out_specs, check_vma=False)
```

profile of v0, /device:TPU:1, one launch (start us, length us, event | category | flops | bytes accessed | tf_op | source)
XLA Modules:
  0.0 170.1 jit_solution(1015293120006021418)
XLA Ops:
  0.6 0.0 copy-start.12
  0.6 0.0 copy-start.10
  0.7 0.0 copy-start
  0.7 1.9 %copy-done = f32[4,48,32,128]{3,2,1,0:T(8,128)S(1)} copy-done((f32[4,48,32,128]{3,2,1,0:T(8,128)S(1)}, f32[4,48,32,128]{3,2,1,0:T(8,128)}, u32[]{:S(2)}) %copy-start) | copy-done | bytes 3145752
  2.6 0.8 copy-done.3
  3.4 0.9 copy-done.6
  4.3 0.8 copy-done.9
  5.1 1.8 %pack.1 = (f32[6,16,128]{2,1,0:T(8,128)S(1)}, f32[4,48,128]{2,1,0:T(8,128)S(1)}, f32[4,48,128]{2,1,0:T(8,128)S(1)}, f32[3,128,128]{2,1,0:T(8,128)S(1)}, f32[2,3,...) custom-call(f32[4,48,32,128]{3,2,1,0:T(8,128)S(1)} %copy-done, f32[2,128,128]{2,1,0:T(8,128)S(1)} %bitcast.26, ...), custom_call_target="tpu_custom_call" | custom-call | tf_op jit(solution)/shard_map/pack/pallas_call | solution.py:340
  6.9 0.0 copy-done.12
  6.9 20.0 %exchange_first.1 = (f32[8,3,16,128]{3,2,1,0:T(8,128)S(1)}, f32[2,6,16,128]{3,2,1,0:T(8,128)S(1)}, f32[2,192,128]{2,1,0:T(8,128)S(1)}, f32[16,16,128]{2,1,0:T(8,128)S(1)}, s32[16,1,128]{2,1,0:T(1,128)S(1)}) custom-call(f32[3,128,128]{2,1,0:T(8,128)S(1)} %get-tuple-element.33.refs_0_, f32[2,3,8,128]{3,2,1,0:T(8,128)S(1)} %get-tuple-element.34.refs_1_, ...), custom_call_target="tpu_custom_call" | custom-call | tf_op jit(solution)/shard_map/exchange_first/pallas_call | solution.py:527
  26.9 0.0 copy-done.2
  26.9 0.0 copy-done.4
  26.9 0.0 copy-start.7
  27.0 0.9 copy-done.7
  27.8 0.9 copy-done.8
  28.8 21.5 %contact_first.1 = (f32[2,128,128]{2,1,0:T(8,128)S(1)}, f32[2,128,128]{2,1,0:T(8,128)S(1)}, f32[2,2,8,128]{3,2,1,0:T(8,128)S(1)}, f32[16,16,128]{2,1,0:T(8,128)S(1)}) custom-call(f32[2,128,128]{2,1,0:T(8,128)S(1)} %bitcast.27, f32[2,128,128]{2,1,0:T(8,128)S(1)} %bitcast.29, f32[128,128]{1,0:T(8,128)S(1)} %bitcast.23, s32[4,128,128]{2,1,0:T(8,128)S(1)} %bitcast.19, ...), custom_call_target="tpu_custom_call" | custom-call | tf_op jit(solution)/shard_map/contact_first/pallas_call | solution.py:280
  50.2 15.0 %exchange_second.1 = (f32[8,2,16,128]{3,2,1,0:T(8,128)S(1)}, f32[12,16,128]{2,1,0:T(8,128)S(1)}) custom-call(f32[2,128,128]{2,1,0:T(8,128)S(1)} %get-tuple-element.41.refs_0_.pos, f32[2,2,8,128]{3,2,1,0:T(8,128)S(1)} %get-tuple-element.43.refs_1_, f32[16,16,128]{2,1,0:T(8,128)S(1)} %get-tuple-element.44.refs_2_), custom_call_target="tpu_custom_call" | custom-call | tf_op jit(solution)/shard_map/exchange_second/pallas_call | solution.py:527
  65.3 21.2 %contact.1 = (f32[2,128,128]{2,1,0:T(8,128)S(1)}, f32[2,128,128]{2,1,0:T(8,128)S(1)}, f32[2,2,8,128]{3,2,1,0:T(8,128)S(1)}) custom-call(f32[2,128,128]{2,1,0:T(8,128)S(1)} %get-tuple-element.41.refs_0_.pos, f32[2,128,128]{2,1,0:T(8,128)S(1)} %get-tuple-element.42.vel, f32[128,128]{1,0:T(8,128)S(1)} %bitcast.24, s32[4,128,128]{2,1,0:T(8,128)S(1)} %bitcast.20, ...), custom_call_target="tpu_custom_call" | custom-call | tf_op jit(solution)/shard_map/contact/pallas_call | solution.py:280
  86.4 20.6 %exchange_third.1.halo = f32[8,2,16,128]{3,2,1,0:T(8,128)S(1)} custom-call(f32[2,128,128]{2,1,0:T(8,128)S(1)} %get-tuple-element.46.refs_0_.pos, f32[2,2,8,128]{3,2,1,0:T(8,128)S(1)} %get-tuple-element.48.refs_1_), custom_call_target="tpu_custom_call" | custom-call | tf_op jit(solution)/shard_map/exchange_third/pallas_call | solution.py:527
  107.0 22.4 %contact_last.1 = (f32[2,128,128]{2,1,0:T(8,128)}, f32[2,128,128]{2,1,0:T(8,128)S(1)}, f32[128,1,128]{2,1,0:T(1,128)S(1)}) custom-call(f32[2,128,128]{2,1,0:T(8,128)S(1)} %get-tuple-element.46.refs_0_.pos, f32[2,128,128]{2,1,0:T(8,128)S(1)} %get-tuple-element.47.vel, f32[128,128]{1,0:T(8,128)S(1)} %bitcast.25, s32[4,128,128]{2,1,0:T(8,128)S(1)} %bitcast.21, ...), custom_call_target="tpu_custom_call" | custom-call | tf_op jit(solution)/shard_map/contact_last/pallas_call | solution.py:280
  129.5 0.0 copy-start.11
  129.5 5.6 %ocean.4 = (f32[4,48,32,128]{3,2,1,0:T(8,128)}, f32[2,32,128]{2,1,0:T(8,128)S(1)}) custom-call(f32[4,48,32,128]{3,2,1,0:T(8,128)S(1)} %copy-done.1, f32[4,48,32,128]{3,2,1,0:T(8,128)S(1)} %copy-done.1, f32[4,48,32,128]{3,2,1,0:T(8,128)S(1)} %copy-done.1, f32[48,32,128]{2,1,0:T(8,128)S(1)} %copy-done.5, f32[2,6,16,128]{3,2,1,0:T(8,128)S(1)} %get-tuple-element.50.lon, ...), custom_call_target="tpu_custom_call" | custom-call | tf_op jit(solution)/shard_map/ocean/pallas_call | solution.py:589
  135.1 33.7 %couple.1 = (f32[2,32,128]{2,1,0:T(8,128)S(1)}, f32[16,8,1,128]{3,2,1,0:T(1,128)S(1)}) custom-call(f32[16,8,1,128]{3,2,1,0:T(1,128)S(1)} %bitcast.34, f32[2,32,128]{2,1,0:T(8,128)S(1)} %get-tuple-element.55.skin, s32[2,128]{1,0:T(2,128)S(1)} %bitcast.37), custom_call_target="tpu_custom_call" | custom-call | tf_op jit(solution)/shard_map/couple/pallas_call | solution.py:699
  168.8 1.3 finish.1
  (12 shorter events, 0.0 us)
Async XLA Ops:
  0.6 6.3 %copy-start.12 = (s32[128]{0:T(128)S(1)}, s32[128]{0:T(128)}, u32[]{:S(2)}) copy-start(s32[128]{0:T(128)} %param.19) | copy-start | bytes 1540
  0.6 106.4 %copy-start.10 = (s32[1,128,2]{1,2,0:T(2,128)S(1)}, s32[1,128,2]{1,2,0:T(2,128)}, u32[]{:S(2)}) copy-start(s32[1,128,2]{1,2,0:T(2,128)} %param.15) | copy-start | bytes 3076
  0.7 1.9 %copy-start = (f32[4,48,32,128]{3,2,1,0:T(8,128)S(1)}, f32[4,48,32,128]{3,2,1,0:T(8,128)}, u32[]{:S(2)}) copy-start(f32[4,48,32,128]{3,2,1,0:T(8,128)} %below.1) | copy-start | bytes 9437188
  2.6 0.8 copy-start.3
  3.4 0.9 copy-start.6
  4.3 0.8 copy-start.9
  5.1 21.9 %copy-start.2 = (s32[4,8,16,128]{3,2,1,0:T(8,128)S(1)}, s32[4,8,16,128]{3,2,1,0:T(8,128)}, u32[]{:S(2)}) copy-start(s32[4,8,16,128]{3,2,1,0:T(8,128)} %param.13) | copy-start | bytes 786436
  5.1 21.9 %copy-start.4 = (f32[8,16,128]{2,1,0:T(8,128)S(1)}, f32[8,16,128]{2,1,0:T(8,128)}, u32[]{:S(2)}) copy-start(f32[8,16,128]{2,1,0:T(8,128)} %param.12) | copy-start | bytes 196612
  5.1 124.4 %copy-start.1 = (f32[4,48,32,128]{3,2,1,0:T(8,128)S(1)}, f32[4,48,32,128]{3,2,1,0:T(8,128)}, u32[]{:S(2)}) copy-start(f32[4,48,32,128]{3,2,1,0:T(8,128)} %below.1) | copy-start | bytes 9437188
  5.1 124.4 %copy-start.5 = (f32[48,32,128]{2,1,0:T(8,128)S(1)}, f32[48,32,128]{2,1,0:T(8,128)}, u32[]{:S(2)}) copy-start(f32[48,32,128]{2,1,0:T(8,128)} %mix.1) | copy-start | bytes 2359300
  26.9 0.9 copy-start.7
  27.8 0.9 copy-start.8
  129.5 5.6 %copy-start.11 = (s32[1,128,2]{1,2,0:T(2,128)S(1)}, s32[1,128,2]{1,2,0:T(2,128)}, u32[]{:S(2)}) copy-start(s32[1,128,2]{1,2,0:T(2,128)} %param.18) | copy-start | bytes 3076
where the time goes:
time: 172 us; the launch traced here: 170 us
  Pallas kernels  163 us (95%)
  local copies, waits for them, and re-layouts  6.23 us (4%)
    pallas_call x3, Pallas kernels, contact_step(): pl.pallas_call(functools.partial(contact_kernel, which, n_gy), out_shape=...  65.1 us
    pallas_call x3, Pallas kernels, exchange(): pl.pallas_call(functools.partial(exchange_kernel, which, n_gx, n_gy), out...  55.6 us
    pallas_call x1, Pallas kernels, couple(): pl.pallas_call(functools.partial(couple_kernel, n_gx, n_gy), out_shape=(s...  33.7 us
    unnamed x26, local copies, waits for them, and re-layouts  6.23 us
    pallas_call x1, Pallas kernels, ocean_step(): pl.pallas_call(functools.partial(ocean_kernel, n_gy), grid=(steps,), out_...  5.58 us

commit v1 on v0

--- a/solution.py
+++ b/solution.py
@@ -21,12 +21,16 @@
 TOGETHER = 4
 STATIC = 2
 ROWS = 2
+GROUP = 4
+ITEMS = 8
 CHUNK = 8
 TURNERS = 12
+EARLY = 32
 TURN_ROWS = 16
 MESH = pl.DeviceIdType.MESH
 VMEM = pl.BlockSpec(memory_space=pltpu.VMEM)
 ANY = pl.BlockSpec(memory_space=pl.ANY)
+HBM = pl.BlockSpec(memory_space=pltpu.HBM)
 
 
 def grant(mib, **more):
@@ -79,11 +83,45 @@
     lax.fori_loop(0, perms.shape[0], one, 0)
 
 
-def contact_kernel(which, n_gy, pos, vel, rad, bonds, mask, halo, halo_first, *refs):
+def own_setup(pos, rad, columns):
+    for comp in range(2):
+        columns[comp] = pos[comp].T
+    columns[2] = rad[...].T
+
+
+def gather_own(pos, rad, b):
+    own = (pos[0, pl.ds(b, 1), :], pos[1, pl.ds(b, 1), :], rad[pl.ds(b, 1), :])
+    return own, jnp.full((8, rad.shape[1]), b, jnp.int32)
+
+
+def visit(source, at, target, acc):
+    own, index = target
+    return pair_terms(*acc, *own, *[lane_take(source[k, at, :], index) for k in range(3)])
+
+
+def own_forces(first, count, pos, rad, columns, force):
+    blocks, discs = rad.shape
+    zero = jnp.zeros((8, discs), jnp.float32)
+
+    def some(t, carry):
+        for u in range(TOGETHER):
+            b = first + t * TOGETHER + u
+            target = gather_own(pos, rad, b)
+            acc = (zero, zero)
+            for c in range(discs // 8):
+                acc = visit(columns, pl.ds(c * 8, 8), target, acc)
+            for k in range(2):
+                force[k, pl.ds(b, 1), :] = jnp.sum(acc[k], axis=0, keepdims=True)
+        return carry
+
+    lax.fori_loop(0, count // TOGETHER, some, 0)
+
+
+def contact_kernel(which, n_gy, pos, vel, rad, bonds, mask, held, halo, halo_rad, *refs):
     last = which == SUB - 1
     if last:
         slots, pos_out, vel_out, sent, *scratch = refs
-    elif which == 0:
+    elif which == 1:
         rows, perms, pos_out, vel_out, edges, turned, *scratch = refs
 
         @pl.when(lax.axis_index("gy") == n_gy - 1)
@@ -92,28 +130,30 @@
 
     else:
         pos_out, vel_out, edges, *scratch = refs
-    wide, columns, found, found_t, force, tally, counts, sem = scratch
+    wide, found, found_t, force, tally, counts, work, sem = scratch
     rows_dev, cols_dev = wide.shape[1] - 2, pos.shape[1] // (wide.shape[1] - 2)
+    blocks, discs = rad.shape
     for comp in range(3):
         source = pos.at[comp] if comp < 2 else rad
-        frame = halo if comp < 2 else halo_first
+
+        def frame(side, first, size):
+            if comp < 2:
+                return halo[side, comp, pl.ds(first, size), :]
+            return halo_rad[side, pl.ds(first, size), :]
+
         for y in range(rows_dev):
             wide[comp, y + 1, pl.ds(1, cols_dev), :] = source[pl.ds(y * cols_dev, cols_dev), :]
-            wide[comp, y + 1, pl.ds(0, 1), :] = frame[3, comp, pl.ds(y, 1), :]
-            wide[comp, y + 1, pl.ds(cols_dev + 1, 1), :] = frame[4, comp, pl.ds(y, 1), :]
+            wide[comp, y + 1, pl.ds(0, 1), :] = frame(3, y, 1)
+            wide[comp, y + 1, pl.ds(cols_dev + 1, 1), :] = frame(4, y, 1)
         for side, y in ((0, 0), (5, rows_dev + 1)):
-            wide[comp, y, pl.ds(0, 1), :] = frame[side, comp, pl.ds(7, 1), :]
-            wide[comp, y, pl.ds(1, cols_dev), :] = frame[side + 1, comp]
-            wide[comp, y, pl.ds(cols_dev + 1, 1), :] = frame[side + 2, comp, pl.ds(0, 1), :]
-    blocks, discs = rad.shape
+            wide[comp, y, pl.ds(0, 1), :] = frame(side, 7, 1)
+            wide[comp, y, pl.ds(1, cols_dev), :] = frame(side + 1, 0, cols_dev)
+            wide[comp, y, pl.ds(cols_dev + 1, 1), :] = frame(side + 2, 0, 1)
     lane = lax.broadcasted_iota(jnp.int32, (8, discs), 1)
     lane_f = lane.astype(jnp.float32)
     tri_row = lax.broadcasted_iota(jnp.int32, (discs, 2 * discs), 0)
     tri_col = lax.broadcasted_iota(jnp.int32, (discs, 2 * discs), 1)
     triangle = (tri_row <= tri_col).astype(jnp.bfloat16)
-    for comp in range(2):
-        columns[comp] = pos[comp].T
-    columns[2] = rad[...].T
 
     def collect(start):
         def one_row(step_y, carry):
@@ -178,57 +218,54 @@
         copy.start()
         copy.wait()
 
-    def gather_own(b):
-        own = (pos[0, pl.ds(b, 1), :], pos[1, pl.ds(b, 1), :], rad[pl.ds(b, 1), :])
-        return own, jnp.full((8, discs), b, jnp.int32)
-
-    def visit(source, at, target, acc):
-        own, index = target
-        return pair_terms(*acc, *own, *[lane_take(source[k, at, :], index) for k in range(3)])
-
     zero = jnp.zeros((8, discs), jnp.float32)
-
-    def sweep(first, static_groups):
-        def some(t, carry):
-            blocks_here = [t * TOGETHER + u for u in range(TOGETHER)]
-            targets = [gather_own(b) for b in blocks_here]
-            accs = [(zero, zero)] * TOGETHER
+    span = 8 * GROUP
+
+    def group(b, g, scale, target, acc):
+        for c in range(GROUP):
+            at = pl.ds(pl.multiple_of(g * span + c * 8, 8), 8)
+            acc = visit(found_t, at, target, acc)
+        return acc
+
+    def sweep(static):
+        def some(t, size):
             for u in range(TOGETHER):
-                if first:
-                    for c in range(discs // 8):
-                        accs[u] = visit(columns, pl.ds(c * 8, 8), targets[u], accs[u])
-                for c in range(4 * static_groups):
-                    accs[u] = visit(found_t, pl.ds(c * 8, 8), targets[u], accs[u])
-
-            def group(g, accs):
-                accs = list(accs)
-                for u in range(TOGETHER):
-                    for c in range(4):
-                        at = pl.ds(pl.multiple_of(g * 32 + c * 8, 8), 8)
-                        accs[u] = visit(found_t, at, targets[u], accs[u])
-                return tuple(accs)
-
-            most = counts[0, blocks_here[0]]
-            for b in blocks_here[1:]:
-                most = jnp.maximum(most, counts[0, b])
-            accs = lax.fori_loop(static_groups, most, group, tuple(accs))
-            for u in range(TOGETHER):
+                b = t * TOGETHER + u
+                target = gather_own(pos, rad, b)
+                acc = (zero, zero)
+                for g in range(static):
+                    acc = group(b, g, None, target, acc)
+                if static:
+                    for k in range(2):
+                        force[k, pl.ds(b, 1), :] = jnp.sum(acc[k], axis=0, keepdims=True)
+                for g in range(static, discs // span):
+                    work[size] = b * 8 + g
+                    size = size + (counts[0, b] > g).astype(jnp.int32)
+            return size
+
+        size = lax.fori_loop(0, blocks // TOGETHER, some, 0)
+
+        def rest(i, carry):
+            for u in range(ITEMS):
+                slot = i * ITEMS + u
+                item = jnp.where(slot < size, work[slot], 0)
+                scale = jnp.where(slot < size, 1.0, 0.0)
+                b, g = item // 8, item % 8
+                target = gather_own(pos, rad, b)
+                acc = group(b, g, scale, target, (zero, zero))
                 for k in range(2):
-                    total = jnp.sum(accs[u][k], axis=0, keepdims=True)
-                    if first:
-                        force[k, pl.ds(blocks_here[u], 1), :] = total
-                    else:
-                        force[k, pl.ds(blocks_here[u], 1), :] += total
+                    total = jnp.sum(acc[k], axis=0, keepdims=True)
+                    force[k, pl.ds(b, 1), :] += total * scale
             return carry
 
-        lax.fori_loop(0, blocks // TOGETHER, some, 0)
+        lax.fori_loop(0, (size + ITEMS - 1) // ITEMS, rest, 0)
 
     collect(0.0)
-    sweep(True, STATIC)
+    sweep(STATIC)
 
     def more(p, carry):
         collect(p.astype(jnp.float32) * discs)
-        sweep(False, 0)
+        sweep(0)
         return carry
 
     lax.fori_loop(1, counts[8, 0], more, 0)
@@ -242,7 +279,7 @@
             bonded = lane_take(here, bonds[0, at, :])
             for p in range(1, BONDS):
                 bonded = bonded + lane_take(here, bonds[p, at, :])
-            total = BOND_STIFF * (bonded - BONDS * here) - STIFFNESS * force[k, at, :]
+            total = BOND_STIFF * (bonded - BONDS * here) - STIFFNESS * (held[k, at, :] + force[k, at, :])
             speed = vel[k, at, :] + total * scale
             vel_out[k, at, :] = speed
             pos_out[k, at, :] = here + TIME_STEP * speed
@@ -268,15 +305,15 @@
                 edges[side, comp] = pos_out[comp, at, :]
 
 
-def contact_step(which, n_gy, pos, vel, rad, bonds, mask, halo, halo_first, *extra):
+def contact_step(which, n_gy, pos, vel, rad, bonds, mask, held, halo, halo_rad, *extra):
     blocks, discs = rad.shape
     rows_dev = blocks // 16
     square = shape(2, blocks, discs)
     tail = shape(blocks, 1, discs) if which == SUB - 1 else shape(2, 2, rows_dev, discs)
     outs = (square, square, tail)
-    if which == 0:
+    if which == 1:
         outs += (shape(*extra[0].shape),)
-    args = (pos, vel, rad, bonds, mask, halo, halo_first) + extra
+    args = (pos, vel, rad, bonds, mask, held, halo, halo_rad) + extra
     return pl.pallas_call(
         functools.partial(contact_kernel, which, n_gy),
         out_shape=outs,
@@ -284,12 +321,12 @@
         out_specs=(VMEM,) * len(outs),
         scratch_shapes=[
             pltpu.VMEM((3, rows_dev + 2, 24, discs), jnp.float32),
-            pltpu.VMEM((3, discs, blocks), jnp.float32),
             pltpu.VMEM((4, blocks, discs), jnp.float32),
             pltpu.VMEM((3, discs, blocks), jnp.float32),
             pltpu.VMEM((2, blocks, discs), jnp.float32),
             pltpu.VMEM((16, blocks), jnp.int32),
             pltpu.SMEM((16, blocks), jnp.int32),
+            pltpu.SMEM((blocks * 4 + 2 * ITEMS,), jnp.int32),
             pltpu.SemaphoreType.DMA,
         ],
         compiler_params=grant(16),
@@ -297,7 +334,48 @@
     )(*args)
 
 
-def pack_kernel(n_gy, ocean, pos, rad, allowed, columns, bottom, top, state, edges, mask):
+def prep_kernel(n_gy, pos_in, rad_in, allowed_in, pos, rad, edges, mask, allowed, sems):
+    copies = [
+        pltpu.make_async_copy(allowed_in, allowed, sems.at[0]),
+        pltpu.make_async_copy(pos_in, pos, sems.at[1]),
+        pltpu.make_async_copy(rad_in, rad, sems.at[2]),
+    ]
+    for copy in copies:
+        copy.start()
+    copies[0].wait()
+    lane = lax.broadcasted_iota(jnp.int32, (8, 128), 1)
+    _, rows_dev, cols_dev = allowed.shape
+    spread = jnp.zeros((8, 128), jnp.float32)
+    for y in range(rows_dev):
+        part = allowed[:, y, :].astype(jnp.float32)
+        part = jnp.concatenate([part, jnp.zeros((8, 128 - cols_dev), jnp.float32)], axis=1)
+        spread = spread + (pltpu.roll(part, y * cols_dev, 1) if y else part)
+    which = lax.broadcasted_iota(jnp.int32, (8, 128), 0)
+    shift_y = jnp.where(which < 3, -1, jnp.where(which < 5, 0, 1))
+    row = lax.axis_index("gy") * rows_dev + lane // cols_dev + shift_y
+    spread = jnp.where((row >= 0) & (row < n_gy * rows_dev), spread, 0.0)
+    mask[...] = jnp.concatenate([spread, jnp.zeros((120, 128), jnp.float32)], axis=0).T
+    copies[1].wait()
+    copies[2].wait()
+    for comp in range(3):
+        source = pos.at[comp] if comp < 2 else rad
+        for side in range(2):
+            edges[side, comp] = source[pl.ds(side * 15, 8, stride=16), :]
+
+
+def prep(n_gy, pos, rad, allowed):
+    return pl.pallas_call(
+        functools.partial(prep_kernel, n_gy),
+        out_shape=(shape(*pos.shape), shape(*rad.shape), shape(2, 3, 8, 128), shape(*rad.shape)),
+        in_specs=[HBM] * 3,
+        out_specs=(VMEM,) * 4,
+        scratch_shapes=[pltpu.VMEM(allowed.shape, jnp.int32), pltpu.SemaphoreType.DMA((3,))],
+        compiler_params=grant(4),
+        name="prep",
+    )(pos, rad, allowed)
+
+
+def pack_kernel(ocean, after, columns, bottom, top):
     rows = ocean.shape[2]
     lane = lax.broadcasted_iota(jnp.int32, (8, 128), 1)
     packed = [jnp.zeros((8, 128), jnp.float32)] * 2
@@ -312,69 +390,36 @@
     bottom[...] = ocean[:, :, 0, :]
     top[...] = ocean[:, :, rows - 1, :]
 
-    @pl.when(pl.program_id(0) == 0)
-    def _():
-        for comp in range(3):
-            source = pos.at[comp] if comp < 2 else rad
-            state[comp] = source[...]
-            for side in range(2):
-                edges[side, comp] = source[pl.ds(side * 15, 8, stride=16), :]
-        _, rows_dev, cols_dev = allowed.shape
-        spread = jnp.zeros((8, 128), jnp.float32)
-        for y in range(rows_dev):
-            part = allowed[:, y, :].astype(jnp.float32)
-            part = jnp.concatenate([part, jnp.zeros((8, 128 - cols_dev), jnp.float32)], axis=1)
-            spread = spread + (pltpu.roll(part, y * cols_dev, 1) if y else part)
-        which = lax.broadcasted_iota(jnp.int32, (8, 128), 0)
-        shift_y = jnp.where(which < 3, -1, jnp.where(which < 5, 0, 1))
-        row = lax.axis_index("gy") * rows_dev + lane // cols_dev + shift_y
-        spread = jnp.where((row >= 0) & (row < n_gy * rows_dev), spread, 0.0)
-        mask[...] = jnp.concatenate([spread, jnp.zeros((120, 128), jnp.float32)], axis=0).T
-
-
-def pack(n_gy, ocean, pos, rad, allowed):
+
+def pack(ocean, after):
     fields, layers, rows, lanes = ocean.shape
     steps = layers // CHUNK
-    whole = lambda *dims: pl.BlockSpec(dims, lambda i: (0,) * len(dims))
     row = pl.BlockSpec((fields, CHUNK, lanes), lambda i: (0, i, 0))
     return pl.pallas_call(
-        functools.partial(pack_kernel, n_gy),
+        pack_kernel,
         grid=(steps,),
         out_shape=(
             shape(steps, 16, lanes),
             shape(fields, layers, lanes),
             shape(fields, layers, lanes),
-            shape(3, *rad.shape),
-            shape(2, 3, 8, lanes),
-            shape(*rad.shape),
         ),
-        in_specs=[
-            pl.BlockSpec((fields, CHUNK, rows, lanes), lambda i: (0, i, 0, 0)),
-            whole(*pos.shape),
-            whole(*rad.shape),
-            whole(*allowed.shape),
-        ],
-        out_specs=(
-            pl.BlockSpec((1, 16, lanes), lambda i: (i, 0, 0)),
-            row,
-            row,
-            whole(3, *rad.shape),
-            whole(2, 3, 8, lanes),
-            whole(*rad.shape),
-        ),
+        in_specs=[pl.BlockSpec((fields, CHUNK, rows, lanes), lambda i: (0, i, 0, 0)), ANY],
+        out_specs=(pl.BlockSpec((1, 16, lanes), lambda i: (i, 0, 0)), row, row),
         compiler_params=grant(8),
         name="pack",
-    )(ocean, pos, rad, allowed)
+    )(ocean, after)
 
 
 def exchange_kernel(which, n_gx, n_gy, *refs):
     if which == 0:
-        state, edges, top, bottom, columns, perm, halo, lon, lat, rows, perms, *sems = refs
-        send_sem, recv_sem, sea_send, sea_recv, far_send, far_recv, perm_send, perm_recv, own = sems
+        pos, rad, edges, halo, held, halo_rad, columns, send_sem, recv_sem, rad_send, rad_recv = refs
     elif which == 1:
-        state, edges, turned, halo, mirror, send_sem, recv_sem, far_send, far_recv, own = refs
+        pos, rad, edges, top, bottom, sides, perm, halo, held, lon, lat, rows, perms, *scratch = refs
+        columns, send_sem, recv_sem, sea_send, sea_recv, far_send, far_recv, *scratch = scratch
+        perm_send, perm_recv, own = scratch
     else:
-        state, edges, halo, send_sem, recv_sem = refs
+        pos, rad, edges, turned, halo, held, mirror, columns, send_sem, recv_sem, *scratch = refs
+        far_send, far_recv, own = scratch
     gx, gy = lax.axis_index("gx"), lax.axis_index("gy")
     is_top = gy == n_gy - 1
 
@@ -384,12 +429,20 @@
     barrier = pltpu.get_barrier_semaphore()
     for dy, dx in NEIGHBOURS:
         pl.semaphore_signal(barrier, inc=1, device_id=at(dx, dy), device_id_type=MESH)
-    if which < 2:
+    if which > 0:
 
         @pl.when(is_top)
         def _():
             for d in range(1, n_gx):
                 pl.semaphore_signal(barrier, inc=1, device_id=at(d, 0), device_id_type=MESH)
+
+    blocks = rad.shape[0]
+    own_setup(pos, rad, columns)
+    own_forces(0, EARLY, pos, rad, columns, held)
+    if which > 0:
+
+        @pl.when(is_top)
+        def _():
             pl.semaphore_wait(barrier, len(NEIGHBOURS) + n_gx - 1)
 
         @pl.when(jnp.logical_not(is_top))
@@ -409,130 +462,148 @@
             device_id_type=MESH,
         )
 
-    blocks = state.shape[1]
-    copies = []
-    for k, (sy, sx) in enumerate(NEIGHBOURS):
-        device = at(-sx, -sy)
-        first = 0 if sy == 1 else blocks - 16
-        if sy == 0:
-            source, target = edges.at[0 if sx == 1 else 1], halo.at[k, :, pl.ds(0, 8), :]
-        elif sx == 0:
-            source, target = state.at[:, pl.ds(first, 16), :], halo.at[k]
-        else:
-            first = first if sx == 1 else first + 8
-            source, target = state.at[:, pl.ds(first, 8), :], halo.at[k, :, pl.ds(0, 8), :]
-        copies.append(send(source, target, (send_sem, recv_sem), k, device))
+    def halo_copies(body, part, target, sems):
+        copies = []
+        for k, (sy, sx) in enumerate(NEIGHBOURS):
+            first = 0 if sy == 1 else blocks - 16
+            first = first + 8 if sx == -1 else first
+            size = 16 if sx == 0 else 8
+            source = part(0 if sx == 1 else 1) if sy == 0 else body(pl.ds(first, size))
+            copies.append(send(source, target(k, pl.ds(0, size)), sems, k, at(-sx, -sy)))
+        return copies
+
+    copies = halo_copies(
+        lambda rows: pos.at[:, rows, :],
+        lambda side: edges.at[side, pl.ds(0, 2)],
+        lambda k, rows: halo.at[k, :, rows, :],
+        (send_sem, recv_sem),
+    )
+    if which == 0:
+        copies += halo_copies(
+            lambda rows: rad.at[rows, :],
+            lambda side: edges.at[side, 2],
+            lambda k, rows: halo_rad.at[k, rows, :],
+            (rad_send, rad_recv),
+        )
     for copy in copies:
         copy.start()
-    if which == 0:
+    if which == 1:
         sea = (sea_send, sea_recv)
         later = [
-            send(columns, lon.at[0], sea, 0, at(1, 0)),
-            send(columns, lon.at[1], sea, 1, at(-1, 0)),
+            send(sides, lon.at[0], sea, 0, at(1, 0)),
+            send(sides, lon.at[1], sea, 1, at(-1, 0)),
             send(top, lat.at[0], sea, 2, at(0, 1)),
             send(bottom, lat.at[1], sea, 3, at(0, -1)),
         ]
         copies += later
 
-    if which == 0:
+    if which == 1:
+        first = pl.multiple_of(jnp.minimum(gx, TURNERS - 1) * TURN_ROWS, TURN_ROWS)
+        kept = pltpu.make_async_copy(perm, perms.at[gx], own.at[0])
+        mine = pltpu.make_async_copy(top.at[pl.ds(first, TURN_ROWS), :], rows.at[gx], own.at[1])
+        notes, far = [], []
+        for d in range(1, n_gx):
+            peer = lax.rem(gx + d, n_gx)
+            start = pl.multiple_of(jnp.minimum(peer, TURNERS - 1) * TURN_ROWS, TURN_ROWS)
+            notes.append(send(perm, perms.at[gx], (perm_send, perm_recv), d - 1, at(d, 0)))
+            source = top.at[pl.ds(start, TURN_ROWS), :]
+            far.append(send(source, rows.at[gx], (far_send, far_recv), d - 1, at(d, 0)))
 
         @pl.when(is_top)
         def _():
-            kept = pltpu.make_async_copy(perm, perms.at[gx], own.at[0])
             kept.start()
-            notes = [
-                send(perm, perms.at[gx], (perm_send, perm_recv), d - 1, at(d, 0))
-                for d in range(1, n_gx)
-            ]
-            for note in notes:
-                note.start()
-            far = []
             for d in range(1, n_gx):
-                peer = lax.rem(gx + d, n_gx)
-                first = pl.multiple_of(jnp.minimum(peer, TURNERS - 1) * TURN_ROWS, TURN_ROWS)
-                source = top.at[pl.ds(first, TURN_ROWS), :]
-                far.append(send(source, rows.at[gx], (far_send, far_recv), d - 1, at(d, 0)))
-
-                @pl.when(peer < TURNERS)
-                def _(copy=far[-1]):
+                notes[d - 1].start()
+
+                @pl.when(lax.rem(gx + d, n_gx) < TURNERS)
+                def _(copy=far[d - 1]):
                     copy.start()
 
             @pl.when(gx < TURNERS)
             def _():
-                first = pl.multiple_of(jnp.minimum(gx, TURNERS - 1) * TURN_ROWS, TURN_ROWS)
-                mine = pltpu.make_async_copy(top.at[pl.ds(first, TURN_ROWS), :], rows.at[gx], own.at[1])
                 mine.start()
+
+        for copy in later:
+            copy.start()
+
+    if which == 2:
+        me = jnp.minimum(gx, TURNERS - 1)
+        mine = pltpu.make_async_copy(turned.at[gx], mirror.at[me], own)
+        far = []
+        for d in range(1, n_gx):
+            source = turned.at[lax.rem(gx + d, n_gx)]
+            far.append(send(source, mirror.at[me], (far_send, far_recv), d - 1, at(d, 0)))
+
+        @pl.when(is_top & (gx < TURNERS))
+        def _():
+            mine.start()
+            for copy in far:
+                copy.start()
+
+    own_forces(EARLY, blocks - EARLY, pos, rad, columns, held)
+    for copy in copies:
+        copy.wait()
+    if which == 1:
+
+        @pl.when(is_top)
+        def _():
+            kept.wait()
+            for d in range(1, n_gx):
+                notes[d - 1].wait()
+
+                @pl.when(lax.rem(gx + d, n_gx) < TURNERS)
+                def _(copy=far[d - 1]):
+                    copy.wait_send()
+
+            @pl.when(gx < TURNERS)
+            def _():
                 mine.wait()
                 for copy in far:
                     copy.wait_recv()
 
-            for d in range(1, n_gx):
-
-                @pl.when(lax.rem(gx + d, n_gx) < TURNERS)
-                def _(copy=far[d - 1]):
-                    copy.wait_send()
-
-            kept.wait()
-            for note in notes:
-                note.wait()
-
-        for copy in later:
-            copy.start()
-
-    if which == 1:
+    if which == 2:
+
+        @pl.when(is_top & (gx < TURNERS))
+        def _():
+            mine.wait()
+            for copy in far:
+                copy.wait_send()
 
         @pl.when(is_top)
         def _():
-            me = jnp.minimum(gx, TURNERS - 1)
-            far = [
-                send(turned.at[lax.rem(gx + d, n_gx)], mirror.at[me], (far_send, far_recv), d - 1, at(d, 0))
-                for d in range(1, n_gx)
-            ]
-
-            @pl.when(gx < TURNERS)
-            def _():
-                mine = pltpu.make_async_copy(turned.at[gx], mirror.at[me], own)
-                mine.start()
-                for copy in far:
-                    copy.start()
-                mine.wait()
-                for copy in far:
-                    copy.wait_send()
-
             for d in range(1, n_gx):
 
                 @pl.when(lax.rem(gx - d + n_gx, n_gx) < TURNERS)
                 def _(copy=far[d - 1]):
                     copy.wait_recv()
 
-    for copy in copies:
-        copy.wait()
-
-
-def exchange(which, n_gx, n_gy, state, edges, *args):
-    comps = state.shape[0]
-    lanes = state.shape[2]
-    outs = [shape(8, comps, 16, lanes)]
+
+def exchange(which, n_gx, n_gy, pos, rad, edges, *args):
+    lanes = rad.shape[1]
+    outs = [shape(8, 2, 16, lanes), shape(*pos.shape)]
     dma = pltpu.SemaphoreType.DMA
-    scratch = [dma((8,)), dma((8,))]
+    scratch = [pltpu.VMEM((3, lanes, rad.shape[0]), jnp.float32), dma((8,)), dma((8,))]
     far = [dma((n_gx - 1,)), dma((n_gx - 1,))]
     if which == 0:
-        top, bottom, columns, perm = args
-        outs += [shape(2, *columns.shape), shape(2, *top.shape)]
+        outs += [shape(8, 16, lanes)]
+        scratch += [dma((8,)), dma((8,))]
+    if which == 1:
+        top, bottom, sides, perm = args
+        outs += [shape(2, *sides.shape), shape(2, *top.shape)]
         outs += [shape(n_gx, TURN_ROWS, lanes), jax.ShapeDtypeStruct((n_gx, 1, lanes), jnp.int32)]
         scratch += [dma((4,)), dma((4,))] + far + far + [dma((2,))]
-    if which == 1:
+    if which == 2:
         outs += [shape(TURNERS, TURN_ROWS, lanes)]
         scratch += far + [dma]
     return pl.pallas_call(
         functools.partial(exchange_kernel, which, n_gx, n_gy),
         out_shape=tuple(outs),
-        in_specs=[VMEM] * (2 + len(args)),
+        in_specs=[VMEM] * (3 + len(args)),
         out_specs=(VMEM,) * len(outs),
         scratch_shapes=scratch,
-        compiler_params=grant(4, collective_id=which, has_side_effects=True),
+        compiler_params=grant(8, collective_id=which, has_side_effects=True),
         name=("exchange_first", "exchange_second", "exchange_third")[which],
-    )(state, edges, *args)
+    )(pos, rad, edges, *args)
 
 
 def ocean_kernel(n_gy, ocean, above, below, mix, lon, lat, mirror, out, skin):
@@ -760,22 +831,22 @@
     rad = radius.reshape(blocks, discs)
     bonds = bond_list.reshape(BONDS, blocks, discs)
     sea_shape = (4, mix_coef.shape[0], discs)
-    columns, bottom, top, state, edges, mask = pack(n_gy, ocean_state, position, rad, contact_mask)
     flat = (4 * mix_coef.shape[0], discs)
-    halo, lon, lat, rows, perms = exchange(
-        0, n_gx, n_gy, state, edges, top.reshape(flat), bottom.reshape(flat), columns, perm
+    position, rad, edges, mask = prep(n_gy, position, rad, contact_mask)
+    halo, held, halo_rad = exchange(0, n_gx, n_gy, position, rad, edges)
+    position, velocity, edges = contact_step(
+        0, n_gy, position, velocity, rad, bonds, mask, held, halo, halo_rad
     )
-    first = halo
+    sides, bottom, top = pack(ocean_state, edges)
+    halo, held, lon, lat, rows, perms = exchange(
+        1, n_gx, n_gy, position, rad, edges, top.reshape(flat), bottom.reshape(flat), sides, perm
+    )
     position, velocity, edges, turned = contact_step(
-        0, n_gy, position, velocity, rad, bonds, mask, halo, first, rows, perms
+        1, n_gy, position, velocity, rad, bonds, mask, held, halo, halo_rad, rows, perms
     )
-    halo, mirror = exchange(1, n_gx, n_gy, position, edges, turned)
-    position, velocity, edges = contact_step(
-        1, n_gy, position, velocity, rad, bonds, mask, halo, first
-    )
-    (halo,) = exchange(2, n_gx, n_gy, position, edges)
+    halo, held, mirror = exchange(2, n_gx, n_gy, position, rad, edges, turned)
     position, velocity, sent = contact_step(
-        2, n_gy, position, velocity, rad, bonds, mask, halo, first, slots
+        2, n_gy, position, velocity, rad, bonds, mask, held, halo, halo_rad, slots
     )
     ocean, skin = ocean_step(
         n_gy, ocean_state, mix_coef, lon, lat.reshape(2, *sea_shape), mirror.reshape(sea_shape)

time: 172 us -> 146 us (0.85)
  Pallas kernels: 163 us -> 138 us
    pallas_call x3, Pallas kernels: 55.6 us -> 36.4 us  [exchange(): pl.pallas_call(functools.partial(exchange_kernel, which, n_gx, n_gy), out...]
    pallas_call x3, Pallas kernels: 65.1 us -> 61.7 us  [contact_step(): pl.pallas_call(functools.partial(contact_kernel, which, n_gy), out_shape=...]
    pallas_call x1, Pallas kernels: 33.7 us -> 31.5 us  [couple(): pl.pallas_call(functools.partial(couple_kernel, n_gx, n_gy), out_shape=(s...]
    unnamed x26 -> x24, local copies, waits for them, and re-layouts: 6.23 us -> 6.3 us
where the time goes in v1:
time: 146 us
  Pallas kernels  138 us (95%)
  local copies, waits for them, and re-layouts  6.3 us (4%)
    pallas_call x3, Pallas kernels, contact_step(): pl.pallas_call(functools.partial(contact_kernel, which, n_gy), out_shape=...  61.7 us
    pallas_call x3, Pallas kernels, exchange(): pl.pallas_call(functools.partial(exchange_kernel, which, n_gx, n_gy), out...  36.4 us
    pallas_call x1, Pallas kernels, couple(): pl.pallas_call(functools.partial(couple_kernel, n_gx, n_gy), out_shape=(s...  31.5 us
    unnamed x24, local copies, waits for them, and re-layouts  6.3 us
    pallas_call x1, Pallas kernels, ocean_step(): pl.pallas_call(functools.partial(ocean_kernel, n_gy), grid=(steps,), out_...  5.58 us

profile of v1, /device:TPU:1, one launch (start us, length us, event | category | flops | bytes accessed | tf_op | source)
XLA Modules:
  0.0 145.6 jit_solution(5006393974912765985)
XLA Ops:
  0.6 0.0 copy-start.3
  0.6 0.0 copy-start.6
  0.7 0.9 copy-done.6
  1.6 0.8 copy-done.7
  2.4 0.8 copy-done.8
  3.2 0.5 prep.1
  3.7 0.0 copy-start.9
  3.7 15.2 %exchange_first.1 = (f32[8,2,16,128]{3,2,1,0:T(8,128)S(1)}, f32[2,128,128]{2,1,0:T(8,128)S(1)}, f32[8,16,128]{2,1,0:T(8,128)S(1)}) custom-call(f32[2,128,128]{2,1,0:T(8,128)S(1)} %get-tuple-element.38.refs_0_.pos, f32[128,128]{1,0:T(8,128)S(1)} %get-tuple-element.39.refs_1_.rad, f32[2,3,8,128]{3,2,1,0:T(8,128)S(1)} %get-tuple-element.41.refs_2_), custom_call_target="tpu_custom_call" | custom-call | tf_op jit(solution)/shard_map/exchange_first/pallas_call | solution.py:598
  18.9 0.0 copy-start.2
  18.9 0.9 copy-done.2
  19.9 0.9 copy-done.5
  20.8 22.7 %contact_first.1 = (f32[2,128,128]{2,1,0:T(8,128)S(1)}, f32[2,128,128]{2,1,0:T(8,128)S(1)}, f32[2,2,8,128]{3,2,1,0:T(8,128)S(1)}) custom-call(f32[2,128,128]{2,1,0:T(8,128)S(1)} %get-tuple-element.38.refs_0_.pos, f32[2,128,128]{2,1,0:T(8,128)S(1)} %bitcast.23, f32[128,128]{1,0:T(8,128)S(1)} %get-tuple-element.39.refs_1_.rad, s32[4,128,128]{2,1,0:T(8,128)S(1)} %bitcast.19, ...), custom_call_target="tpu_custom_call" | custom-call | tf_op jit(solution)/shard_map/contact_first/pallas_call | solution.py:317
  43.5 0.0 copy-start
  43.5 1.9 %copy-done = f32[4,48,32,128]{3,2,1,0:T(8,128)S(1)} copy-done((f32[4,48,32,128]{3,2,1,0:T(8,128)S(1)}, f32[4,48,32,128]{3,2,1,0:T(8,128)}, u32[]{:S(2)}) %copy-start) | copy-done | bytes 3145752
  45.4 1.6 %pack.1 = (f32[6,16,128]{2,1,0:T(8,128)S(1)}, f32[4,48,128]{2,1,0:T(8,128)S(1)}, f32[4,48,128]{2,1,0:T(8,128)S(1)}) custom-call(f32[4,48,32,128]{3,2,1,0:T(8,128)S(1)} %copy-done, f32[2,2,8,128]{3,2,1,0:T(8,128)S(1)} %get-tuple-element.47.after.refs_2_), custom_call_target="tpu_custom_call" | custom-call | tf_op jit(solution)/shard_map/pack/pallas_call | solution.py:398
  47.0 0.0 copy-done.11
  47.0 10.8 %exchange_second.1 = (f32[8,2,16,128]{3,2,1,0:T(8,128)S(1)}, f32[2,128,128]{2,1,0:T(8,128)S(1)}, f32[2,6,16,128]{3,2,1,0:T(8,128)S(1)}, f32[2,192,128]{2,1,0:T(8...) custom-call(f32[2,128,128]{2,1,0:T(8,128)S(1)} %get-tuple-element.45.refs_0_.pos, ...), custom_call_target="tpu_custom_call" | custom-call | tf_op jit(solution)/shard_map/exchange_second/pallas_call | solution.py:598
  57.8 22.9 %contact.1 = (f32[2,128,128]{2,1,0:T(8,128)S(1)}, f32[2,128,128]{2,1,0:T(8,128)S(1)}, f32[2,2,8,128]{3,2,1,0:T(8,128)S(1)}, f32[16,16,128]{2,1,0:T(8,128)S(1)}) custom-call(f32[2,128,128]{2,1,0:T(8,128)S(1)} %get-tuple-element.45.refs_0_.pos, f32[2,128,128]{2,1,0:T(8,128)S(1)} %get-tuple-element.46.vel, f32[128,128]{1,0:T(8,128)S(1)} %get-tuple-element.39.refs_1_.rad, ...), custom_call_target="tpu_custom_call" | custom-call | tf_op jit(solution)/shard_map/contact/pallas_call | solution.py:317
  80.8 10.4 %exchange_third.1 = (f32[8,2,16,128]{3,2,1,0:T(8,128)S(1)}, f32[2,128,128]{2,1,0:T(8,128)S(1)}, f32[12,16,128]{2,1,0:T(8,128)S(1)}) custom-call(f32[2,128,128]{2,1,0:T(8,128)S(1)} %get-tuple-element.55.refs_0_.pos, f32[128,128]{1,0:T(8,128)S(1)} %get-tuple-element.39.refs_1_.rad, f32[2,2,8,128]{3,2,1,0:T(8,128)S(1)} %get-tuple-element.57.refs_2_, ...), custom_call_target="tpu_custom_call" | custom-call | tf_op jit(solution)/shard_map/exchange_third/pallas_call | solution.py:598
  91.2 16.0 %contact_last.1 = (f32[2,128,128]{2,1,0:T(8,128)}, f32[2,128,128]{2,1,0:T(8,128)S(1)}, f32[128,1,128]{2,1,0:T(1,128)S(1)}) custom-call(f32[2,128,128]{2,1,0:T(8,128)S(1)} %get-tuple-element.55.refs_0_.pos, f32[2,128,128]{2,1,0:T(8,128)S(1)} %get-tuple-element.56.vel, f32[128,128]{1,0:T(8,128)S(1)} %get-tuple-element.39.refs_1_.rad, ...), custom_call_target="tpu_custom_call" | custom-call | tf_op jit(solution)/shard_map/contact_last/pallas_call | solution.py:317
  107.2 0.0 copy-start.10
  107.2 5.6 %ocean.4 = (f32[4,48,32,128]{3,2,1,0:T(8,128)}, f32[2,32,128]{2,1,0:T(8,128)S(1)}) custom-call(f32[4,48,32,128]{3,2,1,0:T(8,128)S(1)} %copy-done.1, f32[4,48,32,128]{3,2,1,0:T(8,128)S(1)} %copy-done.1, f32[4,48,32,128]{3,2,1,0:T(8,128)S(1)} %copy-done.1, f32[48,32,128]{2,1,0:T(8,128)S(1)} %copy-done.4, f32[2,6,16,128]{3,2,1,0:T(8,128)S(1)} %get-tuple-element.62.lon, ...), custom_call_target="tpu_custom_call" | custom-call | tf_op jit(solution)/shard_map/ocean/pallas_call | solution.py:660
  112.8 31.5 %couple.1 = (f32[2,32,128]{2,1,0:T(8,128)S(1)}, f32[16,8,1,128]{3,2,1,0:T(1,128)S(1)}) custom-call(f32[16,8,1,128]{3,2,1,0:T(1,128)S(1)} %bitcast.30, f32[2,32,128]{2,1,0:T(8,128)S(1)} %get-tuple-element.67.skin, s32[2,128]{1,0:T(2,128)S(1)} %bitcast.33), custom_call_target="tpu_custom_call" | custom-call | tf_op jit(solution)/shard_map/couple/pallas_call | solution.py:770
  144.3 1.3 finish.1
  (11 shorter events, 0.0 us)
Async XLA Ops:
  0.6 57.2 %copy-start.3 = (s32[4,8,16,128]{3,2,1,0:T(8,128)S(1)}, s32[4,8,16,128]{3,2,1,0:T(8,128)}, u32[]{:S(2)}) copy-start(s32[4,8,16,128]{3,2,1,0:T(8,128)} %param.13) | copy-start | bytes 786436
  0.6 0.9 copy-start.6
  1.6 0.8 copy-start.7
  2.4 0.8 copy-start.8
  3.2 43.8 %copy-start.11 = (s32[128]{0:T(128)S(1)}, s32[128]{0:T(128)}, u32[]{:S(2)}) copy-start(s32[128]{0:T(128)} %param.19) | copy-start | bytes 1540
  3.7 87.5 %copy-start.9 = (s32[1,128,2]{1,2,0:T(2,128)S(1)}, s32[1,128,2]{1,2,0:T(2,128)}, u32[]{:S(2)}) copy-start(s32[1,128,2]{1,2,0:T(2,128)} %param.15) | copy-start | bytes 3076
  18.9 1.0 copy-start.2
  19.8 0.9 copy-start.5
  20.8 86.4 %copy-start.4 = (f32[48,32,128]{2,1,0:T(8,128)S(1)}, f32[48,32,128]{2,1,0:T(8,128)}, u32[]{:S(2)}) copy-start(f32[48,32,128]{2,1,0:T(8,128)} %mix.1) | copy-start | bytes 2359300
  43.5 1.9 %copy-start = (f32[4,48,32,128]{3,2,1,0:T(8,128)S(1)}, f32[4,48,32,128]{3,2,1,0:T(8,128)}, u32[]{:S(2)}) copy-start(f32[4,48,32,128]{3,2,1,0:T(8,128)} %below.1) | copy-start | bytes 9437188
  45.4 61.9 %copy-start.1 = (f32[4,48,32,128]{3,2,1,0:T(8,128)S(1)}, f32[4,48,32,128]{3,2,1,0:T(8,128)}, u32[]{:S(2)}) copy-start(f32[4,48,32,128]{3,2,1,0:T(8,128)} %below.1) | copy-start | bytes 9437188
  107.2 5.6 %copy-start.10 = (s32[1,128,2]{1,2,0:T(2,128)S(1)}, s32[1,128,2]{1,2,0:T(2,128)}, u32[]{:S(2)}) copy-start(s32[1,128,2]{1,2,0:T(2,128)} %param.18) | copy-start | bytes 3076

commit v2 on v1

--- a/solution.py
+++ b/solution.py
@@ -18,11 +18,12 @@
 VERT_MIX = 0.1
 SPIN_RATE = 0.3
 NEIGHBOURS = ((-1, -1), (-1, 0), (-1, 1), (0, -1), (0, 1), (1, -1), (1, 0), (1, 1))
-TOGETHER = 4
-STATIC = 2
-ROWS = 2
-GROUP = 4
-ITEMS = 8
+ROWS = 1
+OWN_STEP = 8
+NEAR_STEP = 16
+REST_STEP = 8
+HALF = 64
+MARKS = 16
 CHUNK = 8
 TURNERS = 12
 EARLY = 32
@@ -55,15 +56,66 @@
 
 
 def lane_take(rows, index):
-    return jnp.take_along_axis(rows, index, axis=1, mode="promise_in_bounds")
-
-
-def pair_terms(acc_x, acc_y, own_x, own_y, own_r, other_x, other_y, other_r):
-    sep_x = other_x - own_x
-    sep_y = other_y - own_y
-    inverse = lax.rsqrt(sep_x * sep_x + sep_y * sep_y + SOFTEN)
-    push = jnp.maximum((other_r + own_r) * inverse - 1.0, 0.0)
-    return acc_x + push * sep_x, acc_y + push * sep_y
+    return lax.gather(
+        rows,
+        index[..., None],
+        lax.GatherDimensionNumbers(
+            offset_dims=(),
+            collapsed_slice_dims=(1,),
+            start_index_map=(1,),
+            operand_batching_dims=(0,),
+            start_indices_batching_dims=(0,),
+        ),
+        slice_sizes=(1, 1),
+        mode=lax.GatherScatterMode.PROMISE_IN_BOUNDS,
+    )
+
+
+def pieces(value):
+    high = value.astype(jnp.bfloat16).astype(jnp.float32)
+    middle = (value - high).astype(jnp.bfloat16).astype(jnp.float32)
+    return high, middle, value - high - middle
+
+
+def write_marks(parts, marks):
+    for comp, part in enumerate(parts):
+        for i, piece in enumerate(pieces(part)):
+            marks[pl.ds(3 * comp + i, part.shape[0], stride=MARKS), :] = piece
+
+
+def other_side(marks):
+    row = lax.broadcasted_iota(jnp.int32, marks.shape, 0)
+    marks = jnp.where(row < 9, marks, jnp.where(row < 12, 1.0, 0.0))
+    return marks.T.astype(jnp.bfloat16)
+
+
+def own_side(marks):
+    row = lax.broadcasted_iota(jnp.int32, marks.shape, 0)
+    sides = []
+    for comp in range(3):
+        moved = pltpu.roll(marks, 9 - 3 * comp, 0)
+        moved = moved if comp == 2 else -moved
+        fixed = jnp.where(row // 3 == comp, 1.0, 0.0)
+        sides.append(jnp.where((row >= 9) & (row < 12), moved, fixed))
+    return jnp.concatenate(sides, axis=1).astype(jnp.bfloat16)
+
+
+def pair_sums(other, own):
+    pairs = jnp.dot(other, own, preferred_element_type=jnp.float32)
+    lanes = pairs.shape[1] // 3
+    acc_x = acc_y = jnp.zeros((8, lanes), jnp.float32)
+    for c in range(pairs.shape[0] // 8):
+        rows = pairs[8 * c : 8 * c + 8]
+        sep_x, sep_y, reach = rows[:, :lanes], rows[:, lanes : 2 * lanes], rows[:, 2 * lanes :]
+        inverse = lax.rsqrt(sep_x * sep_x + sep_y * sep_y + SOFTEN)
+        push = jnp.maximum(reach * inverse - 1.0, 0.0)
+        acc_x = acc_x + push * sep_x
+        acc_y = acc_y + push * sep_y
+    return acc_x, acc_y
+
+
+def marks_of(marks, b):
+    return marks[pl.ds(pl.multiple_of(b * MARKS, MARKS), MARKS), :]
 
 
 def turn(rows, perms, turned):
@@ -83,41 +135,21 @@
     lax.fori_loop(0, perms.shape[0], one, 0)
 
 
-def own_setup(pos, rad, columns):
-    for comp in range(2):
-        columns[comp] = pos[comp].T
-    columns[2] = rad[...].T
-
-
-def gather_own(pos, rad, b):
-    own = (pos[0, pl.ds(b, 1), :], pos[1, pl.ds(b, 1), :], rad[pl.ds(b, 1), :])
-    return own, jnp.full((8, rad.shape[1]), b, jnp.int32)
-
-
-def visit(source, at, target, acc):
-    own, index = target
-    return pair_terms(*acc, *own, *[lane_take(source[k, at, :], index) for k in range(3)])
-
-
-def own_forces(first, count, pos, rad, columns, force):
-    blocks, discs = rad.shape
-    zero = jnp.zeros((8, discs), jnp.float32)
-
+def own_forces(first, count, marks, force):
     def some(t, carry):
-        for u in range(TOGETHER):
-            b = first + t * TOGETHER + u
-            target = gather_own(pos, rad, b)
-            acc = (zero, zero)
-            for c in range(discs // 8):
-                acc = visit(columns, pl.ds(c * 8, 8), target, acc)
+        for u in range(OWN_STEP):
+            b = first + t * OWN_STEP + u
+            own = marks_of(marks, b)
+            acc = pair_sums(other_side(own), own_side(own))
+            at = pl.ds(pl.multiple_of(b * 8, 8), 8)
             for k in range(2):
-                force[k, pl.ds(b, 1), :] = jnp.sum(acc[k], axis=0, keepdims=True)
+                force[k, at, :] = acc[k]
         return carry
 
-    lax.fori_loop(0, count // TOGETHER, some, 0)
-
-
-def contact_kernel(which, n_gy, pos, vel, rad, bonds, mask, held, halo, halo_rad, *refs):
+    lax.fori_loop(0, count // OWN_STEP, some, 0)
+
+
+def contact_kernel(which, n_gy, pos, vel, rad, bonds, mask, marks, held, halo, halo_rad, *refs):
     last = which == SUB - 1
     if last:
         slots, pos_out, vel_out, sent, *scratch = refs
@@ -130,7 +162,7 @@
 
     else:
         pos_out, vel_out, edges, *scratch = refs
-    wide, found, found_t, force, tally, counts, work, sem = scratch
+    wide, found, seen, force, tally, work, sem = scratch
     rows_dev, cols_dev = wide.shape[1] - 2, pos.shape[1] // (wide.shape[1] - 2)
     blocks, discs = rad.shape
     for comp in range(3):
@@ -154,121 +186,118 @@
     tri_row = lax.broadcasted_iota(jnp.int32, (discs, 2 * discs), 0)
     tri_col = lax.broadcasted_iota(jnp.int32, (discs, 2 * discs), 1)
     triangle = (tri_row <= tri_col).astype(jnp.bfloat16)
+    low_row = lax.broadcasted_iota(jnp.int32, (blocks, blocks), 0)
+    low_col = lax.broadcasted_iota(jnp.int32, (blocks, blocks), 1)
+    lower = (low_col <= low_row).astype(jnp.bfloat16)
 
     def collect(start):
         def one_row(step_y, carry):
+            units, totals = [], []
             for half in range(ROWS * cols_dev // 8):
                 y = step_y * ROWS + half // (cols_dev // 8)
                 x0 = half % (cols_dev // 8) * 8
-                at = pl.multiple_of(y * cols_dev + x0, 8)
-                own = [pos[0, pl.ds(at, 8), :], pos[1, pl.ds(at, 8), :], rad[pl.ds(at, 8), :]]
+                at = pl.ds(pl.multiple_of(y * cols_dev + x0, 8), 8)
+                own = [pos[0, at, :], pos[1, at, :], rad[at, :]]
                 reach = jnp.max(own[2], axis=1, keepdims=True)
                 low = [jnp.min(own[c], axis=1, keepdims=True) - reach for c in range(2)]
                 high = [jnp.max(own[c], axis=1, keepdims=True) + reach for c in range(2)]
-                weights = mask[pl.ds(at, 8), :]
-                near = []
+                weights = mask[at, :]
+                flags = []
+                places = []
                 for k, (sy, sx) in enumerate(NEIGHBOURS):
-                    where = (y + 1 + sy, pl.ds(x0 + 1 + sx, 8), slice(None))
-                    nx = wide[(0,) + where] + float(sx)
-                    ny = wide[(1,) + where] + float(sy)
-                    nr = wide[(2,) + where]
-                    close = (nx - nr < high[0]) & (nx + nr > low[0])
-                    close = close & (ny - nr < high[1]) & (ny + nr > low[1])
+                    place = (y + 1 + sy, pl.ds(x0 + 1 + sx, 8), slice(None))
+                    nx, ny, nr = (wide[(c,) + place] for c in range(3))
+                    close = (nx - nr < high[0] - float(sx)) & (nx + nr > low[0] - float(sx))
+                    close = close & (ny - nr < high[1] - float(sy)) & (ny + nr > low[1] - float(sy))
                     close = close & (weights[:, k : k + 1] > 0.5)
-                    near.append((nx, ny, nr, close))
-                flags = jnp.concatenate([n[3].astype(jnp.float32) for n in near], axis=0)
+                    flags.append(close.astype(jnp.float32))
+                    places.append(place)
                 ranks = jnp.dot(
-                    flags.astype(jnp.bfloat16), triangle, preferred_element_type=jnp.float32
+                    jnp.concatenate(flags, axis=0).astype(jnp.bfloat16),
+                    triangle,
+                    preferred_element_type=jnp.float32,
                 )
                 base = jnp.zeros((8, discs), jnp.float32) - start
-                gx = jnp.zeros((8, discs), jnp.float32)
-                gy = jnp.zeros((8, discs), jnp.float32)
-                gr = jnp.full((8, discs), -1.0, jnp.float32)
                 for k in range(8):
-                    nx, ny, nr, _ = near[k]
                     rank = ranks[8 * k : 8 * k + 8, :discs]
                     total = ranks[8 * k : 8 * k + 8, discs:]
                     want = lane_f - base
                     source = jnp.zeros((8, discs), jnp.int32)
-                    step = discs // 2
-                    while step >= 1:
-                        probe = lane_take(rank, source + (step - 1))
-                        source = jnp.where(probe <= want, source + step, source)
-                        step //= 2
-                    valid = (want >= 0.0) & (want < total)
-                    gx = jnp.where(valid, lane_take(nx, source), gx)
-                    gy = jnp.where(valid, lane_take(ny, source), gy)
-                    gr = jnp.where(valid, lane_take(nr, source), gr)
+                    units.append((half, k, source, places[k], rank, total, want))
                     base = base + total
-                found[0, pl.ds(at, 8), :] = gx
-                found[1, pl.ds(at, 8), :] = gy
-                found[2, pl.ds(at, 8), :] = gr
-                found[3, pl.ds(at, 8), :] = base
+                totals.append((at, base))
+            sources = [u[2] for u in units]
+            step = discs // 2
+            while step >= 1:
+                probes = [lane_take(u[4], i + (step - 1)) for u, i in zip(units, sources)]
+                sources = [
+                    jnp.where(probe <= u[6], i + step, i)
+                    for probe, u, i in zip(probes, units, sources)
+                ]
+                step //= 2
+            for half, (at, base) in enumerate(totals):
+                mine = [(u, i) for u, i in zip(units, sources) if u[0] == half]
+                for comp in range(3):
+                    got = jnp.full((8, discs), -1.0 if comp == 2 else 0.0, jnp.float32)
+                    for (_, k, _, place, _, total, want), source in mine:
+                        valid = (want >= 0.0) & (want < total)
+                        value = wide[(comp,) + place]
+                        if comp < 2 and NEIGHBOURS[k][1 - comp] != 0:
+                            value = value + float(NEIGHBOURS[k][1 - comp])
+                        got = jnp.where(valid, lane_take(value, source), got)
+                    found[comp, at, :] = got
+                found[3, at, :] = base
             return carry
 
         lax.fori_loop(0, rows_dev // ROWS, one_row, 0)
-        for comp in range(3):
-            found_t[comp] = found[comp].T
-        left = found[3].T[0:8]
-        groups = jnp.clip(jnp.ceil(left * (1.0 / 32.0)), 0.0, 4.0).astype(jnp.int32)
-        passes = jnp.ceil(jnp.max(left, axis=1, keepdims=True) * (1.0 / discs)).astype(jnp.int32)
-        tally[0:8] = groups
-        tally[8:16] = jnp.broadcast_to(passes, (8, discs))
-        copy = pltpu.make_async_copy(tally, counts, sem)
+        write_marks([found[k] for k in range(3)], seen)
+        left = found[3]
+        size = jnp.where(left > float(HALF), 1.0, 0.0)
+        ends = jnp.dot(lower, size.astype(jnp.bfloat16), preferred_element_type=jnp.float32)
+        spot = lax.broadcasted_iota(jnp.int32, (1, discs), 1).astype(jnp.float32)
+        block = jnp.sum(jnp.where(ends <= spot, 1.0, 0.0), axis=0, keepdims=True)
+        tally[0:1] = block.astype(jnp.int32)
+        tally[1:2] = ends[blocks - 1 :].astype(jnp.int32)
+        deepest = jnp.max(left, axis=0, keepdims=True)
+        tally[2:3] = jnp.ceil(deepest * (1.0 / discs)).astype(jnp.int32)
+        copy = pltpu.make_async_copy(tally, work, sem)
         copy.start()
         copy.wait()
 
-    zero = jnp.zeros((8, discs), jnp.float32)
-    span = 8 * GROUP
-
-    def group(b, g, scale, target, acc):
-        for c in range(GROUP):
-            at = pl.ds(pl.multiple_of(g * span + c * 8, 8), 8)
-            acc = visit(found_t, at, target, acc)
-        return acc
-
-    def sweep(static):
-        def some(t, size):
-            for u in range(TOGETHER):
-                b = t * TOGETHER + u
-                target = gather_own(pos, rad, b)
-                acc = (zero, zero)
-                for g in range(static):
-                    acc = group(b, g, None, target, acc)
-                if static:
-                    for k in range(2):
-                        force[k, pl.ds(b, 1), :] = jnp.sum(acc[k], axis=0, keepdims=True)
-                for g in range(static, discs // span):
-                    work[size] = b * 8 + g
-                    size = size + (counts[0, b] > g).astype(jnp.int32)
-            return size
-
-        size = lax.fori_loop(0, blocks // TOGETHER, some, 0)
-
-        def rest(i, carry):
-            for u in range(ITEMS):
-                slot = i * ITEMS + u
-                item = jnp.where(slot < size, work[slot], 0)
-                scale = jnp.where(slot < size, 1.0, 0.0)
-                b, g = item // 8, item % 8
-                target = gather_own(pos, rad, b)
-                acc = group(b, g, scale, target, (zero, zero))
-                for k in range(2):
-                    total = jnp.sum(acc[k], axis=0, keepdims=True)
-                    force[k, pl.ds(b, 1), :] += total * scale
+    def meet(b, part, fresh):
+        at = pl.ds(pl.multiple_of(b * 8, 8), 8)
+        b = jnp.minimum(b, blocks - 1)
+        other = other_side(marks_of(seen, b))[part * HALF : (part + 1) * HALF]
+        acc = pair_sums(other, own_side(marks_of(marks, b)))
+        for k in range(2):
+            if fresh:
+                force[k, at, :] = acc[k]
+            else:
+                force[k, at, :] += acc[k]
+
+    def sweep(fresh):
+        def some(t, carry):
+            for u in range(NEAR_STEP):
+                meet(t * NEAR_STEP + u, 0, fresh)
             return carry
 
-        lax.fori_loop(0, (size + ITEMS - 1) // ITEMS, rest, 0)
+        def rest(t, carry):
+            for u in range(REST_STEP):
+                meet(work[0, t * REST_STEP + u], 1, False)
+            return carry
+
+        lax.fori_loop(0, blocks // NEAR_STEP, some, 0)
+        lax.fori_loop(0, (work[1, 0] + (REST_STEP - 1)) // REST_STEP, rest, 0)
 
     collect(0.0)
-    sweep(STATIC)
+    sweep(True)
 
     def more(p, carry):
         collect(p.astype(jnp.float32) * discs)
-        sweep(0)
+        sweep(False)
         return carry
 
-    lax.fori_loop(1, counts[8, 0], more, 0)
+    lax.fori_loop(1, work[2, 0], more, 0)
 
     def update(g, carry):
         at = pl.ds(pl.multiple_of(g * 8, 8), 8)
@@ -279,7 +308,11 @@
             bonded = lane_take(here, bonds[0, at, :])
             for p in range(1, BONDS):
                 bonded = bonded + lane_take(here, bonds[p, at, :])
-            total = BOND_STIFF * (bonded - BONDS * here) - STIFFNESS * (held[k, at, :] + force[k, at, :])
+            push = jnp.zeros((8, discs), jnp.float32)
+            for r in range(8):
+                rows = pl.ds(g * 64 + r, 8, stride=8)
+                push = push + (held[k, rows, :] + force[k, rows, :])
+            total = BOND_STIFF * (bonded - BONDS * here) - STIFFNESS * push
             speed = vel[k, at, :] + total * scale
             vel_out[k, at, :] = speed
             pos_out[k, at, :] = here + TIME_STEP * speed
@@ -305,7 +338,7 @@
                 edges[side, comp] = pos_out[comp, at, :]
 
 
-def contact_step(which, n_gy, pos, vel, rad, bonds, mask, held, halo, halo_rad, *extra):
+def contact_step(which, n_gy, pos, vel, rad, bonds, mask, marks, held, halo, halo_rad, *extra):
     blocks, discs = rad.shape
     rows_dev = blocks // 16
     square = shape(2, blocks, discs)
@@ -313,7 +346,7 @@
     outs = (square, square, tail)
     if which == 1:
         outs += (shape(*extra[0].shape),)
-    args = (pos, vel, rad, bonds, mask, held, halo, halo_rad) + extra
+    args = (pos, vel, rad, bonds, mask, marks, held, halo, halo_rad) + extra
     return pl.pallas_call(
         functools.partial(contact_kernel, which, n_gy),
         out_shape=outs,
@@ -322,11 +355,10 @@
         scratch_shapes=[
             pltpu.VMEM((3, rows_dev + 2, 24, discs), jnp.float32),
             pltpu.VMEM((4, blocks, discs), jnp.float32),
-            pltpu.VMEM((3, discs, blocks), jnp.float32),
-            pltpu.VMEM((2, blocks, discs), jnp.float32),
-            pltpu.VMEM((16, blocks), jnp.int32),
-            pltpu.SMEM((16, blocks), jnp.int32),
-            pltpu.SMEM((blocks * 4 + 2 * ITEMS,), jnp.int32),
+            pltpu.VMEM((MARKS * blocks, discs), jnp.float32),
+            pltpu.VMEM((2, 8 * blocks + 8, discs), jnp.float32),
+            pltpu.VMEM((8, discs), jnp.int32),
+            pltpu.SMEM((8, discs), jnp.int32),
             pltpu.SemaphoreType.DMA,
         ],
         compiler_params=grant(16),
@@ -412,14 +444,15 @@
 
 def exchange_kernel(which, n_gx, n_gy, *refs):
     if which == 0:
-        pos, rad, edges, halo, held, halo_rad, columns, send_sem, recv_sem, rad_send, rad_recv = refs
+        pos, rad, edges, halo, held, marks, halo_rad, *scratch = refs
+        send_sem, recv_sem, rad_send, rad_recv = scratch
     elif which == 1:
-        pos, rad, edges, top, bottom, sides, perm, halo, held, lon, lat, rows, perms, *scratch = refs
-        columns, send_sem, recv_sem, sea_send, sea_recv, far_send, far_recv, *scratch = scratch
-        perm_send, perm_recv, own = scratch
+        pos, rad, edges, top, bottom, sides, perm, halo, held, marks, lon, lat, rows, perms, *scratch = refs
+        send_sem, recv_sem, sea_send, sea_recv, *scratch = scratch
+        far_send, far_recv, perm_send, perm_recv, own = scratch
     else:
-        pos, rad, edges, turned, halo, held, mirror, columns, send_sem, recv_sem, *scratch = refs
-        far_send, far_recv, own = scratch
+        pos, rad, edges, turned, halo, held, marks, mirror, *scratch = refs
+        send_sem, recv_sem, far_send, far_recv, own = scratch
     gx, gy = lax.axis_index("gx"), lax.axis_index("gy")
     is_top = gy == n_gy - 1
 
@@ -437,8 +470,8 @@
                 pl.semaphore_signal(barrier, inc=1, device_id=at(d, 0), device_id_type=MESH)
 
     blocks = rad.shape[0]
-    own_setup(pos, rad, columns)
-    own_forces(0, EARLY, pos, rad, columns, held)
+    write_marks([pos[0], pos[1], rad[...]], marks)
+    own_forces(0, EARLY, marks, held)
     if which > 0:
 
         @pl.when(is_top)
@@ -540,7 +573,7 @@
             for copy in far:
                 copy.start()
 
-    own_forces(EARLY, blocks - EARLY, pos, rad, columns, held)
+    own_forces(EARLY, blocks - EARLY, marks, held)
     for copy in copies:
         copy.wait()
     if which == 1:
@@ -580,9 +613,11 @@
 
 def exchange(which, n_gx, n_gy, pos, rad, edges, *args):
     lanes = rad.shape[1]
-    outs = [shape(8, 2, 16, lanes), shape(*pos.shape)]
+    blocks = rad.shape[0]
+    outs = [shape(8, 2, 16, lanes), shape(2, 8 * blocks, lanes)]
+    outs += [shape(MARKS * blocks, lanes)]
     dma = pltpu.SemaphoreType.DMA
-    scratch = [pltpu.VMEM((3, lanes, rad.shape[0]), jnp.float32), dma((8,)), dma((8,))]
+    scratch = [dma((8,)), dma((8,))]
     far = [dma((n_gx - 1,)), dma((n_gx - 1,))]
     if which == 0:
         outs += [shape(8, 16, lanes)]
@@ -833,20 +868,20 @@
     sea_shape = (4, mix_coef.shape[0], discs)
     flat = (4 * mix_coef.shape[0], discs)
     position, rad, edges, mask = prep(n_gy, position, rad, contact_mask)
-    halo, held, halo_rad = exchange(0, n_gx, n_gy, position, rad, edges)
+    halo, held, marks, halo_rad = exchange(0, n_gx, n_gy, position, rad, edges)
     position, velocity, edges = contact_step(
-        0, n_gy, position, velocity, rad, bonds, mask, held, halo, halo_rad
+        0, n_gy, position, velocity, rad, bonds, mask, marks, held, halo, halo_rad
     )
     sides, bottom, top = pack(ocean_state, edges)
-    halo, held, lon, lat, rows, perms = exchange(
+    halo, held, marks, lon, lat, rows, perms = exchange(
         1, n_gx, n_gy, position, rad, edges, top.reshape(flat), bottom.reshape(flat), sides, perm
     )
     position, velocity, edges, turned = contact_step(
-        1, n_gy, position, velocity, rad, bonds, mask, held, halo, halo_rad, rows, perms
+        1, n_gy, position, velocity, rad, bonds, mask, marks, held, halo, halo_rad, rows, perms
     )
-    halo, held, mirror = exchange(2, n_gx, n_gy, position, rad, edges, turned)
+    halo, held, marks, mirror = exchange(2, n_gx, n_gy, position, rad, edges, turned)
     position, velocity, sent = contact_step(
-        2, n_gy, position, velocity, rad, bonds, mask, held, halo, halo_rad, slots
+        2, n_gy, position, velocity, rad, bonds, mask, marks, held, halo, halo_rad, slots
     )
     ocean, skin = ocean_step(
         n_gy, ocean_state, mix_coef, lon, lat.reshape(2, *sea_shape), mirror.reshape(sea_shape)

time: 146 us -> 152 us (1.041)
  Pallas kernels: 138 us -> 147 us
  local copies, waits for them, and re-layouts: 6.3 us -> 4.52 us
    pallas_call x3, Pallas kernels: 36.4 us -> 56.7 us  [exchange(): pl.pallas_call(functools.partial(exchange_kernel, which, n_gx, n_gy), out...]
    pallas_call x3, Pallas kernels: 61.7 us -> 46 us  [contact_step(): pl.pallas_call(functools.partial(contact_kernel, which, n_gy), out_shape=...]
    pallas_call x1, Pallas kernels: 31.5 us -> 35 us  [couple(): pl.pallas_call(functools.partial(couple_kernel, n_gx, n_gy), out_shape=(s...]
    unnamed x24 -> x22, local copies, waits for them, and re-layouts: 6.3 us -> 4.52 us
where the time goes in v2:
time: 152 us
  Pallas kernels  147 us (97%)
  local copies, waits for them, and re-layouts  4.52 us (3%)
    pallas_call x3, Pallas kernels, exchange(): pl.pallas_call(functools.partial(exchange_kernel, which, n_gx, n_gy), out...  56.7 us
    pallas_call x3, Pallas kernels, contact_step(): pl.pallas_call(functools.partial(contact_kernel, which, n_gy), out_shape=...  46 us
    pallas_call x1, Pallas kernels, couple(): pl.pallas_call(functools.partial(couple_kernel, n_gx, n_gy), out_shape=(s...  35 us
    pallas_call x1, Pallas kernels, ocean_step(): pl.pallas_call(functools.partial(ocean_kernel, n_gy), grid=(steps,), out_...  5.58 us
    unnamed x22, local copies, waits for them, and re-layouts  4.52 us

profile of v2, /device:TPU:1, one launch (start us, length us, event | category | flops | bytes accessed | tf_op | source)
XLA Modules:
  0.0 152.2 jit_solution(7229743689474867739)
XLA Ops:
  0.6 0.0 copy-start
  0.6 0.0 copy-start.5
  0.7 1.0 copy-done.5
  1.7 0.8 copy-done.6
  2.5 0.8 copy-done.7
  3.3 0.5 prep.1
  3.8 13.4 %exchange_first.1 = (f32[8,2,16,128]{3,2,1,0:T(8,128)S(1)}, f32[2,1024,128]{2,1,0:T(8,128)S(1)}, f32[2048,128]{1,0:T(8,128)S(1)}, f32[8,16,128]{2,1,0:T(8,128)S(1)}) custom-call(f32[2,128,128]{2,1,0:T(8,128)S(1)} %get-tuple-element.41.refs_0_.pos, f32[128,128]{1,0:T(8,128)S(1)} %get-tuple-element.42.refs_1_.rad, f32[2,3,8,128]{3,2,1,0:T(8,128)S(1)} %get-tuple-element.44.refs_2_), custom_call_target="tpu_custom_call" | custom-call | tf_op jit(solution)/shard_map/exchange_first/pallas_call | solution.py:633
  17.2 0.0 copy-start.1
  17.2 0.9 copy-done.1
  18.2 0.9 copy-done.4
  19.1 15.2 %contact_first.1 = (f32[2,128,128]{2,1,0:T(8,128)S(1)}, f32[2,128,128]{2,1,0:T(8,128)S(1)}, f32[2,2,8,128]{3,2,1,0:T(8,128)S(1)}) custom-call(f32[2,128,128]{2,1,0:T(8,128)S(1)} %get-tuple-element.41.refs_0_.pos, f32[2,128,128]{2,1,0:T(8,128)S(1)} %bitcast.23, f32[128,128]{1,0:T(8,128)S(1)} %get-tuple-element.42.refs_1_.rad, s32[4,128,128]{2,1,0:T(8,128)S(1)} %bitcast.19, ...), custom_call_target="tpu_custom_call" | custom-call | tf_op jit(solution)/shard_map/contact_first/pallas_call | solution.py:350
  34.3 0.0 copy-done
  34.3 0.0 copy-start.8
  34.3 1.6 %pack.1 = (f32[6,16,128]{2,1,0:T(8,128)S(1)}, f32[4,48,128]{2,1,0:T(8,128)S(1)}, f32[4,48,128]{2,1,0:T(8,128)S(1)}) custom-call(f32[4,48,32,128]{3,2,1,0:T(8,128)S(1)} %copy-done, f32[2,2,8,128]{3,2,1,0:T(8,128)S(1)} %get-tuple-element.51.after.refs_2_), custom_call_target="tpu_custom_call" | custom-call | tf_op jit(solution)/shard_map/pack/pallas_call | solution.py:430
  35.9 18.6 %exchange_second.1 = (f32[8,2,16,128]{3,2,1,0:T(8,128)S(1)}, f32[2,1024,128]{2,1,0:T(8,128)S(1)}, f32[2048,128]{1,0:T(8,128)S(1)}, f32[2,6,16,128]{3,2,1,0:T(8,1...) custom-call(f32[2,128,128]{2,1,0:T(8,128)S(1)} %get-tuple-element.49.refs_0_.pos, ...), custom_call_target="tpu_custom_call" | custom-call | tf_op jit(solution)/shard_map/exchange_second/pallas_call | solution.py:633
  54.5 0.0 copy-done.2
  54.5 0.0 copy-start.3
  54.5 15.2 %contact.1 = (f32[2,128,128]{2,1,0:T(8,128)S(1)}, f32[2,128,128]{2,1,0:T(8,128)S(1)}, f32[2,2,8,128]{3,2,1,0:T(8,128)S(1)}, f32[16,16,128]{2,1,0:T(8,128)S(1)}) custom-call(f32[2,128,128]{2,1,0:T(8,128)S(1)} %get-tuple-element.49.refs_0_.pos, f32[2,128,128]{2,1,0:T(8,128)S(1)} %get-tuple-element.50.vel, f32[128,128]{1,0:T(8,128)S(1)} %get-tuple-element.42.refs_1_.rad, ...), custom_call_target="tpu_custom_call" | custom-call | tf_op jit(solution)/shard_map/contact/pallas_call | solution.py:350
  69.7 24.7 %exchange_third.1 = (f32[8,2,16,128]{3,2,1,0:T(8,128)S(1)}, f32[2,1024,128]{2,1,0:T(8,128)S(1)}, f32[2048,128]{1,0:T(8,128)S(1)}, f32[12,16,128]{2,1,0:T(8,128)S(1)}) custom-call(f32[2,128,128]{2,1,0:T(8,128)S(1)} %get-tuple-element.60.refs_0_.pos, f32[128,128]{1,0:T(8,128)S(1)} %get-tuple-element.42.refs_1_.rad, ...), custom_call_target="tpu_custom_call" | custom-call | tf_op jit(solution)/shard_map/exchange_third/pallas_call | solution.py:633
  94.5 15.7 %contact_last.1 = (f32[2,128,128]{2,1,0:T(8,128)}, f32[2,128,128]{2,1,0:T(8,128)S(1)}, f32[128,1,128]{2,1,0:T(1,128)S(1)}) custom-call(f32[2,128,128]{2,1,0:T(8,128)S(1)} %get-tuple-element.60.refs_0_.pos, f32[2,128,128]{2,1,0:T(8,128)S(1)} %get-tuple-element.61.vel, f32[128,128]{1,0:T(8,128)S(1)} %get-tuple-element.42.refs_1_.rad, ...), custom_call_target="tpu_custom_call" | custom-call | tf_op jit(solution)/shard_map/contact_last/pallas_call | solution.py:350
  110.2 0.0 copy-start.9
  110.2 5.6 %ocean.4 = (f32[4,48,32,128]{3,2,1,0:T(8,128)}, f32[2,32,128]{2,1,0:T(8,128)S(1)}) custom-call(f32[4,48,32,128]{3,2,1,0:T(8,128)S(1)} %copy-done, f32[4,48,32,128]{3,2,1,0:T(8,128)S(1)} %copy-done, f32[4,48,32,128]{3,2,1,0:T(8,128)S(1)} %copy-done, f32[48,32,128]{2,1,0:T(8,128)S(1)} %copy-done.3, f32[2,6,16,128]{3,2,1,0:T(8,128)S(1)} %get-tuple-element.68.lon, ...), custom_call_target="tpu_custom_call" | custom-call | tf_op jit(solution)/shard_map/ocean/pallas_call | solution.py:695
  115.8 35.0 %couple.1 = (f32[2,32,128]{2,1,0:T(8,128)S(1)}, f32[16,8,1,128]{3,2,1,0:T(1,128)S(1)}) custom-call(f32[16,8,1,128]{3,2,1,0:T(1,128)S(1)} %bitcast.30, f32[2,32,128]{2,1,0:T(8,128)S(1)} %get-tuple-element.73.skin, s32[2,128]{1,0:T(2,128)S(1)} %bitcast.33), custom_call_target="tpu_custom_call" | custom-call | tf_op jit(solution)/shard_map/couple/pallas_call | solution.py:805
  150.8 1.3 finish.1
  (9 shorter events, 0.0 us)
Async XLA Ops:
  0.6 33.6 %copy-start = (f32[4,48,32,128]{3,2,1,0:T(8,128)S(1)}, f32[4,48,32,128]{3,2,1,0:T(8,128)}, u32[]{:S(2)}) copy-start(f32[4,48,32,128]{3,2,1,0:T(8,128)} %below.1) | copy-start | bytes 9437188
  0.6 1.1 copy-start.5
  1.7 0.8 copy-start.6
  2.5 0.8 copy-start.7
  17.2 1.0 copy-start.1
  18.2 0.9 copy-start.4
  19.1 16.8 %copy-start.10 = (s32[128]{0:T(128)S(1)}, s32[128]{0:T(128)}, u32[]{:S(2)}) copy-start(s32[128]{0:T(128)} %param.19) | copy-start | bytes 1540
  19.1 35.4 %copy-start.2 = (s32[4,8,16,128]{3,2,1,0:T(8,128)S(1)}, s32[4,8,16,128]{3,2,1,0:T(8,128)}, u32[]{:S(2)}) copy-start(s32[4,8,16,128]{3,2,1,0:T(8,128)} %param.13) | copy-start | bytes 786436
  34.3 60.2 %copy-start.8 = (s32[1,128,2]{1,2,0:T(2,128)S(1)}, s32[1,128,2]{1,2,0:T(2,128)}, u32[]{:S(2)}) copy-start(s32[1,128,2]{1,2,0:T(2,128)} %param.15) | copy-start | bytes 3076
  54.5 55.7 %copy-start.3 = (f32[48,32,128]{2,1,0:T(8,128)S(1)}, f32[48,32,128]{2,1,0:T(8,128)}, u32[]{:S(2)}) copy-start(f32[48,32,128]{2,1,0:T(8,128)} %mix.1) | copy-start | bytes 2359300
  110.2 5.6 %copy-start.9 = (s32[1,128,2]{1,2,0:T(2,128)S(1)}, s32[1,128,2]{1,2,0:T(2,128)}, u32[]{:S(2)}) copy-start(s32[1,128,2]{1,2,0:T(2,128)} %param.18) | copy-start | bytes 3076

commit v3 on v2

--- a/solution.py
+++ b/solution.py
@@ -29,6 +29,7 @@
 EARLY = 32
 TURN_ROWS = 16
 MESH = pl.DeviceIdType.MESH
+BUSY = pl.CostEstimate(flops=1 << 32, bytes_accessed=1 << 24, transcendentals=1 << 22)
 VMEM = pl.BlockSpec(memory_space=pltpu.VMEM)
 ANY = pl.BlockSpec(memory_space=pl.ANY)
 HBM = pl.BlockSpec(memory_space=pltpu.HBM)
@@ -149,6 +150,21 @@
     lax.fori_loop(0, count // OWN_STEP, some, 0)
 
 
+def write_mask(n_gy, allowed, mask):
+    lane = lax.broadcasted_iota(jnp.int32, (8, 128), 1)
+    _, rows_dev, cols_dev = allowed.shape
+    spread = jnp.zeros((8, 128), jnp.float32)
+    for y in range(rows_dev):
+        part = allowed[:, y, :].astype(jnp.float32)
+        part = jnp.concatenate([part, jnp.zeros((8, 128 - cols_dev), jnp.float32)], axis=1)
+        spread = spread + (pltpu.roll(part, y * cols_dev, 1) if y else part)
+    which = lax.broadcasted_iota(jnp.int32, (8, 128), 0)
+    shift_y = jnp.where(which < 3, -1, jnp.where(which < 5, 0, 1))
+    row = lax.axis_index("gy") * rows_dev + lane // cols_dev + shift_y
+    spread = jnp.where((row >= 0) & (row < n_gy * rows_dev), spread, 0.0)
+    mask[...] = jnp.concatenate([spread, jnp.zeros((120, 128), jnp.float32)], axis=0).T
+
+
 def contact_kernel(which, n_gy, pos, vel, rad, bonds, mask, marks, held, halo, halo_rad, *refs):
     last = which == SUB - 1
     if last:
@@ -161,7 +177,9 @@
             turn(rows, perms, turned)
 
     else:
-        pos_out, vel_out, edges, *scratch = refs
+        allowed, mask = mask, refs[3]
+        pos_out, vel_out, edges, _, *scratch = refs
+        write_mask(n_gy, allowed, mask)
     wide, found, seen, force, tally, work, sem = scratch
     rows_dev, cols_dev = wide.shape[1] - 2, pos.shape[1] // (wide.shape[1] - 2)
     blocks, discs = rad.shape
@@ -344,6 +362,8 @@
     square = shape(2, blocks, discs)
     tail = shape(blocks, 1, discs) if which == SUB - 1 else shape(2, 2, rows_dev, discs)
     outs = (square, square, tail)
+    if which == 0:
+        outs += (shape(*rad.shape),)
     if which == 1:
         outs += (shape(*extra[0].shape),)
     args = (pos, vel, rad, bonds, mask, marks, held, halo, halo_rad) + extra
@@ -362,49 +382,36 @@
             pltpu.SemaphoreType.DMA,
         ],
         compiler_params=grant(16),
+        cost_estimate=BUSY,
         name=("contact_first", "contact", "contact_last")[which],
     )(*args)
 
 
-def prep_kernel(n_gy, pos_in, rad_in, allowed_in, pos, rad, edges, mask, allowed, sems):
+def prep_kernel(pos_in, rad_in, pos, rad, edges, sems):
     copies = [
-        pltpu.make_async_copy(allowed_in, allowed, sems.at[0]),
-        pltpu.make_async_copy(pos_in, pos, sems.at[1]),
-        pltpu.make_async_copy(rad_in, rad, sems.at[2]),
+        pltpu.make_async_copy(pos_in, pos, sems.at[0]),
+        pltpu.make_async_copy(rad_in, rad, sems.at[1]),
     ]
     for copy in copies:
         copy.start()
-    copies[0].wait()
-    lane = lax.broadcasted_iota(jnp.int32, (8, 128), 1)
-    _, rows_dev, cols_dev = allowed.shape
-    spread = jnp.zeros((8, 128), jnp.float32)
-    for y in range(rows_dev):
-        part = allowed[:, y, :].astype(jnp.float32)
-        part = jnp.concatenate([part, jnp.zeros((8, 128 - cols_dev), jnp.float32)], axis=1)
-        spread = spread + (pltpu.roll(part, y * cols_dev, 1) if y else part)
-    which = lax.broadcasted_iota(jnp.int32, (8, 128), 0)
-    shift_y = jnp.where(which < 3, -1, jnp.where(which < 5, 0, 1))
-    row = lax.axis_index("gy") * rows_dev + lane // cols_dev + shift_y
-    spread = jnp.where((row >= 0) & (row < n_gy * rows_dev), spread, 0.0)
-    mask[...] = jnp.concatenate([spread, jnp.zeros((120, 128), jnp.float32)], axis=0).T
-    copies[1].wait()
-    copies[2].wait()
+    for copy in copies:
+        copy.wait()
     for comp in range(3):
         source = pos.at[comp] if comp < 2 else rad
         for side in range(2):
             edges[side, comp] = source[pl.ds(side * 15, 8, stride=16), :]
 
 
-def prep(n_gy, pos, rad, allowed):
+def prep(pos, rad):
     return pl.pallas_call(
-        functools.partial(prep_kernel, n_gy),
-        out_shape=(shape(*pos.shape), shape(*rad.shape), shape(2, 3, 8, 128), shape(*rad.shape)),
-        in_specs=[HBM] * 3,
-        out_specs=(VMEM,) * 4,
-        scratch_shapes=[pltpu.VMEM(allowed.shape, jnp.int32), pltpu.SemaphoreType.DMA((3,))],
+        prep_kernel,
+        out_shape=(shape(*pos.shape), shape(*rad.shape), shape(2, 3, 8, 128)),
+        in_specs=[HBM] * 2,
+        out_specs=(VMEM,) * 3,
+        scratch_shapes=[pltpu.SemaphoreType.DMA((2,))],
         compiler_params=grant(4),
         name="prep",
-    )(pos, rad, allowed)
+    )(pos, rad)
 
 
 def pack_kernel(ocean, after, columns, bottom, top):
@@ -637,33 +644,37 @@
         out_specs=(VMEM,) * len(outs),
         scratch_shapes=scratch,
         compiler_params=grant(8, collective_id=which, has_side_effects=True),
+        cost_estimate=BUSY,
         name=("exchange_first", "exchange_second", "exchange_third")[which],
     )(pos, rad, edges, *args)
 
 
-def ocean_kernel(n_gy, ocean, above, below, mix, lon, lat, mirror, out, skin):
-    step = pl.program_id(0)
-    rows, lanes = ocean.shape[2], ocean.shape[3]
+def stencil(step, n_gy, ocean, mix, lon, lat, mirror, out):
+    layers, rows, lanes = ocean.shape[1:]
     gy = lax.axis_index("gy")
+    first = step * CHUNK
     lane = lax.broadcasted_iota(jnp.int32, (rows, lanes), 1)
     sub = lax.broadcasted_iota(jnp.int32, (rows, lanes), 0)
     lane8 = lax.broadcasted_iota(jnp.int32, (8, lanes), 1)
     bands = []
     for half in range(2):
         at = pl.ds(8 * half, 8)
-        west, east = pltpu.roll(lon[0, 0, at, :], 1, 1), pltpu.roll(lon[1, 0, at, :], lanes - 1, 1)
+        west = pltpu.roll(lon[0, step, at, :], 1, 1)
+        east = pltpu.roll(lon[1, step, at, :], lanes - 1, 1)
         bands.append(jnp.where(lane8 % 2 == 1, west, east))
     spin = 2.0 * ((gy * rows + sub).astype(jnp.float32) + 0.5) / (rows * n_gy) - 1.0
     spin = SPIN_RATE * spin
     is_top, is_low = gy == n_gy - 1, gy == 0
+    level = pl.ds(pl.multiple_of(first, CHUNK), CHUNK)
     for field in range(4):
-        folded = -mirror[field] if field < 2 else mirror[field]
-        upper = jnp.where(is_top, folded, lat[1, field])
-        lower = jnp.where(is_low, 0.0, lat[0, field])
+        folded = -mirror[field, level, :] if field < 2 else mirror[field, level, :]
+        upper = jnp.where(is_top, folded, lat[1, field, level, :])
+        lower = jnp.where(is_low, 0.0, lat[0, field, level, :])
         for layer in range(CHUNK):
-            here = ocean[field, layer]
-            up = ocean[field, layer - 1] if layer > 0 else above[field, 0]
-            down = ocean[field, layer + 1] if layer < CHUNK - 1 else below[field, 0]
+            at = first + layer
+            here = ocean[field, at]
+            up = ocean[field, jnp.maximum(at - 1, 0)]
+            down = ocean[field, jnp.minimum(at + 1, layers - 1)]
             sides = []
             for v in range(rows // 8):
                 g = (field * CHUNK + layer) * (rows // 8) + v
@@ -674,48 +685,28 @@
             south = jnp.where(sub == 0, lower[layer : layer + 1], pltpu.roll(here, 1, 0))
             north = jnp.where(sub == rows - 1, upper[layer : layer + 1], pltpu.roll(here, rows - 1, 0))
             laplace = east + west + north + south - 4.0 * here
-            value = here + mix[layer] * laplace + VERT_MIX * (up + down - 2.0 * here)
+            value = here + mix[at] * laplace + VERT_MIX * (up + down - 2.0 * here)
             if field == 0:
-                value = value + spin * ocean[1, layer]
+                value = value + spin * ocean[1, at]
             if field == 1:
-                value = value - spin * ocean[0, layer]
-            out[field, layer] = value
-            if field < 2 and layer == 0:
-
-                @pl.when(step == 0)
-                def _():
-                    skin[field] = value
-
-
-def ocean_step(n_gy, ocean, mix, lon, lat, mirror):
-    fields, layers, rows, lanes = ocean.shape
-    steps = layers // CHUNK
-    block = pl.BlockSpec((fields, CHUNK, rows, lanes), lambda i: (0, i, 0, 0))
-    one = (fields, 1, rows, lanes)
-    return pl.pallas_call(
-        functools.partial(ocean_kernel, n_gy),
-        grid=(steps,),
-        out_shape=(shape(*ocean.shape), shape(2, rows, lanes)),
-        in_specs=[
-            block,
-            pl.BlockSpec(one, lambda i: (0, jnp.maximum(i * CHUNK - 1, 0), 0, 0)),
-            pl.BlockSpec(one, lambda i: (0, jnp.minimum(i * CHUNK + CHUNK, layers - 1), 0, 0)),
-            pl.BlockSpec((CHUNK, rows, lanes), lambda i: (i, 0, 0)),
-            pl.BlockSpec((2, 1, 16, lanes), lambda i: (0, i, 0, 0)),
-            pl.BlockSpec((2, fields, CHUNK, lanes), lambda i: (0, 0, i, 0)),
-            pl.BlockSpec((fields, CHUNK, lanes), lambda i: (0, i, 0)),
-        ],
-        out_specs=(block, pl.BlockSpec((2, rows, lanes), lambda i: (0, 0, 0))),
-        compiler_params=grant(24),
-        name="ocean",
-    )(ocean, ocean, ocean, mix, lon, lat, mirror)
-
-
-def couple_kernel(n_gx, n_gy, sent, skin, cell, surface, current, *refs):
-    here, there, back, home, *sems = refs
+                value = value - spin * ocean[0, at]
+            out[field, at] = value
+
+
+def couple_kernel(n_gx, n_gy, sent, cell, ocean, mix, lon, lat, mirror, *refs):
+    surface, current, plain, here, there, back, home, *sems = refs
     gx, gy = lax.axis_index("gx"), lax.axis_index("gy")
-    tiles, lanes = n_gx * n_gy, skin.shape[2]
-    rows = skin.shape[1]
+    tiles = n_gx * n_gy
+    rows, lanes = ocean.shape[2:]
+    steps = ocean.shape[1] // CHUNK
+
+    def work(first, last):
+        def one(step, carry):
+            stencil(step, n_gy, ocean, mix, lon, lat, mirror, plain)
+            return carry
+
+        lax.fori_loop(first, last, one, 0)
+
     barrier = pltpu.get_barrier_semaphore()
     for d in range(1, n_gx):
         peer = (lax.rem(gx + d, n_gx), gy)
@@ -725,7 +716,7 @@
         pl.semaphore_signal(barrier, inc=1, device_id=peer, device_id_type=MESH)
     pl.semaphore_wait(barrier, n_gx + n_gy - 2)
 
-    def swap(source, middle, target, sems):
+    def swap(source, middle, target, sems, marks):
         send_x, recv_x, send_y, recv_y, local = sems
         own = pltpu.make_async_copy(source.at[gx], middle.at[gx], local)
         own.start()
@@ -744,6 +735,7 @@
             )
         for copy in copies:
             copy.start()
+        work(marks[0], marks[1])
         own.wait()
         for copy in copies:
             copy.wait()
@@ -764,11 +756,12 @@
             )
         for copy in copies:
             copy.start()
+        work(marks[1], marks[2])
         own.wait()
         for copy in copies:
             copy.wait()
 
-    swap(sent, here, there, sems[0:5])
+    swap(sent, here, there, sems[0:5], (0, steps // 3, steps // 2))
     cells = jnp.concatenate([cell[0:1], cell[1:2]], axis=1)
     cell_row, cell_col = cells // lanes, cells % lanes
     pick = (lax.broadcasted_iota(jnp.int32, (lanes, 2 * tiles), 0) == cell_col).astype(jnp.bfloat16)
@@ -784,7 +777,8 @@
         (((1,), (1,)), ((), ())),
         preferred_element_type=jnp.float32,
     )
-    level = skin[...].reshape(2 * rows, lanes) + joined(forcing)
+    skin = jnp.concatenate([plain[0, 0], plain[1, 0]], axis=0)
+    level = skin + joined(forcing)
     surface[...] = level.reshape(2, rows, lanes)
     found = joined(jnp.dot(split(level), pick, preferred_element_type=jnp.float32))
     replies = []
@@ -794,28 +788,39 @@
         replies += [values[:, :tiles], values[:, tiles:]]
     replies.append(jnp.zeros((lanes - 4, tiles), jnp.float32))
     back[...] = jnp.concatenate(replies, axis=0).T.reshape(back.shape)
-    swap(back, home, current, sems[5:10])
-
-
-def couple(n_gx, n_gy, sent, skin, cell):
-    tiles, lanes = n_gx * n_gy, skin.shape[2]
+    swap(back, home, current, sems[5:10], (steps // 2, steps - 1, steps))
+
+
+def couple(n_gx, n_gy, sent, cell, ocean, *sea):
+    tiles = n_gx * n_gy
+    rows, lanes = ocean.shape[2:]
     box = (n_gx, n_gy, 1, lanes)
     dma = pltpu.SemaphoreType.DMA
     sems = [dma((n_gx - 1,)), dma((n_gx - 1,)), dma((n_gy - 1,)), dma((n_gy - 1,)), dma]
     return pl.pallas_call(
         functools.partial(couple_kernel, n_gx, n_gy),
-        out_shape=(shape(*skin.shape), shape(*box)),
-        in_specs=[VMEM] * 3,
-        out_specs=(VMEM,) * 2,
+        out_shape=(shape(2, rows, lanes), shape(*box), shape(*ocean.shape)),
+        in_specs=[VMEM] * (3 + len(sea)),
+        out_specs=(VMEM,) * 3,
         scratch_shapes=[pltpu.VMEM(box, jnp.float32)] * 4 + sems + sems,
-        compiler_params=grant(4, collective_id=SUB, has_side_effects=True),
+        compiler_params=grant(16, collective_id=SUB, has_side_effects=True),
         name="couple",
-    )(sent.reshape(box), skin, cell)
-
-
-def finish_kernel(ocean, surface, current, slots, vel, vel_out, ocean_out, sem):
-    copy = pltpu.make_async_copy(surface, ocean_out.at[pl.ds(0, 2), 0], sem)
-    copy.start()
+    )(sent.reshape(box), cell, ocean, *sea)
+
+
+def finish_kernel(plain, surface, current, slots, vel, vel_out, ocean_out, sems):
+    layers = plain.shape[1]
+    copies = [
+        pltpu.make_async_copy(surface, ocean_out.at[pl.ds(0, 2), 0], sems.at[0]),
+        pltpu.make_async_copy(plain.at[pl.ds(2, 2)], ocean_out.at[pl.ds(2, 2)], sems.at[1]),
+    ]
+    for field in range(2):
+        deep = pl.ds(1, layers - 1)
+        copies.append(
+            pltpu.make_async_copy(plain.at[field, deep], ocean_out.at[field, deep], sems.at[2 + field])
+        )
+    for copy in copies:
+        copy.start()
     blocks, discs = vel.shape[1], vel.shape[2]
     tiles = current.shape[0]
     got = current[...].reshape(tiles, discs).T
@@ -826,21 +831,21 @@
         values = jnp.sum(jnp.where(place, values, 0.0), axis=1, keepdims=True)
         speed = vel[comp]
         vel_out[comp] = speed + DRAG_BACK * (values - speed)
-    copy.wait()
-
-
-def finish(ocean, surface, current, slots, vel):
+    for copy in copies:
+        copy.wait()
+
+
+def finish(plain, surface, current, slots, vel):
     tiles = current.shape[0] * current.shape[1]
     return pl.pallas_call(
         finish_kernel,
-        out_shape=(shape(*vel.shape), shape(*ocean.shape)),
-        in_specs=[ANY, VMEM, VMEM, VMEM, VMEM],
+        out_shape=(shape(*vel.shape), shape(*plain.shape)),
+        in_specs=[VMEM] * 5,
         out_specs=(VMEM, ANY),
-        scratch_shapes=[pltpu.SemaphoreType.DMA],
-        input_output_aliases={0: 1},
+        scratch_shapes=[pltpu.SemaphoreType.DMA((4,))],
         compiler_params=grant(4),
         name="finish",
-    )(ocean, surface, current.reshape(tiles, 1, current.shape[3]), slots, vel)
+    )(plain, surface, current.reshape(tiles, 1, current.shape[3]), slots, vel)
 
 
 def body(
@@ -867,10 +872,10 @@
     bonds = bond_list.reshape(BONDS, blocks, discs)
     sea_shape = (4, mix_coef.shape[0], discs)
     flat = (4 * mix_coef.shape[0], discs)
-    position, rad, edges, mask = prep(n_gy, position, rad, contact_mask)
+    position, rad, edges = prep(position, rad)
     halo, held, marks, halo_rad = exchange(0, n_gx, n_gy, position, rad, edges)
-    position, velocity, edges = contact_step(
-        0, n_gy, position, velocity, rad, bonds, mask, marks, held, halo, halo_rad
+    position, velocity, edges, mask = contact_step(
+        0, n_gy, position, velocity, rad, bonds, contact_mask, marks, held, halo, halo_rad
     )
     sides, bottom, top = pack(ocean_state, edges)
     halo, held, marks, lon, lat, rows, perms = exchange(
@@ -883,11 +888,9 @@
     position, velocity, sent = contact_step(
         2, n_gy, position, velocity, rad, bonds, mask, marks, held, halo, halo_rad, slots
     )
-    ocean, skin = ocean_step(
-        n_gy, ocean_state, mix_coef, lon, lat.reshape(2, *sea_shape), mirror.reshape(sea_shape)
-    )
-    surface, current = couple(n_gx, n_gy, sent, skin, cell)
-    vel_next, ocean_next = finish(ocean, surface, current, slots, velocity)
+    sea = (mix_coef, lon, lat.reshape(2, *sea_shape), mirror.reshape(sea_shape))
+    surface, current, plain = couple(n_gx, n_gy, sent, cell, ocean_state, *sea)
+    vel_next, ocean_next = finish(plain, surface, current, slots, velocity)
     return (position.reshape(disc_pos.shape), vel_next.reshape(disc_vel.shape), ocean_next)
 
 

time: 152 us -> 147 us (0.967)
  Pallas kernels: 147 us -> 143 us
  local copies, waits for them, and re-layouts: 4.52 us -> 1.79 us
    pallas_call x3, Pallas kernels: 46 us -> 71.2 us  [contact_step(): pl.pallas_call(functools.partial(contact_kernel, which, n_gy), out_shape=...]
    pallas_call x3, Pallas kernels: 56.7 us -> 44.4 us  [exchange(): pl.pallas_call(functools.partial(exchange_kernel, which, n_gx, n_gy), out...]
    pallas_call x1, Pallas kernels: 35 us -> 23.4 us  [couple(): pl.pallas_call(functools.partial(couple_kernel, n_gx, n_gy), out_shape=(s...]
    pallas_call x3 -> x2, Pallas kernels: 7.38 us -> 2.62 us  [the longest x1 2.37 us: finish(): pl.pallas_call(finish_kernel, out_shape=(shape(*vel.shape), shape(*plain....]
    unnamed x22 -> x20, local copies, waits for them, and re-layouts: 4.52 us -> 1.79 us
where the time goes in v3:
time: 147 us; the launch traced here: 146 us
  Pallas kernels  143 us (97%)
  local copies, waits for them, and re-layouts  1.79 us (1%)
    pallas_call x3, Pallas kernels, contact_step(): pl.pallas_call(functools.partial(contact_kernel, which, n_gy), out_shape=...  71.2 us
    pallas_call x3, Pallas kernels, exchange(): pl.pallas_call(functools.partial(exchange_kernel, which, n_gx, n_gy), out...  44.4 us
    pallas_call x1, Pallas kernels, couple(): pl.pallas_call(functools.partial(couple_kernel, n_gx, n_gy), out_shape=(s...  23.4 us

profile of v3, /device:TPU:1, one launch (start us, length us, event | category | flops | bytes accessed | tf_op | source)
XLA Modules:
  0.0 146.0 jit_solution(1098306242911090279)
XLA Ops:
  0.6 0.0 copy-start.2
  0.6 0.9 copy-done.2
  1.5 0.8 copy-done.3
  2.4 0.2 prep.1
  2.6 0.0 copy-start.6
  2.6 0.0 copy-start.7
  2.7 0.0 copy-start.8
  2.7 13.4 %exchange_first.1 = (f32[8,2,16,128]{3,2,1,0:T(8,128)S(1)}, f32[2,1024,128]{2,1,0:T(8,128)S(1)}, f32[2048,128]{1,0:T(8,128)S(1)}, f32[8,16,128]{2,1,0:T(8,128)S(1)}) custom-call(f32[2,128,128]{2,1,0:T(8,128)S(1)} %get-tuple-element.40.refs_0_.pos, f32[128,128]{1,0:T(8,128)S(1)} %get-tuple-element.41.refs_1_.rad, f32[2,3,8,128]{3,2,1,0:T(8,128)S(1)} %get-tuple-element.42.refs_2_), custom_call_target="tpu_custom_call" | custom-call | flops 4294967296 | bytes 16777216 | tf_op jit(solution)/shard_map/exchange_first/pallas_call | solution.py:640
  16.1 0.0 copy-done.6
  16.1 0.0 copy-done.7
  16.1 0.0 copy-done.8
  16.1 0.0 copy-start
  16.1 15.7 %contact_first.1 = (f32[2,128,128]{2,1,0:T(8,128)S(1)}, f32[2,128,128]{2,1,0:T(8,128)S(1)}, f32[2,2,8,128]{3,2,1,0:T(8,128)S(1)}, f32[128,128]{1,0:T(8,128)S(1)}) custom-call(f32[2,128,128]{2,1,0:T(8,128)S(1)} %get-tuple-element.40.refs_0_.pos, f32[2,128,128]{2,1,0:T(8,128)S(1)} %bitcast.31, f32[128,128]{1,0:T(8,128)S(1)} %get-tuple-element.41.refs_1_.rad, ...), custom_call_target="tpu_custom_call" | custom-call | flops 4294967296 | bytes 16777216 | tf_op jit(solution)/shard_map/contact_first/pallas_call | solution.py:370
  31.8 0.0 copy-start.9
  31.8 1.6 %pack.1 = (f32[6,16,128]{2,1,0:T(8,128)S(1)}, f32[4,48,128]{2,1,0:T(8,128)S(1)}, f32[4,48,128]{2,1,0:T(8,128)S(1)}) custom-call(f32[4,48,32,128]{3,2,1,0:T(8,128)S(1)} %copy-done, f32[2,2,8,128]{3,2,1,0:T(8,128)S(1)} %get-tuple-element.50.after.refs_2_), custom_call_target="tpu_custom_call" | custom-call | tf_op jit(solution)/shard_map/pack/pallas_call | solution.py:437
  33.5 21.5 %exchange_second.1 = (f32[8,2,16,128]{3,2,1,0:T(8,128)S(1)}, f32[2,1024,128]{2,1,0:T(8,128)S(1)}, f32[2048,128]{1,0:T(8,128)S(1)}, f32[2,6,16,128]{3,2,1,0:T(8,1...) custom-call(f32[2,128,128]{2,1,0:T(8,128)S(1)} %get-tuple-element.47.refs_0_.pos, ...), custom_call_target="tpu_custom_call" | custom-call | flops 4294967296 | bytes 16777216 | tf_op jit(solution)/shard_map/exchange_second/pallas_call | solution.py:640
  55.0 27.4 %contact.1 = (f32[2,128,128]{2,1,0:T(8,128)S(1)}, f32[2,128,128]{2,1,0:T(8,128)S(1)}, f32[2,2,8,128]{3,2,1,0:T(8,128)S(1)}, f32[16,16,128]{2,1,0:T(8,128)S(1)}) custom-call(f32[2,128,128]{2,1,0:T(8,128)S(1)} %get-tuple-element.47.refs_0_.pos, f32[2,128,128]{2,1,0:T(8,128)S(1)} %get-tuple-element.48.vel, f32[128,128]{1,0:T(8,128)S(1)} %get-tuple-element.41.refs_1_.rad, ...), custom_call_target="tpu_custom_call" | custom-call | flops 4294967296 | bytes 16777216 | tf_op jit(solution)/shard_map/contact/pallas_call | solution.py:370
  82.4 0.0 copy-start.5
  82.4 9.4 %exchange_third.1 = (f32[8,2,16,128]{3,2,1,0:T(8,128)S(1)}, f32[2,1024,128]{2,1,0:T(8,128)S(1)}, f32[2048,128]{1,0:T(8,128)S(1)}, f32[12,16,128]{2,1,0:T(8,128)S(1)}) custom-call(f32[2,128,128]{2,1,0:T(8,128)S(1)} %get-tuple-element.59.refs_0_.pos, f32[128,128]{1,0:T(8,128)S(1)} %get-tuple-element.41.refs_1_.rad, ...), custom_call_target="tpu_custom_call" | custom-call | flops 4294967296 | bytes 16777216 | tf_op jit(solution)/shard_map/exchange_third/pallas_call | solution.py:640
  91.8 0.0 copy-start.1
  91.9 0.0 copy-start.4
  91.9 28.2 %contact_last.1 = (f32[2,128,128]{2,1,0:T(8,128)}, f32[2,128,128]{2,1,0:T(8,128)S(1)}, f32[128,1,128]{2,1,0:T(1,128)S(1)}) custom-call(f32[2,128,128]{2,1,0:T(8,128)S(1)} %get-tuple-element.59.refs_0_.pos, f32[2,128,128]{2,1,0:T(8,128)S(1)} %get-tuple-element.60.vel, f32[128,128]{1,0:T(8,128)S(1)} %get-tuple-element.41.refs_1_.rad, ...), custom_call_target="tpu_custom_call" | custom-call | flops 4294967296 | bytes 16777216 | tf_op jit(solution)/shard_map/contact_last/pallas_call | solution.py:370
  120.1 23.4 %couple.1 = (f32[2,32,128]{2,1,0:T(8,128)S(1)}, f32[16,8,1,128]{3,2,1,0:T(1,128)S(1)}, f32[4,48,32,128]{3,2,1,0:T(8,128)S(1)}) custom-call(f32[16,8,1,128]{3,2,1,0:T(1,128)S(1)} %bitcast.22, s32[2,128]{1,0:T(2,128)S(1)} %bitcast.25, f32[4,48,32,128]{3,2,1,0:T(8,128)S(1)} %copy-done, f32[48,32,128]{2,1,0:T(8,128)S(1)} %copy-done.1, ...), custom_call_target="tpu_custom_call" | custom-call | tf_op jit(solution)/shard_map/couple/pallas_call | solution.py:800
  143.5 2.4 %finish.1 = (f32[2,128,128]{2,1,0:T(8,128)}, f32[4,48,32,128]{3,2,1,0:T(8,128)}) custom-call(f32[4,48,32,128]{3,2,1,0:T(8,128)S(1)} %get-tuple-element.71.plain, f32[2,32,128]{2,1,0:T(8,128)S(1)} %get-tuple-element.72.surface, f32[128,1,128]{2,1,0:T(1,128)S(1)} %bitcast.24, s32[2,128]{1,0:T(2,128)S(1)} %bitcast.27, f32[2,128,128]{2,1,0:T(8,128)S(1)} %get-tuple-element.74.vel), custom_call_target="tpu_custom_call" | custom-call | tf_op jit(solution)/shard_map/finish/pallas_call | solution.py:840
  (6 shorter events, 0.0 us)
Async XLA Ops:
  0.6 0.9 copy-start.2
  1.5 0.8 copy-start.3
  2.6 13.5 %copy-start.6 = (s32[4,8,16,128]{3,2,1,0:T(8,128)S(1)}, s32[4,8,16,128]{3,2,1,0:T(8,128)}, u32[]{:S(2)}) copy-start(s32[4,8,16,128]{3,2,1,0:T(8,128)} %param.13) | copy-start | bytes 786436
  2.6 13.5 %copy-start.7 = (f32[2,8,16,128]{3,2,1,0:T(8,128)S(1)}, f32[2,8,16,128]{3,2,1,0:T(8,128)}, u32[]{:S(2)}) copy-start(f32[2,8,16,128]{3,2,1,0:T(8,128)} %param.11) | copy-start | bytes 393220
  2.7 13.5 %copy-start.8 = (s32[8,8,16]{2,1,0:T(8,128)S(1)}, s32[8,8,16]{2,1,0:T(8,128)}, u32[]{:S(2)}) copy-start(s32[8,8,16]{2,1,0:T(8,128)} %mask.1) | copy-start | bytes 12292
  16.1 15.7 %copy-start = (f32[4,48,32,128]{3,2,1,0:T(8,128)S(1)}, f32[4,48,32,128]{3,2,1,0:T(8,128)}, u32[]{:S(2)}) copy-start(f32[4,48,32,128]{3,2,1,0:T(8,128)} %ocean.3) | copy-start | bytes 9437188
  31.8 1.6 %copy-start.9 = (s32[128]{0:T(128)S(1)}, s32[128]{0:T(128)}, u32[]{:S(2)}) copy-start(s32[128]{0:T(128)} %param.19) | copy-start | bytes 1540
  82.4 9.5 %copy-start.5 = (s32[1,128,2]{1,2,0:T(2,128)S(1)}, s32[1,128,2]{1,2,0:T(2,128)}, u32[]{:S(2)}) copy-start(s32[1,128,2]{1,2,0:T(2,128)} %param.15) | copy-start | bytes 3076
  91.8 28.2 %copy-start.1 = (f32[48,32,128]{2,1,0:T(8,128)S(1)}, f32[48,32,128]{2,1,0:T(8,128)}, u32[]{:S(2)}) copy-start(f32[48,32,128]{2,1,0:T(8,128)} %mix.1) | copy-start | bytes 2359300
  91.9 28.2 %copy-start.4 = (s32[1,128,2]{1,2,0:T(2,128)S(1)}, s32[1,128,2]{1,2,0:T(2,128)}, u32[]{:S(2)}) copy-start(s32[1,128,2]{1,2,0:T(2,128)} %param.18) | copy-start | bytes 3076

commit v4 on v3

--- a/solution.py
+++ b/solution.py
@@ -19,9 +19,9 @@
 SPIN_RATE = 0.3
 NEIGHBOURS = ((-1, -1), (-1, 0), (-1, 1), (0, -1), (0, 1), (1, -1), (1, 0), (1, 1))
 ROWS = 1
-OWN_STEP = 8
-NEAR_STEP = 16
-REST_STEP = 8
+OWN_STEP = 16
+NEAR_STEP = 32
+REST_STEP = 16
 HALF = 64
 MARKS = 16
 CHUNK = 8

time: 147 us -> 140 us (0.952)
  Pallas kernels: 143 us -> 137 us
    pallas_call x3, Pallas kernels: 71.2 us -> 40.6 us  [contact_step(): pl.pallas_call(functools.partial(contact_kernel, which, n_gy), out_shape=...]
    pallas_call x3, Pallas kernels: 44.4 us -> 59.7 us  [exchange(): pl.pallas_call(functools.partial(exchange_kernel, which, n_gx, n_gy), out...]
    pallas_call x1, Pallas kernels: 23.4 us -> 32.7 us  [couple(): pl.pallas_call(functools.partial(couple_kernel, n_gx, n_gy), out_shape=(s...]
where the time goes in v4:
time: 140 us
  Pallas kernels  137 us (98%)
  local copies, waits for them, and re-layouts  1.79 us (1%)
    pallas_call x3, Pallas kernels, exchange(): pl.pallas_call(functools.partial(exchange_kernel, which, n_gx, n_gy), out...  59.7 us
    pallas_call x3, Pallas kernels, contact_step(): pl.pallas_call(functools.partial(contact_kernel, which, n_gy), out_shape=...  40.6 us
    pallas_call x1, Pallas kernels, couple(): pl.pallas_call(functools.partial(couple_kernel, n_gx, n_gy), out_shape=(s...  32.7 us

profile of v4, /device:TPU:1, one launch (start us, length us, event | category | flops | bytes accessed | tf_op | source)
XLA Modules:
  0.0 140.0 jit_solution(17760416853477598699)
XLA Ops:
  0.6 0.0 copy-start.2
  0.6 0.9 copy-done.2
  1.5 0.8 copy-done.3
  2.4 0.2 prep.1
  2.6 0.0 copy-start.6
  2.6 0.0 copy-start.7
  2.7 0.0 copy-start.8
  2.7 12.4 %exchange_first.1 = (f32[8,2,16,128]{3,2,1,0:T(8,128)S(1)}, f32[2,1024,128]{2,1,0:T(8,128)S(1)}, f32[2048,128]{1,0:T(8,128)S(1)}, f32[8,16,128]{2,1,0:T(8,128)S(1)}) custom-call(f32[2,128,128]{2,1,0:T(8,128)S(1)} %get-tuple-element.40.refs_0_.pos, f32[128,128]{1,0:T(8,128)S(1)} %get-tuple-element.41.refs_1_.rad, f32[2,3,8,128]{3,2,1,0:T(8,128)S(1)} %get-tuple-element.42.refs_2_), custom_call_target="tpu_custom_call" | custom-call | flops 4294967296 | bytes 16777216 | tf_op jit(solution)/shard_map/exchange_first/pallas_call | solution.py:640
  15.1 0.0 copy-start
  15.1 13.3 %contact_first.1 = (f32[2,128,128]{2,1,0:T(8,128)S(1)}, f32[2,128,128]{2,1,0:T(8,128)S(1)}, f32[2,2,8,128]{3,2,1,0:T(8,128)S(1)}, f32[128,128]{1,0:T(8,128)S(1)}) custom-call(f32[2,128,128]{2,1,0:T(8,128)S(1)} %get-tuple-element.40.refs_0_.pos, f32[2,128,128]{2,1,0:T(8,128)S(1)} %bitcast.31, f32[128,128]{1,0:T(8,128)S(1)} %get-tuple-element.41.refs_1_.rad, ...), custom_call_target="tpu_custom_call" | custom-call | flops 4294967296 | bytes 16777216 | tf_op jit(solution)/shard_map/contact_first/pallas_call | solution.py:370
  28.3 0.0 copy-start.9
  28.4 1.6 %pack.1 = (f32[6,16,128]{2,1,0:T(8,128)S(1)}, f32[4,48,128]{2,1,0:T(8,128)S(1)}, f32[4,48,128]{2,1,0:T(8,128)S(1)}) custom-call(f32[4,48,32,128]{3,2,1,0:T(8,128)S(1)} %copy-done, f32[2,2,8,128]{3,2,1,0:T(8,128)S(1)} %get-tuple-element.50.after.refs_2_), custom_call_target="tpu_custom_call" | custom-call | tf_op jit(solution)/shard_map/pack/pallas_call | solution.py:437
  30.0 0.0 copy-done.9
  30.0 23.4 %exchange_second.1 = (f32[8,2,16,128]{3,2,1,0:T(8,128)S(1)}, f32[2,1024,128]{2,1,0:T(8,128)S(1)}, f32[2048,128]{1,0:T(8,128)S(1)}, f32[2,6,16,128]{3,2,1,0:T(8,1...) custom-call(f32[2,128,128]{2,1,0:T(8,128)S(1)} %get-tuple-element.47.refs_0_.pos, ...), custom_call_target="tpu_custom_call" | custom-call | flops 4294967296 | bytes 16777216 | tf_op jit(solution)/shard_map/exchange_second/pallas_call | solution.py:640
  53.4 13.1 %contact.1 = (f32[2,128,128]{2,1,0:T(8,128)S(1)}, f32[2,128,128]{2,1,0:T(8,128)S(1)}, f32[2,2,8,128]{3,2,1,0:T(8,128)S(1)}, f32[16,16,128]{2,1,0:T(8,128)S(1)}) custom-call(f32[2,128,128]{2,1,0:T(8,128)S(1)} %get-tuple-element.47.refs_0_.pos, f32[2,128,128]{2,1,0:T(8,128)S(1)} %get-tuple-element.48.vel, f32[128,128]{1,0:T(8,128)S(1)} %get-tuple-element.41.refs_1_.rad, ...), custom_call_target="tpu_custom_call" | custom-call | flops 4294967296 | bytes 16777216 | tf_op jit(solution)/shard_map/contact/pallas_call | solution.py:370
  66.5 0.0 copy-start.5
  66.5 23.9 %exchange_third.1 = (f32[8,2,16,128]{3,2,1,0:T(8,128)S(1)}, f32[2,1024,128]{2,1,0:T(8,128)S(1)}, f32[2048,128]{1,0:T(8,128)S(1)}, f32[12,16,128]{2,1,0:T(8,128)S(1)}) custom-call(f32[2,128,128]{2,1,0:T(8,128)S(1)} %get-tuple-element.59.refs_0_.pos, f32[128,128]{1,0:T(8,128)S(1)} %get-tuple-element.41.refs_1_.rad, ...), custom_call_target="tpu_custom_call" | custom-call | flops 4294967296 | bytes 16777216 | tf_op jit(solution)/shard_map/exchange_third/pallas_call | solution.py:640
  90.5 0.0 copy-start.1
  90.5 0.0 copy-start.4
  90.5 14.2 %contact_last.1 = (f32[2,128,128]{2,1,0:T(8,128)}, f32[2,128,128]{2,1,0:T(8,128)S(1)}, f32[128,1,128]{2,1,0:T(1,128)S(1)}) custom-call(f32[2,128,128]{2,1,0:T(8,128)S(1)} %get-tuple-element.59.refs_0_.pos, f32[2,128,128]{2,1,0:T(8,128)S(1)} %get-tuple-element.60.vel, f32[128,128]{1,0:T(8,128)S(1)} %get-tuple-element.41.refs_1_.rad, ...), custom_call_target="tpu_custom_call" | custom-call | flops 4294967296 | bytes 16777216 | tf_op jit(solution)/shard_map/contact_last/pallas_call | solution.py:370
  104.7 0.0 copy-done.1
  104.8 0.0 copy-done.4
  104.8 32.7 %couple.1 = (f32[2,32,128]{2,1,0:T(8,128)S(1)}, f32[16,8,1,128]{3,2,1,0:T(1,128)S(1)}, f32[4,48,32,128]{3,2,1,0:T(8,128)S(1)}) custom-call(f32[16,8,1,128]{3,2,1,0:T(1,128)S(1)} %bitcast.22, s32[2,128]{1,0:T(2,128)S(1)} %bitcast.25, f32[4,48,32,128]{3,2,1,0:T(8,128)S(1)} %copy-done, f32[48,32,128]{2,1,0:T(8,128)S(1)} %copy-done.1, ...), custom_call_target="tpu_custom_call" | custom-call | tf_op jit(solution)/shard_map/couple/pallas_call | solution.py:800
  137.5 2.4 %finish.1 = (f32[2,128,128]{2,1,0:T(8,128)}, f32[4,48,32,128]{3,2,1,0:T(8,128)}) custom-call(f32[4,48,32,128]{3,2,1,0:T(8,128)S(1)} %get-tuple-element.71.plain, f32[2,32,128]{2,1,0:T(8,128)S(1)} %get-tuple-element.72.surface, f32[128,1,128]{2,1,0:T(1,128)S(1)} %bitcast.24, s32[2,128]{1,0:T(2,128)S(1)} %bitcast.27, f32[2,128,128]{2,1,0:T(8,128)S(1)} %get-tuple-element.74.vel), custom_call_target="tpu_custom_call" | custom-call | tf_op jit(solution)/shard_map/finish/pallas_call | solution.py:840
  (6 shorter events, 0.0 us)
Async XLA Ops:
  0.6 0.9 copy-start.2
  1.5 0.8 copy-start.3
  2.6 12.4 %copy-start.6 = (s32[4,8,16,128]{3,2,1,0:T(8,128)S(1)}, s32[4,8,16,128]{3,2,1,0:T(8,128)}, u32[]{:S(2)}) copy-start(s32[4,8,16,128]{3,2,1,0:T(8,128)} %param.13) | copy-start | bytes 786436
  2.6 12.4 %copy-start.7 = (f32[2,8,16,128]{3,2,1,0:T(8,128)S(1)}, f32[2,8,16,128]{3,2,1,0:T(8,128)}, u32[]{:S(2)}) copy-start(f32[2,8,16,128]{3,2,1,0:T(8,128)} %param.11) | copy-start | bytes 393220
  2.7 12.4 %copy-start.8 = (s32[8,8,16]{2,1,0:T(8,128)S(1)}, s32[8,8,16]{2,1,0:T(8,128)}, u32[]{:S(2)}) copy-start(s32[8,8,16]{2,1,0:T(8,128)} %mask.1) | copy-start | bytes 12292
  15.1 13.3 %copy-start = (f32[4,48,32,128]{3,2,1,0:T(8,128)S(1)}, f32[4,48,32,128]{3,2,1,0:T(8,128)}, u32[]{:S(2)}) copy-start(f32[4,48,32,128]{3,2,1,0:T(8,128)} %ocean.3) | copy-start | bytes 9437188
  28.3 1.6 %copy-start.9 = (s32[128]{0:T(128)S(1)}, s32[128]{0:T(128)}, u32[]{:S(2)}) copy-start(s32[128]{0:T(128)} %param.19) | copy-start | bytes 1540
  66.5 24.0 %copy-start.5 = (s32[1,128,2]{1,2,0:T(2,128)S(1)}, s32[1,128,2]{1,2,0:T(2,128)}, u32[]{:S(2)}) copy-start(s32[1,128,2]{1,2,0:T(2,128)} %param.15) | copy-start | bytes 3076
  90.5 14.3 %copy-start.1 = (f32[48,32,128]{2,1,0:T(8,128)S(1)}, f32[48,32,128]{2,1,0:T(8,128)}, u32[]{:S(2)}) copy-start(f32[48,32,128]{2,1,0:T(8,128)} %mix.1) | copy-start | bytes 2359300
  90.5 14.3 %copy-start.4 = (s32[1,128,2]{1,2,0:T(2,128)S(1)}, s32[1,128,2]{1,2,0:T(2,128)}, u32[]{:S(2)}) copy-start(s32[1,128,2]{1,2,0:T(2,128)} %param.18) | copy-start | bytes 3076

commit v5 on v4

--- a/solution.py
+++ b/solution.py
@@ -18,7 +18,6 @@
 VERT_MIX = 0.1
 SPIN_RATE = 0.3
 NEIGHBOURS = ((-1, -1), (-1, 0), (-1, 1), (0, -1), (0, 1), (1, -1), (1, 0), (1, 1))
-ROWS = 1
 OWN_STEP = 16
 NEAR_STEP = 32
 REST_STEP = 16
@@ -208,74 +207,77 @@
     low_col = lax.broadcasted_iota(jnp.int32, (blocks, blocks), 1)
     lower = (low_col <= low_row).astype(jnp.bfloat16)
 
-    def collect(start):
-        def one_row(step_y, carry):
-            units, totals = [], []
-            for half in range(ROWS * cols_dev // 8):
-                y = step_y * ROWS + half // (cols_dev // 8)
-                x0 = half % (cols_dev // 8) * 8
-                at = pl.ds(pl.multiple_of(y * cols_dev + x0, 8), 8)
-                own = [pos[0, at, :], pos[1, at, :], rad[at, :]]
-                reach = jnp.max(own[2], axis=1, keepdims=True)
-                low = [jnp.min(own[c], axis=1, keepdims=True) - reach for c in range(2)]
-                high = [jnp.max(own[c], axis=1, keepdims=True) + reach for c in range(2)]
-                weights = mask[at, :]
-                flags = []
-                places = []
-                for k, (sy, sx) in enumerate(NEIGHBOURS):
-                    place = (y + 1 + sy, pl.ds(x0 + 1 + sx, 8), slice(None))
-                    nx, ny, nr = (wide[(c,) + place] for c in range(3))
-                    close = (nx - nr < high[0] - float(sx)) & (nx + nr > low[0] - float(sx))
-                    close = close & (ny - nr < high[1] - float(sy)) & (ny + nr > low[1] - float(sy))
-                    close = close & (weights[:, k : k + 1] > 0.5)
-                    flags.append(close.astype(jnp.float32))
-                    places.append(place)
-                ranks = jnp.dot(
-                    jnp.concatenate(flags, axis=0).astype(jnp.bfloat16),
-                    triangle,
-                    preferred_element_type=jnp.float32,
-                )
-                base = jnp.zeros((8, discs), jnp.float32) - start
-                for k in range(8):
-                    rank = ranks[8 * k : 8 * k + 8, :discs]
-                    total = ranks[8 * k : 8 * k + 8, discs:]
-                    want = lane_f - base
-                    source = jnp.zeros((8, discs), jnp.int32)
-                    units.append((half, k, source, places[k], rank, total, want))
-                    base = base + total
-                totals.append((at, base))
-            sources = [u[2] for u in units]
-            step = discs // 2
-            while step >= 1:
-                probes = [lane_take(u[4], i + (step - 1)) for u, i in zip(units, sources)]
-                sources = [
-                    jnp.where(probe <= u[6], i + step, i)
-                    for probe, u, i in zip(probes, units, sources)
-                ]
-                step //= 2
-            for half, (at, base) in enumerate(totals):
-                mine = [(u, i) for u, i in zip(units, sources) if u[0] == half]
-                for comp in range(3):
-                    got = jnp.full((8, discs), -1.0 if comp == 2 else 0.0, jnp.float32)
-                    for (_, k, _, place, _, total, want), source in mine:
-                        valid = (want >= 0.0) & (want < total)
-                        value = wide[(comp,) + place]
-                        if comp < 2 and NEIGHBOURS[k][1 - comp] != 0:
-                            value = value + float(NEIGHBOURS[k][1 - comp])
-                        got = jnp.where(valid, lane_take(value, source), got)
-                    found[comp, at, :] = got
-                found[3, at, :] = base
+    def collect_row(y, start):
+        units, totals = [], []
+        for half in range(cols_dev // 8):
+            x0 = half * 8
+            at = pl.ds(pl.multiple_of(y * cols_dev + x0, 8), 8)
+            own = [pos[0, at, :], pos[1, at, :], rad[at, :]]
+            reach = jnp.max(own[2], axis=1, keepdims=True)
+            low = [jnp.min(own[c], axis=1, keepdims=True) - reach for c in range(2)]
+            high = [jnp.max(own[c], axis=1, keepdims=True) + reach for c in range(2)]
+            weights = mask[at, :]
+            flags = []
+            places = []
+            for k, (sy, sx) in enumerate(NEIGHBOURS):
+                place = (y + 1 + sy, pl.ds(x0 + 1 + sx, 8), slice(None))
+                nx, ny, nr = (wide[(c,) + place] for c in range(3))
+                close = (nx - nr < high[0] - float(sx)) & (nx + nr > low[0] - float(sx))
+                close = close & (ny - nr < high[1] - float(sy)) & (ny + nr > low[1] - float(sy))
+                close = close & (weights[:, k : k + 1] > 0.5)
+                flags.append(close.astype(jnp.float32))
+                places.append(place)
+            ranks = jnp.dot(
+                jnp.concatenate(flags, axis=0).astype(jnp.bfloat16),
+                triangle,
+                preferred_element_type=jnp.float32,
+            )
+            base = jnp.zeros((8, discs), jnp.float32) - start
+            for k in range(8):
+                rank = ranks[8 * k : 8 * k + 8, :discs]
+                total = ranks[8 * k : 8 * k + 8, discs:]
+                want = lane_f - base
+                source = jnp.zeros((8, discs), jnp.int32)
+                units.append((half, k, source, places[k], rank, total, want))
+                base = base + total
+            totals.append((at, base))
+        sources = [u[2] for u in units]
+        step = discs // 2
+        while step >= 1:
+            probes = [lane_take(u[4], i + (step - 1)) for u, i in zip(units, sources)]
+            sources = [
+                jnp.where(probe <= u[6], i + step, i)
+                for probe, u, i in zip(probes, units, sources)
+            ]
+            step //= 2
+        for half, (at, base) in enumerate(totals):
+            mine = [(u, i) for u, i in zip(units, sources) if u[0] == half]
+            for comp in range(3):
+                got = jnp.full((8, discs), -1.0 if comp == 2 else 0.0, jnp.float32)
+                for (_, k, _, place, _, total, want), source in mine:
+                    valid = (want >= 0.0) & (want < total)
+                    value = wide[(comp,) + place]
+                    if comp < 2 and NEIGHBOURS[k][1 - comp] != 0:
+                        value = value + float(NEIGHBOURS[k][1 - comp])
+                    got = jnp.where(valid, lane_take(value, source), got)
+                found[comp, at, :] = got
+            found[3, at, :] = base
+
+    def collect():
+        def one_row(y, carry):
+            collect_row(y, 0.0)
             return carry
 
-        lax.fori_loop(0, rows_dev // ROWS, one_row, 0)
+        lax.fori_loop(0, rows_dev, one_row, 0)
         write_marks([found[k] for k in range(3)], seen)
         left = found[3]
-        size = jnp.where(left > float(HALF), 1.0, 0.0)
-        ends = jnp.dot(lower, size.astype(jnp.bfloat16), preferred_element_type=jnp.float32)
         spot = lax.broadcasted_iota(jnp.int32, (1, discs), 1).astype(jnp.float32)
-        block = jnp.sum(jnp.where(ends <= spot, 1.0, 0.0), axis=0, keepdims=True)
-        tally[0:1] = block.astype(jnp.int32)
-        tally[1:2] = ends[blocks - 1 :].astype(jnp.int32)
+        for row, bound in ((0, HALF), (3, discs)):
+            size = jnp.where(left > float(bound), 1.0, 0.0)
+            ends = jnp.dot(lower, size.astype(jnp.bfloat16), preferred_element_type=jnp.float32)
+            block = jnp.sum(jnp.where(ends <= spot, 1.0, 0.0), axis=0, keepdims=True)
+            tally[row : row + 1] = block.astype(jnp.int32)
+            tally[row + 1 : row + 2] = ends[blocks - 1 :].astype(jnp.int32)
         deepest = jnp.max(left, axis=0, keepdims=True)
         tally[2:3] = jnp.ceil(deepest * (1.0 / discs)).astype(jnp.int32)
         copy = pltpu.make_async_copy(tally, work, sem)
@@ -293,29 +295,36 @@
             else:
                 force[k, at, :] += acc[k]
 
-    def sweep(fresh):
-        def some(t, carry):
-            for u in range(NEAR_STEP):
-                meet(t * NEAR_STEP + u, 0, fresh)
+    def some(t, carry):
+        for u in range(NEAR_STEP):
+            meet(t * NEAR_STEP + u, 0, True)
+        return carry
+
+    def rest(t, carry):
+        for u in range(REST_STEP):
+            meet(work[0, t * REST_STEP + u], 1, False)
+        return carry
+
+    def crowded(i, carry):
+        b = work[3, i]
+        y = b // cols_dev
+        at = pl.ds(pl.multiple_of(y * cols_dev, cols_dev), cols_dev)
+        first = pl.multiple_of(y * (cols_dev * MARKS), cols_dev * MARKS)
+        near = seen.at[pl.ds(first, cols_dev * MARKS), :]
+
+        def deeper(p, carry):
+            collect_row(y, p.astype(jnp.float32) * discs)
+            write_marks([found[k, at, :] for k in range(3)], near)
+            for part in range(2):
+                meet(b, part, False)
             return carry
 
-        def rest(t, carry):
-            for u in range(REST_STEP):
-                meet(work[0, t * REST_STEP + u], 1, False)
-            return carry
-
-        lax.fori_loop(0, blocks // NEAR_STEP, some, 0)
-        lax.fori_loop(0, (work[1, 0] + (REST_STEP - 1)) // REST_STEP, rest, 0)
-
-    collect(0.0)
-    sweep(True)
-
-    def more(p, carry):
-        collect(p.astype(jnp.float32) * discs)
-        sweep(False)
-        return carry
-
-    lax.fori_loop(1, work[2, 0], more, 0)
+        return lax.fori_loop(1, work[2, 0], deeper, carry)
+
+    collect()
+    lax.fori_loop(0, blocks // NEAR_STEP, some, 0)
+    lax.fori_loop(0, (work[1, 0] + (REST_STEP - 1)) // REST_STEP, rest, 0)
+    lax.fori_loop(0, work[4, 0], crowded, 0)
 
     def update(g, carry):
         at = pl.ds(pl.multiple_of(g * 8, 8), 8)

time: 140 us -> 117 us (0.84); the launches traced: 140 us -> 115 us
  Pallas kernels: 137 us -> 113 us
    pallas_call x3, Pallas kernels: 59.7 us -> 36.9 us  [exchange(): pl.pallas_call(functools.partial(exchange_kernel, which, n_gx, n_gy), out...]
    pallas_call x1, Pallas kernels: 32.7 us -> 31.1 us  [couple(): pl.pallas_call(functools.partial(couple_kernel, n_gx, n_gy), out_shape=(s...]
where the time goes in v5:
time: 117 us; the launch traced here: 115 us
  Pallas kernels  113 us (97%)
  local copies, waits for them, and re-layouts  1.79 us (2%)
    pallas_call x3, Pallas kernels, contact_step(): pl.pallas_call(functools.partial(contact_kernel, which, n_gy), out_shape=...  40.3 us
    pallas_call x3, Pallas kernels, exchange(): pl.pallas_call(functools.partial(exchange_kernel, which, n_gx, n_gy), out...  36.9 us
    pallas_call x1, Pallas kernels, couple(): pl.pallas_call(functools.partial(couple_kernel, n_gx, n_gy), out_shape=(s...  31.1 us
    pallas_call x1, Pallas kernels, finish(): pl.pallas_call(finish_kernel, out_shape=(shape(*vel.shape), shape(*plain....  2.37 us

profile of v5, /device:TPU:1, one launch (start us, length us, event | category | flops | bytes accessed | tf_op | source)
XLA Modules:
  0.0 115.3 jit_solution(2013980215396496377)
XLA Ops:
  0.6 0.0 copy-start.2
  0.6 0.9 copy-done.2
  1.5 0.8 copy-done.3
  2.4 0.2 prep.1
  2.6 0.0 copy-start.6
  2.6 0.0 copy-start.7
  2.7 0.0 copy-start.8
  2.7 12.4 %exchange_first.1 = (f32[8,2,16,128]{3,2,1,0:T(8,128)S(1)}, f32[2,1024,128]{2,1,0:T(8,128)S(1)}, f32[2048,128]{1,0:T(8,128)S(1)}, f32[8,16,128]{2,1,0:T(8,128)S(1)}) custom-call(f32[2,128,128]{2,1,0:T(8,128)S(1)} %get-tuple-element.40.refs_0_.pos, f32[128,128]{1,0:T(8,128)S(1)} %get-tuple-element.41.refs_1_.rad, f32[2,3,8,128]{3,2,1,0:T(8,128)S(1)} %get-tuple-element.42.refs_2_), custom_call_target="tpu_custom_call" | custom-call | flops 4294967296 | bytes 16777216 | tf_op jit(solution)/shard_map/exchange_first/pallas_call | solution.py:649
  15.0 0.0 copy-done.6
  15.0 0.0 copy-done.7
  15.1 0.0 copy-done.8
  15.1 0.0 copy-start
  15.1 13.3 %contact_first.1 = (f32[2,128,128]{2,1,0:T(8,128)S(1)}, f32[2,128,128]{2,1,0:T(8,128)S(1)}, f32[2,2,8,128]{3,2,1,0:T(8,128)S(1)}, f32[128,128]{1,0:T(8,128)S(1)}) custom-call(f32[2,128,128]{2,1,0:T(8,128)S(1)} %get-tuple-element.40.refs_0_.pos, f32[2,128,128]{2,1,0:T(8,128)S(1)} %bitcast.31, f32[128,128]{1,0:T(8,128)S(1)} %get-tuple-element.41.refs_1_.rad, ...), custom_call_target="tpu_custom_call" | custom-call | flops 4294967296 | bytes 16777216 | tf_op jit(solution)/shard_map/contact_first/pallas_call | solution.py:379
  28.4 0.0 copy-start.9
  28.4 1.6 %pack.1 = (f32[6,16,128]{2,1,0:T(8,128)S(1)}, f32[4,48,128]{2,1,0:T(8,128)S(1)}, f32[4,48,128]{2,1,0:T(8,128)S(1)}) custom-call(f32[4,48,32,128]{3,2,1,0:T(8,128)S(1)} %copy-done, f32[2,2,8,128]{3,2,1,0:T(8,128)S(1)} %get-tuple-element.50.after.refs_2_), custom_call_target="tpu_custom_call" | custom-call | tf_op jit(solution)/shard_map/pack/pallas_call | solution.py:446
  30.1 11.7 %exchange_second.1 = (f32[8,2,16,128]{3,2,1,0:T(8,128)S(1)}, f32[2,1024,128]{2,1,0:T(8,128)S(1)}, f32[2048,128]{1,0:T(8,128)S(1)}, f32[2,6,16,128]{3,2,1,0:T(8,1...) custom-call(f32[2,128,128]{2,1,0:T(8,128)S(1)} %get-tuple-element.47.refs_0_.pos, ...), custom_call_target="tpu_custom_call" | custom-call | flops 4294967296 | bytes 16777216 | tf_op jit(solution)/shard_map/exchange_second/pallas_call | solution.py:649
  41.7 13.2 %contact.1 = (f32[2,128,128]{2,1,0:T(8,128)S(1)}, f32[2,128,128]{2,1,0:T(8,128)S(1)}, f32[2,2,8,128]{3,2,1,0:T(8,128)S(1)}, f32[16,16,128]{2,1,0:T(8,128)S(1)}) custom-call(f32[2,128,128]{2,1,0:T(8,128)S(1)} %get-tuple-element.47.refs_0_.pos, f32[2,128,128]{2,1,0:T(8,128)S(1)} %get-tuple-element.48.vel, f32[128,128]{1,0:T(8,128)S(1)} %get-tuple-element.41.refs_1_.rad, ...), custom_call_target="tpu_custom_call" | custom-call | flops 4294967296 | bytes 16777216 | tf_op jit(solution)/shard_map/contact/pallas_call | solution.py:379
  54.9 0.0 copy-start.5
  54.9 12.9 %exchange_third.1 = (f32[8,2,16,128]{3,2,1,0:T(8,128)S(1)}, f32[2,1024,128]{2,1,0:T(8,128)S(1)}, f32[2048,128]{1,0:T(8,128)S(1)}, f32[12,16,128]{2,1,0:T(8,128)S(1)}) custom-call(f32[2,128,128]{2,1,0:T(8,128)S(1)} %get-tuple-element.59.refs_0_.pos, f32[128,128]{1,0:T(8,128)S(1)} %get-tuple-element.41.refs_1_.rad, ...), custom_call_target="tpu_custom_call" | custom-call | flops 4294967296 | bytes 16777216 | tf_op jit(solution)/shard_map/exchange_third/pallas_call | solution.py:649
  67.8 0.0 copy-start.1
  67.8 0.0 copy-start.4
  67.9 13.8 %contact_last.1 = (f32[2,128,128]{2,1,0:T(8,128)}, f32[2,128,128]{2,1,0:T(8,128)S(1)}, f32[128,1,128]{2,1,0:T(1,128)S(1)}) custom-call(f32[2,128,128]{2,1,0:T(8,128)S(1)} %get-tuple-element.59.refs_0_.pos, f32[2,128,128]{2,1,0:T(8,128)S(1)} %get-tuple-element.60.vel, f32[128,128]{1,0:T(8,128)S(1)} %get-tuple-element.41.refs_1_.rad, ...), custom_call_target="tpu_custom_call" | custom-call | flops 4294967296 | bytes 16777216 | tf_op jit(solution)/shard_map/contact_last/pallas_call | solution.py:379
  81.7 31.1 %couple.1 = (f32[2,32,128]{2,1,0:T(8,128)S(1)}, f32[16,8,1,128]{3,2,1,0:T(1,128)S(1)}, f32[4,48,32,128]{3,2,1,0:T(8,128)S(1)}) custom-call(f32[16,8,1,128]{3,2,1,0:T(1,128)S(1)} %bitcast.22, s32[2,128]{1,0:T(2,128)S(1)} %bitcast.25, f32[4,48,32,128]{3,2,1,0:T(8,128)S(1)} %copy-done, f32[48,32,128]{2,1,0:T(8,128)S(1)} %copy-done.1, ...), custom_call_target="tpu_custom_call" | custom-call | tf_op jit(solution)/shard_map/couple/pallas_call | solution.py:809
  112.8 2.4 %finish.1 = (f32[2,128,128]{2,1,0:T(8,128)}, f32[4,48,32,128]{3,2,1,0:T(8,128)}) custom-call(f32[4,48,32,128]{3,2,1,0:T(8,128)S(1)} %get-tuple-element.71.plain, f32[2,32,128]{2,1,0:T(8,128)S(1)} %get-tuple-element.72.surface, f32[128,1,128]{2,1,0:T(1,128)S(1)} %bitcast.24, s32[2,128]{1,0:T(2,128)S(1)} %bitcast.27, f32[2,128,128]{2,1,0:T(8,128)S(1)} %get-tuple-element.74.vel), custom_call_target="tpu_custom_call" | custom-call | tf_op jit(solution)/shard_map/finish/pallas_call | solution.py:849
  (6 shorter events, 0.0 us)
Async XLA Ops:
  0.6 0.9 copy-start.2
  1.5 0.8 copy-start.3
  2.6 12.4 %copy-start.6 = (s32[4,8,16,128]{3,2,1,0:T(8,128)S(1)}, s32[4,8,16,128]{3,2,1,0:T(8,128)}, u32[]{:S(2)}) copy-start(s32[4,8,16,128]{3,2,1,0:T(8,128)} %param.13) | copy-start | bytes 786436
  2.6 12.4 %copy-start.7 = (f32[2,8,16,128]{3,2,1,0:T(8,128)S(1)}, f32[2,8,16,128]{3,2,1,0:T(8,128)}, u32[]{:S(2)}) copy-start(f32[2,8,16,128]{3,2,1,0:T(8,128)} %param.11) | copy-start | bytes 393220
  2.7 12.4 %copy-start.8 = (s32[8,8,16]{2,1,0:T(8,128)S(1)}, s32[8,8,16]{2,1,0:T(8,128)}, u32[]{:S(2)}) copy-start(s32[8,8,16]{2,1,0:T(8,128)} %mask.1) | copy-start | bytes 12292
  15.1 13.4 %copy-start = (f32[4,48,32,128]{3,2,1,0:T(8,128)S(1)}, f32[4,48,32,128]{3,2,1,0:T(8,128)}, u32[]{:S(2)}) copy-start(f32[4,48,32,128]{3,2,1,0:T(8,128)} %ocean.3) | copy-start | bytes 9437188
  28.4 1.6 %copy-start.9 = (s32[128]{0:T(128)S(1)}, s32[128]{0:T(128)}, u32[]{:S(2)}) copy-start(s32[128]{0:T(128)} %param.19) | copy-start | bytes 1540
  54.9 12.9 %copy-start.5 = (s32[1,128,2]{1,2,0:T(2,128)S(1)}, s32[1,128,2]{1,2,0:T(2,128)}, u32[]{:S(2)}) copy-start(s32[1,128,2]{1,2,0:T(2,128)} %param.15) | copy-start | bytes 3076
  67.8 13.8 %copy-start.1 = (f32[48,32,128]{2,1,0:T(8,128)S(1)}, f32[48,32,128]{2,1,0:T(8,128)}, u32[]{:S(2)}) copy-start(f32[48,32,128]{2,1,0:T(8,128)} %mix.1) | copy-start | bytes 2359300
  67.8 13.8 %copy-start.4 = (s32[1,128,2]{1,2,0:T(2,128)S(1)}, s32[1,128,2]{1,2,0:T(2,128)}, u32[]{:S(2)}) copy-start(s32[1,128,2]{1,2,0:T(2,128)} %param.18) | copy-start | bytes 3076

commit v6 on v5

--- a/solution.py
+++ b/solution.py
@@ -121,18 +121,20 @@
 def turn(rows, perms, turned):
     lanes = rows.shape[2]
 
-    def one(h, carry):
-        wanted = jnp.broadcast_to(perms[h], (8, lanes))
-        owner, column = wanted // lanes, wanted % lanes
-        for half in range(TURN_ROWS // 8):
-            at = pl.ds(8 * half, 8)
-            got = jnp.zeros((8, lanes), jnp.float32)
-            for source in range(rows.shape[0]):
-                got = jnp.where(owner == source, lane_take(rows[source, at, :], column), got)
-            turned[h, at, :] = got
+    def one(step, carry):
+        for u in range(4):
+            h = step * 4 + u
+            wanted = jnp.broadcast_to(perms[h], (8, lanes))
+            owner, column = wanted // lanes, wanted % lanes
+            for half in range(TURN_ROWS // 8):
+                at = pl.ds(8 * half, 8)
+                got = jnp.zeros((8, lanes), jnp.float32)
+                for source in range(rows.shape[0]):
+                    got = jnp.where(owner == source, lane_take(rows[source, at, :], column), got)
+                turned[h, at, :] = got
         return carry
 
-    lax.fori_loop(0, perms.shape[0], one, 0)
+    lax.fori_loop(0, perms.shape[0] // 4, one, 0)
 
 
 def own_forces(first, count, marks, force):
@@ -463,12 +465,12 @@
         pos, rad, edges, halo, held, marks, halo_rad, *scratch = refs
         send_sem, recv_sem, rad_send, rad_recv = scratch
     elif which == 1:
-        pos, rad, edges, top, bottom, sides, perm, halo, held, marks, lon, lat, rows, perms, *scratch = refs
+        pos, rad, edges, top, bottom, perm, halo, held, marks, lat, rows, perms, *scratch = refs
         send_sem, recv_sem, sea_send, sea_recv, *scratch = scratch
         far_send, far_recv, perm_send, perm_recv, own = scratch
     else:
-        pos, rad, edges, turned, halo, held, marks, mirror, *scratch = refs
-        send_sem, recv_sem, far_send, far_recv, own = scratch
+        pos, rad, edges, turned, sides, halo, held, marks, mirror, lon, *scratch = refs
+        send_sem, recv_sem, sea_send, sea_recv, far_send, far_recv, own = scratch
     gx, gy = lax.axis_index("gx"), lax.axis_index("gy")
     is_top = gy == n_gy - 1
 
@@ -536,14 +538,13 @@
         )
     for copy in copies:
         copy.start()
-    if which == 1:
+    if which > 0:
         sea = (sea_send, sea_recv)
-        later = [
-            send(sides, lon.at[0], sea, 0, at(1, 0)),
-            send(sides, lon.at[1], sea, 1, at(-1, 0)),
-            send(top, lat.at[0], sea, 2, at(0, 1)),
-            send(bottom, lat.at[1], sea, 3, at(0, -1)),
-        ]
+        if which == 1:
+            pairs = ((top, lat.at[0], at(0, 1)), (bottom, lat.at[1], at(0, -1)))
+        else:
+            pairs = ((sides, lon.at[0], at(1, 0)), (sides, lon.at[1], at(-1, 0)))
+        later = [send(pair[0], pair[1], sea, n, pair[2]) for n, pair in enumerate(pairs)]
         copies += later
 
     if which == 1:
@@ -576,6 +577,8 @@
             copy.start()
 
     if which == 2:
+        for copy in later:
+            copy.start()
         me = jnp.minimum(gx, TURNERS - 1)
         mine = pltpu.make_async_copy(turned.at[gx], mirror.at[me], own)
         far = []
@@ -639,13 +642,13 @@
         outs += [shape(8, 16, lanes)]
         scratch += [dma((8,)), dma((8,))]
     if which == 1:
-        top, bottom, sides, perm = args
-        outs += [shape(2, *sides.shape), shape(2, *top.shape)]
+        top, bottom, perm = args
+        outs += [shape(2, *top.shape)]
         outs += [shape(n_gx, TURN_ROWS, lanes), jax.ShapeDtypeStruct((n_gx, 1, lanes), jnp.int32)]
-        scratch += [dma((4,)), dma((4,))] + far + far + [dma((2,))]
+        scratch += [dma((2,)), dma((2,))] + far + far + [dma((2,))]
     if which == 2:
-        outs += [shape(TURNERS, TURN_ROWS, lanes)]
-        scratch += far + [dma]
+        outs += [shape(TURNERS, TURN_ROWS, lanes), shape(2, *args[1].shape)]
+        scratch += [dma((2,)), dma((2,))] + far + [dma]
     return pl.pallas_call(
         functools.partial(exchange_kernel, which, n_gx, n_gy),
         out_shape=tuple(outs),
@@ -887,13 +890,13 @@
         0, n_gy, position, velocity, rad, bonds, contact_mask, marks, held, halo, halo_rad
     )
     sides, bottom, top = pack(ocean_state, edges)
-    halo, held, marks, lon, lat, rows, perms = exchange(
-        1, n_gx, n_gy, position, rad, edges, top.reshape(flat), bottom.reshape(flat), sides, perm
+    halo, held, marks, lat, rows, perms = exchange(
+        1, n_gx, n_gy, position, rad, edges, top.reshape(flat), bottom.reshape(flat), perm
     )
     position, velocity, edges, turned = contact_step(
         1, n_gy, position, velocity, rad, bonds, mask, marks, held, halo, halo_rad, rows, perms
     )
-    halo, held, marks, mirror = exchange(2, n_gx, n_gy, position, rad, edges, turned)
+    halo, held, marks, mirror, lon = exchange(2, n_gx, n_gy, position, rad, edges, turned, sides)
     position, velocity, sent = contact_step(
         2, n_gy, position, velocity, rad, bonds, mask, marks, held, halo, halo_rad, slots
     )

time: 117 us -> 114 us (0.974)
  Pallas kernels: 113 us -> 110 us
    pallas_call x3, Pallas kernels: 36.9 us -> 34.1 us  [exchange(): pl.pallas_call(functools.partial(exchange_kernel, which, n_gx, n_gy), out...]
    pallas_call x3, Pallas kernels: 40.3 us -> 42.6 us  [contact_step(): pl.pallas_call(functools.partial(contact_kernel, which, n_gy), out_shape=...]
    pallas_call x1, Pallas kernels: 31.1 us -> 29.2 us  [couple(): pl.pallas_call(functools.partial(couple_kernel, n_gx, n_gy), out_shape=(s...]
where the time goes in v6:
time: 114 us; the launch traced here: 113 us
  Pallas kernels  110 us (96%)
  local copies, waits for them, and re-layouts  1.79 us (2%)
    pallas_call x3, Pallas kernels, contact_step(): pl.pallas_call(functools.partial(contact_kernel, which, n_gy), out_shape=...  42.6 us
    pallas_call x3, Pallas kernels, exchange(): pl.pallas_call(functools.partial(exchange_kernel, which, n_gx, n_gy), out...  34.1 us
    pallas_call x1, Pallas kernels, couple(): pl.pallas_call(functools.partial(couple_kernel, n_gx, n_gy), out_shape=(s...  29.2 us
    pallas_call x1, Pallas kernels, finish(): pl.pallas_call(finish_kernel, out_shape=(shape(*vel.shape), shape(*plain....  2.37 us

profile of v6, /device:TPU:1, one launch (start us, length us, event | category | flops | bytes accessed | tf_op | source)
XLA Modules:
  0.0 112.9 jit_solution(10574921057125795134)
XLA Ops:
  0.6 0.0 copy-start.2
  0.6 0.9 copy-done.2
  1.5 0.8 copy-done.3
  2.4 0.2 prep.1
  2.6 0.0 copy-start.6
  2.6 0.0 copy-start.7
  2.7 0.0 copy-start.8
  2.7 12.4 %exchange_first.1 = (f32[8,2,16,128]{3,2,1,0:T(8,128)S(1)}, f32[2,1024,128]{2,1,0:T(8,128)S(1)}, f32[2048,128]{1,0:T(8,128)S(1)}, f32[8,16,128]{2,1,0:T(8,128)S(1)}) custom-call(f32[2,128,128]{2,1,0:T(8,128)S(1)} %get-tuple-element.40.refs_0_.pos, f32[128,128]{1,0:T(8,128)S(1)} %get-tuple-element.41.refs_1_.rad, f32[2,3,8,128]{3,2,1,0:T(8,128)S(1)} %get-tuple-element.42.refs_2_), custom_call_target="tpu_custom_call" | custom-call | flops 4294967296 | bytes 16777216 | tf_op jit(solution)/shard_map/exchange_first/pallas_call | solution.py:652
  15.0 0.0 copy-done.6
  15.0 0.0 copy-done.7
  15.1 0.0 copy-done.8
  15.1 0.0 copy-start
  15.1 13.8 %contact_first.1 = (f32[2,128,128]{2,1,0:T(8,128)S(1)}, f32[2,128,128]{2,1,0:T(8,128)S(1)}, f32[2,2,8,128]{3,2,1,0:T(8,128)S(1)}, f32[128,128]{1,0:T(8,128)S(1)}) custom-call(f32[2,128,128]{2,1,0:T(8,128)S(1)} %get-tuple-element.40.refs_0_.pos, f32[2,128,128]{2,1,0:T(8,128)S(1)} %bitcast.31, f32[128,128]{1,0:T(8,128)S(1)} %get-tuple-element.41.refs_1_.rad, ...), custom_call_target="tpu_custom_call" | custom-call | flops 4294967296 | bytes 16777216 | tf_op jit(solution)/shard_map/contact_first/pallas_call | solution.py:381
  28.9 0.0 copy-start.9
  28.9 1.6 %pack.1 = (f32[6,16,128]{2,1,0:T(8,128)S(1)}, f32[4,48,128]{2,1,0:T(8,128)S(1)}, f32[4,48,128]{2,1,0:T(8,128)S(1)}) custom-call(f32[4,48,32,128]{3,2,1,0:T(8,128)S(1)} %copy-done, f32[2,2,8,128]{3,2,1,0:T(8,128)S(1)} %get-tuple-element.50.after.refs_2_), custom_call_target="tpu_custom_call" | custom-call | tf_op jit(solution)/shard_map/pack/pallas_call | solution.py:448
  30.5 11.1 %exchange_second.1 = (f32[8,2,16,128]{3,2,1,0:T(8,128)S(1)}, f32[2,1024,128]{2,1,0:T(8,128)S(1)}, f32[2048,128]{1,0:T(8,128)S(1)}, f32[2,192,128]{2,1,0:T(8,128)...) custom-call(f32[2,128,128]{2,1,0:T(8,128)S(1)} %get-tuple-element.47.refs_0_.pos, ...), custom_call_target="tpu_custom_call" | custom-call | flops 4294967296 | bytes 16777216 | tf_op jit(solution)/shard_map/exchange_second/pallas_call | solution.py:652
  41.7 14.1 %contact.1 = (f32[2,128,128]{2,1,0:T(8,128)S(1)}, f32[2,128,128]{2,1,0:T(8,128)S(1)}, f32[2,2,8,128]{3,2,1,0:T(8,128)S(1)}, f32[16,16,128]{2,1,0:T(8,128)S(1)}) custom-call(f32[2,128,128]{2,1,0:T(8,128)S(1)} %get-tuple-element.47.refs_0_.pos, f32[2,128,128]{2,1,0:T(8,128)S(1)} %get-tuple-element.48.vel, f32[128,128]{1,0:T(8,128)S(1)} %get-tuple-element.41.refs_1_.rad, ...), custom_call_target="tpu_custom_call" | custom-call | flops 4294967296 | bytes 16777216 | tf_op jit(solution)/shard_map/contact/pallas_call | solution.py:381
  55.8 0.0 copy-start.5
  55.8 10.6 %exchange_third.1 = (f32[8,2,16,128]{3,2,1,0:T(8,128)S(1)}, f32[2,1024,128]{2,1,0:T(8,128)S(1)}, f32[2048,128]{1,0:T(8,128)S(1)}, f32[12,16,128]{2,1,0:T(8,128)S(1)}, f32[2,6,16,128]{3,2,1,0:T(8,128)S(1)}) custom-call(f32[2,128,128]{2,1,0:T(8,128)S(1)} %get-tuple-element.58.refs_0_.pos, f32[128,128]{1,0:T(8,128)S(1)} %get-tuple-element.41.refs_1_.rad, ...), custom_call_target="tpu_custom_call" | custom-call | flops 4294967296 | bytes 16777216 | tf_op jit(solution)/shard_map/exchange_third/pallas_call | solution.py:652
  66.4 0.0 copy-start.1
  66.4 0.0 copy-start.4
  66.4 14.7 %contact_last.1 = (f32[2,128,128]{2,1,0:T(8,128)}, f32[2,128,128]{2,1,0:T(8,128)S(1)}, f32[128,1,128]{2,1,0:T(1,128)S(1)}) custom-call(f32[2,128,128]{2,1,0:T(8,128)S(1)} %get-tuple-element.58.refs_0_.pos, f32[2,128,128]{2,1,0:T(8,128)S(1)} %get-tuple-element.59.vel, f32[128,128]{1,0:T(8,128)S(1)} %get-tuple-element.41.refs_1_.rad, ...), custom_call_target="tpu_custom_call" | custom-call | flops 4294967296 | bytes 16777216 | tf_op jit(solution)/shard_map/contact_last/pallas_call | solution.py:381
  81.2 29.2 %couple.1 = (f32[2,32,128]{2,1,0:T(8,128)S(1)}, f32[16,8,1,128]{3,2,1,0:T(1,128)S(1)}, f32[4,48,32,128]{3,2,1,0:T(8,128)S(1)}) custom-call(f32[16,8,1,128]{3,2,1,0:T(1,128)S(1)} %bitcast.22, s32[2,128]{1,0:T(2,128)S(1)} %bitcast.25, f32[4,48,32,128]{3,2,1,0:T(8,128)S(1)} %copy-done, f32[48,32,128]{2,1,0:T(8,128)S(1)} %copy-done.1, ...), custom_call_target="tpu_custom_call" | custom-call | tf_op jit(solution)/shard_map/couple/pallas_call | solution.py:812
  110.3 2.4 %finish.1 = (f32[2,128,128]{2,1,0:T(8,128)}, f32[4,48,32,128]{3,2,1,0:T(8,128)}) custom-call(f32[4,48,32,128]{3,2,1,0:T(8,128)S(1)} %get-tuple-element.71.plain, f32[2,32,128]{2,1,0:T(8,128)S(1)} %get-tuple-element.72.surface, f32[128,1,128]{2,1,0:T(1,128)S(1)} %bitcast.24, s32[2,128]{1,0:T(2,128)S(1)} %bitcast.27, f32[2,128,128]{2,1,0:T(8,128)S(1)} %get-tuple-element.74.vel), custom_call_target="tpu_custom_call" | custom-call | tf_op jit(solution)/shard_map/finish/pallas_call | solution.py:852
  (6 shorter events, 0.0 us)
Async XLA Ops:
  0.6 0.9 copy-start.2
  1.5 0.8 copy-start.3
  2.6 12.4 %copy-start.6 = (s32[4,8,16,128]{3,2,1,0:T(8,128)S(1)}, s32[4,8,16,128]{3,2,1,0:T(8,128)}, u32[]{:S(2)}) copy-start(s32[4,8,16,128]{3,2,1,0:T(8,128)} %param.13) | copy-start | bytes 786436
  2.6 12.4 %copy-start.7 = (f32[2,8,16,128]{3,2,1,0:T(8,128)S(1)}, f32[2,8,16,128]{3,2,1,0:T(8,128)}, u32[]{:S(2)}) copy-start(f32[2,8,16,128]{3,2,1,0:T(8,128)} %param.11) | copy-start | bytes 393220
  2.7 12.4 %copy-start.8 = (s32[8,8,16]{2,1,0:T(8,128)S(1)}, s32[8,8,16]{2,1,0:T(8,128)}, u32[]{:S(2)}) copy-start(s32[8,8,16]{2,1,0:T(8,128)} %mask.1) | copy-start | bytes 12292
  15.1 13.8 %copy-start = (f32[4,48,32,128]{3,2,1,0:T(8,128)S(1)}, f32[4,48,32,128]{3,2,1,0:T(8,128)}, u32[]{:S(2)}) copy-start(f32[4,48,32,128]{3,2,1,0:T(8,128)} %ocean.3) | copy-start | bytes 9437188
  28.9 1.6 %copy-start.9 = (s32[128]{0:T(128)S(1)}, s32[128]{0:T(128)}, u32[]{:S(2)}) copy-start(s32[128]{0:T(128)} %param.19) | copy-start | bytes 1540
  55.8 10.6 %copy-start.5 = (s32[1,128,2]{1,2,0:T(2,128)S(1)}, s32[1,128,2]{1,2,0:T(2,128)}, u32[]{:S(2)}) copy-start(s32[1,128,2]{1,2,0:T(2,128)} %param.15) | copy-start | bytes 3076
  66.4 14.8 %copy-start.1 = (f32[48,32,128]{2,1,0:T(8,128)S(1)}, f32[48,32,128]{2,1,0:T(8,128)}, u32[]{:S(2)}) copy-start(f32[48,32,128]{2,1,0:T(8,128)} %mix.1) | copy-start | bytes 2359300
  66.4 14.8 %copy-start.4 = (s32[1,128,2]{1,2,0:T(2,128)S(1)}, s32[1,128,2]{1,2,0:T(2,128)}, u32[]{:S(2)}) copy-start(s32[1,128,2]{1,2,0:T(2,128)} %param.18) | copy-start | bytes 3076

commit v7 on v6

--- a/solution.py
+++ b/solution.py
@@ -425,39 +425,27 @@
     )(pos, rad)
 
 
-def pack_kernel(ocean, after, columns, bottom, top):
-    rows = ocean.shape[2]
-    lane = lax.broadcasted_iota(jnp.int32, (8, 128), 1)
-    packed = [jnp.zeros((8, 128), jnp.float32)] * 2
-    for field in range(4):
-        for layer in range(CHUNK):
-            for v in range(rows // 8):
-                g = (field * CHUNK + layer) * (rows // 8) + v
-                place = g % 64
-                turned = pltpu.roll(ocean[field, layer, pl.ds(8 * v, 8), :], 2 * place + 1, 1)
-                packed[g // 64] = jnp.where(lane // 2 == place, turned, packed[g // 64])
-    columns[0] = jnp.concatenate(packed, axis=0)
-    bottom[...] = ocean[:, :, 0, :]
-    top[...] = ocean[:, :, rows - 1, :]
-
-
-def pack(ocean, after):
-    fields, layers, rows, lanes = ocean.shape
-    steps = layers // CHUNK
-    row = pl.BlockSpec((fields, CHUNK, lanes), lambda i: (0, i, 0))
-    return pl.pallas_call(
-        pack_kernel,
-        grid=(steps,),
-        out_shape=(
-            shape(steps, 16, lanes),
-            shape(fields, layers, lanes),
-            shape(fields, layers, lanes),
-        ),
-        in_specs=[pl.BlockSpec((fields, CHUNK, rows, lanes), lambda i: (0, i, 0, 0)), ANY],
-        out_specs=(pl.BlockSpec((1, 16, lanes), lambda i: (i, 0, 0)), row, row),
-        compiler_params=grant(8),
-        name="pack",
-    )(ocean, after)
+def pack(ocean, sides, bottom, top):
+    layers, rows, lanes = ocean.shape[1:]
+    lane = lax.broadcasted_iota(jnp.int32, (8, lanes), 1)
+
+    def one(step, carry):
+        first = pl.multiple_of(step * CHUNK, CHUNK)
+        packed = [jnp.zeros((8, lanes), jnp.float32)] * 2
+        for field in range(4):
+            at = pl.ds(pl.multiple_of(field * layers + first, CHUNK), CHUNK)
+            bottom[at, :] = ocean[field, pl.ds(first, CHUNK), 0, :]
+            top[at, :] = ocean[field, pl.ds(first, CHUNK), rows - 1, :]
+            for layer in range(CHUNK):
+                for v in range(rows // 8):
+                    g = (field * CHUNK + layer) * (rows // 8) + v
+                    here = ocean[field, first + layer, pl.ds(8 * v, 8), :]
+                    turned = pltpu.roll(here, 2 * (g % 64) + 1, 1)
+                    packed[g // 64] = jnp.where(lane // 2 == g % 64, turned, packed[g // 64])
+        sides[step] = jnp.concatenate(packed, axis=0)
+        return carry
+
+    lax.fori_loop(0, layers // CHUNK, one, 0)
 
 
 def exchange_kernel(which, n_gx, n_gy, *refs):
@@ -465,7 +453,8 @@
         pos, rad, edges, halo, held, marks, halo_rad, *scratch = refs
         send_sem, recv_sem, rad_send, rad_recv = scratch
     elif which == 1:
-        pos, rad, edges, top, bottom, perm, halo, held, marks, lat, rows, perms, *scratch = refs
+        pos, rad, edges, ocean, perm, halo, held, marks, lat, rows, perms, sides, *scratch = refs
+        top, bottom, *scratch = scratch
         send_sem, recv_sem, sea_send, sea_recv, *scratch = scratch
         far_send, far_recv, perm_send, perm_recv, own = scratch
     else:
@@ -487,6 +476,8 @@
             for d in range(1, n_gx):
                 pl.semaphore_signal(barrier, inc=1, device_id=at(d, 0), device_id_type=MESH)
 
+    if which == 1:
+        pack(ocean, sides, bottom, top)
     blocks = rad.shape[0]
     write_marks([pos[0], pos[1], rad[...]], marks)
     own_forces(0, EARLY, marks, held)
@@ -642,9 +633,11 @@
         outs += [shape(8, 16, lanes)]
         scratch += [dma((8,)), dma((8,))]
     if which == 1:
-        top, bottom, perm = args
-        outs += [shape(2, *top.shape)]
+        layers = args[0].shape[1]
+        outs += [shape(2, 4 * layers, lanes)]
         outs += [shape(n_gx, TURN_ROWS, lanes), jax.ShapeDtypeStruct((n_gx, 1, lanes), jnp.int32)]
+        outs += [shape(layers // CHUNK, 16, lanes)]
+        scratch = [pltpu.VMEM((4 * layers, lanes), jnp.float32)] * 2 + scratch
         scratch += [dma((2,)), dma((2,))] + far + far + [dma((2,))]
     if which == 2:
         outs += [shape(TURNERS, TURN_ROWS, lanes), shape(2, *args[1].shape)]
@@ -883,15 +876,13 @@
     rad = radius.reshape(blocks, discs)
     bonds = bond_list.reshape(BONDS, blocks, discs)
     sea_shape = (4, mix_coef.shape[0], discs)
-    flat = (4 * mix_coef.shape[0], discs)
     position, rad, edges = prep(position, rad)
     halo, held, marks, halo_rad = exchange(0, n_gx, n_gy, position, rad, edges)
     position, velocity, edges, mask = contact_step(
         0, n_gy, position, velocity, rad, bonds, contact_mask, marks, held, halo, halo_rad
     )
-    sides, bottom, top = pack(ocean_state, edges)
-    halo, held, marks, lat, rows, perms = exchange(
-        1, n_gx, n_gy, position, rad, edges, top.reshape(flat), bottom.reshape(flat), perm
+    halo, held, marks, lat, rows, perms, sides = exchange(
+        1, n_gx, n_gy, position, rad, edges, ocean_state, perm
     )
     position, velocity, edges, turned = contact_step(
         1, n_gy, position, velocity, rad, bonds, mask, marks, held, halo, halo_rad, rows, perms

time: 114 us -> 108 us (0.947)
  Pallas kernels: 110 us -> 105 us
    pallas_call x1, Pallas kernels: 29.2 us -> 23.4 us  [couple(): pl.pallas_call(functools.partial(couple_kernel, n_gx, n_gy), out_shape=(s...]
    pallas_call x3, Pallas kernels: 42.6 us -> 46.8 us  [contact_step(): pl.pallas_call(functools.partial(contact_kernel, which, n_gy), out_shape=...]
    pallas_call x3, Pallas kernels: 34.1 us -> 32.3 us  [exchange(): pl.pallas_call(functools.partial(exchange_kernel, which, n_gx, n_gy), out...]
    pallas_call x1 -> x0, Pallas kernels: 1.61 us -> none  [pack(): pl.pallas_call(pack_kernel, grid=(steps,), out_shape=(shape(steps, 16, la...]
where the time goes in v7:
time: 108 us
  Pallas kernels  105 us (97%)
  local copies, waits for them, and re-layouts  1.79 us (2%)
    pallas_call x3, Pallas kernels, contact_step(): pl.pallas_call(functools.partial(contact_kernel, which, n_gy), out_shape=...  46.8 us
    pallas_call x3, Pallas kernels, exchange(): pl.pallas_call(functools.partial(exchange_kernel, which, n_gx, n_gy), out...  32.3 us
    pallas_call x1, Pallas kernels, couple(): pl.pallas_call(functools.partial(couple_kernel, n_gx, n_gy), out_shape=(s...  23.4 us
    pallas_call x1, Pallas kernels, finish(): pl.pallas_call(finish_kernel, out_shape=(shape(*vel.shape), shape(*plain....  2.37 us

profile of v7, /device:TPU:1, one launch (start us, length us, event | category | flops | bytes accessed | tf_op | source)
XLA Modules:
  0.0 107.8 jit_solution(16565458043339987220)
XLA Ops:
  0.6 0.0 copy-start.2
  0.6 0.9 copy-done.2
  1.5 0.8 copy-done.3
  2.4 0.2 prep.1
  2.6 0.0 copy-start.6
  2.6 0.0 copy-start.7
  2.7 0.0 copy-start.8
  2.7 12.4 %exchange_first.1 = (f32[8,2,16,128]{3,2,1,0:T(8,128)S(1)}, f32[2,1024,128]{2,1,0:T(8,128)S(1)}, f32[2048,128]{1,0:T(8,128)S(1)}, f32[8,16,128]{2,1,0:T(8,128)S(1)}) custom-call(f32[2,128,128]{2,1,0:T(8,128)S(1)} %get-tuple-element.38.refs_0_.pos, f32[128,128]{1,0:T(8,128)S(1)} %get-tuple-element.39.refs_1_.rad, f32[2,3,8,128]{3,2,1,0:T(8,128)S(1)} %get-tuple-element.40.refs_2_), custom_call_target="tpu_custom_call" | custom-call | flops 4294967296 | bytes 16777216 | tf_op jit(solution)/shard_map/exchange_first/pallas_call | solution.py:645
  15.0 0.0 copy-done.6
  15.0 0.0 copy-done.7
  15.1 0.0 copy-done.8
  15.1 0.0 copy-start
  15.1 0.0 copy-start.9
  15.1 14.7 %contact_first.1 = (f32[2,128,128]{2,1,0:T(8,128)S(1)}, f32[2,128,128]{2,1,0:T(8,128)S(1)}, f32[2,2,8,128]{3,2,1,0:T(8,128)S(1)}, f32[128,128]{1,0:T(8,128)S(1)}) custom-call(f32[2,128,128]{2,1,0:T(8,128)S(1)} %get-tuple-element.38.refs_0_.pos, f32[2,128,128]{2,1,0:T(8,128)S(1)} %bitcast.29, f32[128,128]{1,0:T(8,128)S(1)} %get-tuple-element.39.refs_1_.rad, ...), custom_call_target="tpu_custom_call" | custom-call | flops 4294967296 | bytes 16777216 | tf_op jit(solution)/shard_map/contact_first/pallas_call | solution.py:381
  29.8 0.0 copy-done
  29.8 10.7 %exchange_second.1 = (f32[8,2,16,128]{3,2,1,0:T(8,128)S(1)}, f32[2,1024,128]{2,1,0:T(8,128)S(1)}, f32[2048,128]{1,0:T(8,128)S(1)}, f32[2,192,128]{2,1,0:T(8,128)...) custom-call(f32[2,128,128]{2,1,0:T(8,128)S(1)} %get-tuple-element.45.refs_0_.pos, ...), custom_call_target="tpu_custom_call" | custom-call | flops 4294967296 | bytes 16777216 | tf_op jit(solution)/shard_map/exchange_second/pallas_call | solution.py:645
  40.5 14.5 %contact.1 = (f32[2,128,128]{2,1,0:T(8,128)S(1)}, f32[2,128,128]{2,1,0:T(8,128)S(1)}, f32[2,2,8,128]{3,2,1,0:T(8,128)S(1)}, f32[16,16,128]{2,1,0:T(8,128)S(1)}) custom-call(f32[2,128,128]{2,1,0:T(8,128)S(1)} %get-tuple-element.45.refs_0_.pos, f32[2,128,128]{2,1,0:T(8,128)S(1)} %get-tuple-element.46.vel, f32[128,128]{1,0:T(8,128)S(1)} %get-tuple-element.39.refs_1_.rad, ...), custom_call_target="tpu_custom_call" | custom-call | flops 4294967296 | bytes 16777216 | tf_op jit(solution)/shard_map/contact/pallas_call | solution.py:381
  55.1 0.0 copy-start.5
  55.1 9.2 %exchange_third.1 = (f32[8,2,16,128]{3,2,1,0:T(8,128)S(1)}, f32[2,1024,128]{2,1,0:T(8,128)S(1)}, f32[2048,128]{1,0:T(8,128)S(1)}, f32[12,16,128]{2,1,0:T(8,128)S(1)}, f32[2,6,16,128]{3,2,1,0:T(8,128)S(1)}) custom-call(f32[2,128,128]{2,1,0:T(8,128)S(1)} %get-tuple-element.54.refs_0_.pos, f32[128,128]{1,0:T(8,128)S(1)} %get-tuple-element.39.refs_1_.rad, ...), custom_call_target="tpu_custom_call" | custom-call | flops 4294967296 | bytes 16777216 | tf_op jit(solution)/shard_map/exchange_third/pallas_call | solution.py:645
  64.3 0.0 copy-start.1
  64.3 0.0 copy-start.4
  64.3 17.5 %contact_last.1 = (f32[2,128,128]{2,1,0:T(8,128)}, f32[2,128,128]{2,1,0:T(8,128)S(1)}, f32[128,1,128]{2,1,0:T(1,128)S(1)}) custom-call(f32[2,128,128]{2,1,0:T(8,128)S(1)} %get-tuple-element.54.refs_0_.pos, f32[2,128,128]{2,1,0:T(8,128)S(1)} %get-tuple-element.55.vel, f32[128,128]{1,0:T(8,128)S(1)} %get-tuple-element.39.refs_1_.rad, ...), custom_call_target="tpu_custom_call" | custom-call | flops 4294967296 | bytes 16777216 | tf_op jit(solution)/shard_map/contact_last/pallas_call | solution.py:381
  81.9 23.4 %couple.1 = (f32[2,32,128]{2,1,0:T(8,128)S(1)}, f32[16,8,1,128]{3,2,1,0:T(1,128)S(1)}, f32[4,48,32,128]{3,2,1,0:T(8,128)S(1)}) custom-call(f32[16,8,1,128]{3,2,1,0:T(1,128)S(1)} %bitcast.20, s32[2,128]{1,0:T(2,128)S(1)} %bitcast.23, f32[4,48,32,128]{3,2,1,0:T(8,128)S(1)} %copy-done, f32[48,32,128]{2,1,0:T(8,128)S(1)} %copy-done.1, ...), custom_call_target="tpu_custom_call" | custom-call | tf_op jit(solution)/shard_map/couple/pallas_call | solution.py:805
  105.3 2.4 %finish.1 = (f32[2,128,128]{2,1,0:T(8,128)}, f32[4,48,32,128]{3,2,1,0:T(8,128)}) custom-call(f32[4,48,32,128]{3,2,1,0:T(8,128)S(1)} %get-tuple-element.67.plain, f32[2,32,128]{2,1,0:T(8,128)S(1)} %get-tuple-element.68.surface, f32[128,1,128]{2,1,0:T(1,128)S(1)} %bitcast.22, s32[2,128]{1,0:T(2,128)S(1)} %bitcast.25, f32[2,128,128]{2,1,0:T(8,128)S(1)} %get-tuple-element.70.vel), custom_call_target="tpu_custom_call" | custom-call | tf_op jit(solution)/shard_map/finish/pallas_call | solution.py:845
  (5 shorter events, 0.0 us)
Async XLA Ops:
  0.6 0.9 copy-start.2
  1.5 0.8 copy-start.3
  2.6 12.4 %copy-start.6 = (s32[4,8,16,128]{3,2,1,0:T(8,128)S(1)}, s32[4,8,16,128]{3,2,1,0:T(8,128)}, u32[]{:S(2)}) copy-start(s32[4,8,16,128]{3,2,1,0:T(8,128)} %param.13) | copy-start | bytes 786436
  2.6 12.4 %copy-start.7 = (f32[2,8,16,128]{3,2,1,0:T(8,128)S(1)}, f32[2,8,16,128]{3,2,1,0:T(8,128)}, u32[]{:S(2)}) copy-start(f32[2,8,16,128]{3,2,1,0:T(8,128)} %param.11) | copy-start | bytes 393220
  2.7 12.4 %copy-start.8 = (s32[8,8,16]{2,1,0:T(8,128)S(1)}, s32[8,8,16]{2,1,0:T(8,128)}, u32[]{:S(2)}) copy-start(s32[8,8,16]{2,1,0:T(8,128)} %mask.1) | copy-start | bytes 12292
  15.1 14.7 %copy-start = (f32[4,48,32,128]{3,2,1,0:T(8,128)S(1)}, f32[4,48,32,128]{3,2,1,0:T(8,128)}, u32[]{:S(2)}) copy-start(f32[4,48,32,128]{3,2,1,0:T(8,128)} %ocean.1) | copy-start | bytes 9437188
  15.1 14.7 %copy-start.9 = (s32[128]{0:T(128)S(1)}, s32[128]{0:T(128)}, u32[]{:S(2)}) copy-start(s32[128]{0:T(128)} %param.19) | copy-start | bytes 1540
  55.1 9.2 %copy-start.5 = (s32[1,128,2]{1,2,0:T(2,128)S(1)}, s32[1,128,2]{1,2,0:T(2,128)}, u32[]{:S(2)}) copy-start(s32[1,128,2]{1,2,0:T(2,128)} %param.15) | copy-start | bytes 3076
  64.3 17.6 %copy-start.1 = (f32[48,32,128]{2,1,0:T(8,128)S(1)}, f32[48,32,128]{2,1,0:T(8,128)}, u32[]{:S(2)}) copy-start(f32[48,32,128]{2,1,0:T(8,128)} %mix.1) | copy-start | bytes 2359300
  64.3 17.6 %copy-start.4 = (s32[1,128,2]{1,2,0:T(2,128)S(1)}, s32[1,128,2]{1,2,0:T(2,128)}, u32[]{:S(2)}) copy-start(s32[1,128,2]{1,2,0:T(2,128)} %param.18) | copy-start | bytes 3076
